TPU v7x, 32 devices: a whole 2x2x4 slice. The times are simulated.
32 devices in a mesh: dp: 8 (over z, x), mp: 4 (over y, core).
Axes of the slice: x: 2, y: 2, z: 4, core: 2. Of those that a mesh axis runs over, the one named last changes fastest.
Arguments:
- activations: bfloat16 [24576, 768], P('dp'), may hold values from -6 to 6
- keep_flags: int32 [24], P('dp'), may hold values from 0 to 1, as said below
- mask_counts: int32 [24], P('dp'), may hold values from 51 to 256, as said below
- mask_positions: int32 [24, 256], P('dp'), may hold values from 0 to 1023, as said below
- cotangents: bfloat16 [24, 256, 768], P('dp'), may hold values from -6 to 6
- projections: float32 [3, 768, 768], P(None, 'dp', 'mp'), may hold values from -0.21875 to 0.21875
- combiner: float32 [768, 768], P('mp', 'dp'), may hold values from -0.625 to 0.625
- expander: float32 [768, 3072], P('dp', 'mp'), may hold values from -0.21875 to 0.21875
- reducer: float32 [3072, 768], P('mp', 'dp'), may hold values from -0.109375 to 0.109375
- offsets: float32 [2, 768], P(None, 'mp'), may hold values from -4 to 4
- shifts: float32 [3072], P('mp'), may hold values from -4 to 4
- vectors: float32 [6, 768], replicated, may hold values from -2 to 2
- momentum_projections: float32 [3, 768, 768], P(None, 'dp', 'mp'), may hold values from -0.005859375 to 0.005859375
- variance_projections: float32 [3, 768, 768], P(None, 'dp', 'mp'), may hold values from 1.4392339e-07 to 2.3027742e-06
- momentum_combiner: float32 [768, 768], P('mp', 'dp'), may hold values from -0.005859375 to 0.005859375
- variance_combiner: float32 [768, 768], P('mp', 'dp'), may hold values from 1.4392339e-07 to 2.3027742e-06
- momentum_expander: float32 [768, 3072], P('dp', 'mp'), may hold values from -0.005859375 to 0.005859375
- variance_expander: float32 [768, 3072], P('dp', 'mp'), may hold values from 1.4392339e-07 to 2.3027742e-06
- momentum_reducer: float32 [3072, 768], P('mp', 'dp'), may hold values from -0.005859375 to 0.005859375
- variance_reducer: float32 [3072, 768], P('mp', 'dp'), may hold values from 1.4392339e-07 to 2.3027742e-06
- momentum_offsets: float32 [2, 768], P(None, 'mp'), may hold values from -0.005859375 to 0.005859375
- variance_offsets: float32 [2, 768], P(None, 'mp'), may hold values from 1.4392339e-07 to 2.3027742e-06
- first_moment_shifts: float32 [3072], P('mp'), may hold values from -0.005859375 to 0.005859375
- second_moment_shifts: float32 [3072], P('mp'), may hold values from 1.4392339e-07 to 2.3027742e-06
- momentum_vectors: float32 [6, 768], replicated, may hold values from -0.005859375 to 0.005859375
- variance_vectors: float32 [6, 768], replicated, may hold values from 1.4392339e-07 to 2.3027742e-06
Outputs:
- layer_output: bfloat16 [24576, 768], P('dp')
- input_gradient: float32 [24576, 768], P('dp')
- kept_count: int32 [], replicated
- gradient_norm: float32 [], replicated
- updated_projections: float32 [3, 768, 768], P(None, 'dp', 'mp')
- averaged_projections: float32 [3, 768, 768], P(None, 'dp', 'mp')
- squared_projections: float32 [3, 768, 768], P(None, 'dp', 'mp')
- updated_combiner: float32 [768, 768], P('mp', 'dp')
- averaged_combiner: float32 [768, 768], P('mp', 'dp')
- squared_combiner: float32 [768, 768], P('mp', 'dp')
- updated_expander: float32 [768, 3072], P('dp', 'mp')
- averaged_expander: float32 [768, 3072], P('dp', 'mp')
- squared_expander: float32 [768, 3072], P('dp', 'mp')
- updated_reducer: float32 [3072, 768], P('mp', 'dp')
- averaged_reducer: float32 [3072, 768], P('mp', 'dp')
- squared_reducer: float32 [3072, 768], P('mp', 'dp')
- updated_offsets: float32 [2, 768], P(None, 'mp')
- averaged_offsets: float32 [2, 768], P(None, 'mp')
- squared_offsets: float32 [2, 768], P(None, 'mp')
- updated_shifts: float32 [3072], P('mp')
- averaged_shifts: float32 [3072], P('mp')
- squared_shifts: float32 [3072], P('mp')
- updated_vectors: float32 [6, 768], replicated
- averaged_vectors: float32 [6, 768], replicated
- squared_vectors: float32 [6, 768], replicated
- rounded_projections: bfloat16 [3, 768, 768], P(None, 'dp', 'mp')
- rounded_combiner: bfloat16 [768, 768], P('mp', 'dp')
- rounded_expander: bfloat16 [768, 3072], P('dp', 'mp')
- rounded_reducer: bfloat16 [3072, 768], P('mp', 'dp')
Inputs may be any that keep to these rules, and one draw needn't show every extreme that they name: `keep_flags`: at least one sequence is kept. `mask_counts`: at least one sequence has exactly 256 masked tokens. `mask_positions`: the 256 entries of a sequence are distinct positions within it; the first mask_counts of them are its masked tokens, the others are not used.
All inputs are finite; a program needn't handle non-finite values.
Results may differ from a plain program's by a relative error of at most 0.015.
The roundings to bfloat16 on the way count: a program that leaves them out, or rounds other values in their place, can miss the bound.
Values may be sent and summed in bfloat16 or wider, within the bound.
A program may use at most 256 MiB of HBM per device.

v0:
```python
import jax
import jax.numpy as jnp
from jax import lax
from jax.sharding import PartitionSpec as P

HD = 64
STEP = 10


clip_limit = 10.0
learn_rate = 0.05
vector_rate = 0.3
decay_rate = 0.01
adam_eps = 1e-06


def row_contract(left, right):
    return lax.dot_general(
        left, right, (((0,), (0,)), ((), ())), preferred_element_type=jnp.float32
    )


def col_contract(left, right):
    return lax.dot_general(
        left, right, (((1,), (1,)), ((), ())), preferred_element_type=jnp.float32
    )


def gelu_exact(value):
    return jax.nn.gelu(value, approximate=False)


def normalize(value, gain, bias):
    mean = jnp.mean(value, -1, keepdims=True)
    centered = value - mean
    rstd = lax.rsqrt(jnp.mean(centered * centered, -1, keepdims=True) + 1e-05)
    unit = centered * rstd
    return (unit * gain + bias, unit, rstd)


def norm_backward(grad, unit, rstd, gain):
    scaled = grad * gain
    inner = (
        scaled
        - jnp.mean(scaled, -1, keepdims=True)
        - unit * jnp.mean(scaled * unit, -1, keepdims=True)
    )
    return (rstd * inner, jnp.sum(grad * unit, 0), jnp.sum(grad, 0))


def squares(value):
    return jnp.sum(value * value)


def adamw_update_step(weight, first, second, grad, clip_factor, rate):
    clipped = grad * clip_factor
    averaged = 0.9 * first + 0.1 * clipped
    squared = 0.98 * second + 0.02 * clipped * clipped
    step_size = averaged / (1.0 - 0.9**STEP) / (jnp.sqrt(squared / (1.0 - 0.98**STEP)) + adam_eps)
    return (weight - rate * (step_size + decay_rate * weight), averaged, squared)


def shards(
    activations,
    keep_flags,
    mask_counts,
    mask_positions,
    cotangents,
    projections,
    combiner,
    expander,
    reducer,
    offsets,
    shifts,
    vectors,
    momentum_projections,
    variance_projections,
    momentum_combiner,
    variance_combiner,
    momentum_expander,
    variance_expander,
    momentum_reducer,
    variance_reducer,
    momentum_offsets,
    variance_offsets,
    first_moment_shifts,
    second_moment_shifts,
    momentum_vectors,
    variance_vectors,
):
    seq_dev = keep_flags.shape[0]
    total_rows = activations.shape[0]
    length = total_rows // seq_dev
    width = activations.shape[1]
    slots = mask_positions.shape[1]
    columns = offsets.shape[1]
    heads_here = columns // HD
    bf16 = jnp.bfloat16
    f32 = jnp.float32
    kept_total = lax.psum(jnp.sum(keep_flags), "dp")
    shares = (
        keep_flags.astype(f32) * jnp.float32(seq_dev * lax.axis_size("dp")) / kept_total.astype(f32)
    )
    wproj, wcomb, wexp, wred = (
        lax.all_gather(projections.astype(bf16), "dp", axis=1, tiled=True),
        lax.all_gather(combiner.astype(bf16), "dp", axis=1, tiled=True),
        lax.all_gather(expander.astype(bf16), "dp", axis=0, tiled=True),
        lax.all_gather(reducer.astype(bf16), "dp", axis=1, tiled=True),
    )
    raw = jnp.einsum("rd,kdc->krc", activations, wproj, preferred_element_type=f32)
    query_low = (raw[0] + offsets[0]).astype(bf16)
    key_low = raw[1].astype(bf16)
    value_low = (raw[2] + offsets[1]).astype(bf16)
    block = min(512, length)
    block_count = length // block

    def to_blocks(rows):
        return rows.reshape(seq_dev, block_count, block, heads_here, HD).transpose(1, 0, 2, 3, 4)

    def from_blocks(parts):
        return parts.transpose(1, 0, 2, 3, 4).reshape(total_rows, columns)

    keys_heads = key_low.reshape(seq_dev, length, heads_here, HD)
    values_heads = value_low.reshape(seq_dev, length, heads_here, HD)
    query_blocks = to_blocks(query_low)

    def attend(query_block):
        scores = (
            jnp.einsum("sbhe,slhe->shbl", query_block, keys_heads, preferred_element_type=f32)
            * 0.125
        )
        top = jnp.max(scores, -1, keepdims=True)
        exponent = jnp.exp(scores - top)
        total = jnp.sum(exponent, -1, keepdims=True)
        probs = exponent / total
        attended = jnp.einsum(
            "shbl,slhe->sbhe", probs.astype(bf16), values_heads, preferred_element_type=f32
        )
        return (attended, (top + jnp.log(total))[..., 0])

    attended_blocks, total_blocks = lax.map(attend, query_blocks)
    outputs_low = from_blocks(attended_blocks).astype(bf16)
    attention = lax.psum(
        jnp.dot(outputs_low, wcomb, preferred_element_type=f32).astype(jnp.bfloat16), "mp"
    ).astype(jnp.float32)
    inputs_float = activations.astype(f32)
    first = inputs_float + (attention + vectors[0])
    normed, unit_one, rstd_one = normalize(first, vectors[2], vectors[3])
    normed_low = normed.astype(bf16)
    inner = jnp.dot(normed_low, wexp, preferred_element_type=f32) + shifts
    hidden_low = gelu_exact(inner).astype(bf16)
    feedforward = lax.psum(
        jnp.dot(hidden_low, wred, preferred_element_type=f32).astype(jnp.bfloat16), "mp"
    ).astype(jnp.float32)
    second = normed + (feedforward + vectors[1])
    final, unit_two, rstd_two = normalize(second, vectors[4], vectors[5])
    share_rows = jnp.repeat(shares, length)[:, None]
    layer_output = (inputs_float + share_rows * (final - inputs_float)).astype(bf16)
    valid = (jnp.arange(slots)[None, :] < mask_counts[:, None]).astype(f32)
    given = (cotangents.astype(f32) * valid[:, :, None]).reshape(seq_dev * slots, width)
    flat_index = (
        mask_positions + (jnp.arange(seq_dev, dtype=jnp.int32) * length)[:, None]
    ).reshape(-1)
    target = jnp.zeros((total_rows, width), f32).at[flat_index].add(given)
    upstream = share_rows * target
    d_second, grad_gain_two, grad_bias_two = norm_backward(upstream, unit_two, rstd_two, vectors[4])
    second_low = d_second.astype(bf16)
    grad_reducer = row_contract(hidden_low, second_low)
    d_hidden = col_contract(second_low, wred)
    d_inner = jax.vjp(gelu_exact, inner)[1](d_hidden)[0]
    inner_grad_low = d_inner.astype(bf16)
    grad_expander = row_contract(normed_low, inner_grad_low)
    d_normed = d_second + lax.psum(
        col_contract(inner_grad_low, wexp).astype(jnp.bfloat16), "mp"
    ).astype(jnp.float32)
    d_first, grad_gain_one, grad_bias_one = norm_backward(d_normed, unit_one, rstd_one, vectors[2])
    first_low = d_first.astype(bf16)
    grad_combiner = row_contract(outputs_low, first_low)
    d_outputs = col_contract(first_low, wcomb)
    grad_vectors = jnp.stack(
        [
            jnp.sum(d_first, 0),
            jnp.sum(d_second, 0),
            grad_gain_one,
            grad_bias_one,
            grad_gain_two,
            grad_bias_two,
        ]
    )
    residual = (1.0 - share_rows) * target + d_first
    residual, d_outputs, grad_combiner, grad_expander, grad_reducer, grad_shifts, grad_vectors = (
        residual,
        d_outputs,
        grad_combiner,
        grad_expander,
        grad_reducer,
        jnp.sum(d_inner, 0),
        grad_vectors,
    )
    grad_blocks = to_blocks(d_outputs.astype(bf16))

    def back_step(carry, items):
        grad_keys, grad_values = carry
        query_block, grad_block, total_block = items
        scores = (
            jnp.einsum("sbhe,slhe->shbl", query_block, keys_heads, preferred_element_type=f32)
            * 0.125
        )
        probs = jnp.exp(scores - total_block[..., None])
        grad_probs = jnp.einsum(
            "sbhe,slhe->shbl", grad_block, values_heads, preferred_element_type=f32
        )
        grad_values = grad_values + jnp.einsum(
            "shbl,sbhe->slhe", probs.astype(bf16), grad_block, preferred_element_type=f32
        )
        grad_scores = probs * (grad_probs - jnp.sum(probs * grad_probs, -1, keepdims=True))
        scores_low = grad_scores.astype(bf16)
        grad_query = (
            jnp.einsum("shbl,slhe->sbhe", scores_low, keys_heads, preferred_element_type=f32)
            * 0.125
        )
        grad_keys = (
            grad_keys
            + jnp.einsum("shbl,sbhe->slhe", scores_low, query_block, preferred_element_type=f32)
            * 0.125
        )
        return ((grad_keys, grad_values), grad_query)

    start = jnp.zeros((seq_dev, length, heads_here, HD), f32)
    (grad_keys, grad_values), query_grads = lax.scan(
        back_step, (start, start), (query_blocks, grad_blocks, total_blocks)
    )
    grad_query = from_blocks(query_grads)
    grad_keys = grad_keys.reshape(total_rows, columns)
    grad_values = grad_values.reshape(total_rows, columns)
    grad_offsets = jnp.stack([jnp.sum(grad_query, 0), jnp.sum(grad_values, 0)])
    stacked_low = jnp.stack([grad_query, grad_keys, grad_values]).astype(bf16)
    grad_projections = jnp.einsum(
        "rd,krc->kdc", activations, stacked_low, preferred_element_type=f32
    )
    input_part = jnp.einsum("krc,kdc->rd", stacked_low, wproj, preferred_element_type=f32)
    input_gradient = residual + lax.psum(input_part.astype(jnp.bfloat16), "mp").astype(jnp.float32)
    share_proj, share_comb, share_expd, share_redc = (
        lax.psum_scatter(grad_projections, "dp", scatter_dimension=1, tiled=True),
        lax.psum_scatter(grad_combiner, "dp", scatter_dimension=1, tiled=True),
        lax.psum_scatter(grad_expander, "dp", scatter_dimension=0, tiled=True),
        lax.psum_scatter(grad_reducer, "dp", scatter_dimension=1, tiled=True),
    )
    sum_offsets, shifts_total, sum_vectors = lax.psum(
        (grad_offsets, grad_shifts, grad_vectors), "dp"
    )
    local_squares = (
        squares(share_proj) + squares(share_comb) + squares(share_expd) + squares(share_redc)
    )
    small_squares = squares(sum_offsets) + squares(shifts_total)
    vector_squares = squares(sum_vectors)
    first_data = lax.axis_index("dp") == 0
    first_tensor = lax.axis_index("mp") == 0
    term = local_squares + jnp.where(
        first_data, small_squares + jnp.where(first_tensor, vector_squares, 0.0), 0.0
    )
    total_squares = lax.psum(term, ("dp", "mp"))
    gradient_norm = jnp.sqrt(total_squares)
    clip_factor = clip_limit / jnp.maximum(gradient_norm, clip_limit)
    next_projections = adamw_update_step(
        projections, momentum_projections, variance_projections, share_proj, clip_factor, learn_rate
    )
    next_combiner = adamw_update_step(
        combiner, momentum_combiner, variance_combiner, share_comb, clip_factor, learn_rate
    )
    next_expander = adamw_update_step(
        expander, momentum_expander, variance_expander, share_expd, clip_factor, learn_rate
    )
    next_reducer = adamw_update_step(
        reducer, momentum_reducer, variance_reducer, share_redc, clip_factor, learn_rate
    )
    next_offsets = adamw_update_step(
        offsets, momentum_offsets, variance_offsets, sum_offsets, clip_factor, vector_rate
    )
    next_shifts = adamw_update_step(
        shifts, first_moment_shifts, second_moment_shifts, shifts_total, clip_factor, vector_rate
    )
    next_vectors = adamw_update_step(
        vectors, momentum_vectors, variance_vectors, sum_vectors, clip_factor, vector_rate
    )
    return (
        layer_output,
        input_gradient,
        kept_total,
        gradient_norm,
        next_projections[0],
        next_projections[1],
        next_projections[2],
        next_combiner[0],
        next_combiner[1],
        next_combiner[2],
        next_expander[0],
        next_expander[1],
        next_expander[2],
        next_reducer[0],
        next_reducer[1],
        next_reducer[2],
        next_offsets[0],
        next_offsets[1],
        next_offsets[2],
        next_shifts[0],
        next_shifts[1],
        next_shifts[2],
        next_vectors[0],
        next_vectors[1],
        next_vectors[2],
        next_projections[0].astype(bf16),
        next_combiner[0].astype(bf16),
        next_expander[0].astype(bf16),
        next_reducer[0].astype(bf16),
    )


def solution(mesh):
    placed = (
        P("dp", None),
        P("dp"),
        P("dp"),
        P("dp", None),
        P("dp", None, None),
        P(None, "dp", "mp"),
        P("mp", "dp"),
        P("dp", "mp"),
        P("mp", "dp"),
        P(None, "mp"),
        P("mp"),
        P(),
        P(None, "dp", "mp"),
        P(None, "dp", "mp"),
        P("mp", "dp"),
        P("mp", "dp"),
        P("dp", "mp"),
        P("dp", "mp"),
        P("mp", "dp"),
        P("mp", "dp"),
        P(None, "mp"),
        P(None, "mp"),
        P("mp"),
        P("mp"),
        P(),
        P(),
    )
    return jax.shard_map(
        shards,
        mesh=mesh,
        in_specs=placed,
        out_specs=(
            P("dp", None),
            P("dp", None),
            P(),
            P(),
            P(None, "dp", "mp"),
            P(None, "dp", "mp"),
            P(None, "dp", "mp"),
            P("mp", "dp"),
            P("mp", "dp"),
            P("mp", "dp"),
            P("dp", "mp"),
            P("dp", "mp"),
            P("dp", "mp"),
            P("mp", "dp"),
            P("mp", "dp"),
            P("mp", "dp"),
            P(None, "mp"),
            P(None, "mp"),
            P(None, "mp"),
            P("mp"),
            P("mp"),
            P("mp"),
            P(),
            P(),
            P(),
            P(None, "dp", "mp"),
            P("mp", "dp"),
            P("dp", "mp"),
            P("mp", "dp"),
        ),
        check_vma=False,
    )
```

profile of v0, /device:TPU:0, one launch (start us, length us, event | category | flops | bytes accessed | tf_op | source)
XLA Modules:
  0.0 946.7 jit_solution(13843378945948732099)
XLA Ops:
  10.4 38.7 %all_gather.12 = bf16[3,768,192]{2,0,1:T(4,128)(2,1)S(1)} all-gather(bf16[3,96,192]{2,0,1:T(4,128)(2,1)S(1)} %copy.115), channel_id=1, replica_groups=mesh['dp'=8,'mp'=4] {'dp'}, dimensions={1}, use_global_device_ids=true | all-gather | bytes 995328 | tf_op jit(solution)/shard_map/all_gather | solution.py:105
  49.0 6.5 convolution_bitcast_fusion
  59.3 33.3 %all_gather.13 = bf16[192,768]{0,1:T(8,128)(2,1)} all-gather(bf16[192,96]{0,1:T(8,128)(2,1)} %copy.121), channel_id=1, replica_groups=mesh['dp'=8,'mp'=4] {'dp'}, dimensions={1}, use_global_device_ids=true | all-gather | bytes 331776 | tf_op jit(solution)/shard_map/all_gather | solution.py:106
  103.3 4.2 squeeze.20
  109.7 58.2 %while.29 = (s32[]{:T(128)}, bf16[2,3,512,3,64]{2,4,3,1,0:T(8,128)(2,1)}, f32[2,3,3,512]{3,2,1,0:T(4,128)}, bf16[2,3,512,3,64]{2,4,3,1,0:T(8,128)(2,1)S(1)}, bf1...) while((s32[]{:T(128)}, bf16[2,3,512,3,64]{2,4,3,1,0:T(8,128)(2,1)}, ...), condition=%wide.region_5.6_spmd.clone, body=%wide.region_2.5_spmd.sunk.clone | while | flops 1250422272 | bytes 61372616 | solution.py:141
  109.7 8.6 multiply_reduce_fusion.22
  118.2 10.3 %fusion.153 = f32[3,3,512]{2,1,0:T(4,128)} fusion(f32[3,3,512,1024]{3,2,1,0:T(8,128)} %get-tuple-element.527, f32[3,3,512]{2,1,0:T(4,128)} %get-tuple-element.528), kind=kLoop, calls=%fused_computation.4.clone.1.clone | loop fusion | flops 14151168 | bytes 18911232 | tf_op jit(solution)/shard_map/while/body/eval_jaxpr/reduce_sum | solution.py:134
  128.6 9.3 fusion.154
  138.6 8.5 multiply_reduce_fusion.22
  147.1 10.3 %fusion.153 = f32[3,3,512]{2,1,0:T(4,128)} fusion(f32[3,3,512,1024]{3,2,1,0:T(8,128)} %get-tuple-element.527, f32[3,3,512]{2,1,0:T(4,128)} %get-tuple-element.528), kind=kLoop, calls=%fused_computation.4.clone.1.clone | loop fusion | flops 14151168 | bytes 18911232 | tf_op jit(solution)/shard_map/while/body/eval_jaxpr/reduce_sum | solution.py:134
  157.4 9.3 fusion.154
  167.9 4.4 copy.120
  176.2 5.0 convolution_convert_fusion.2
  186.4 88.7 %all-reduce.6.cloned.1.call-done = bf16[3072,768]{1,0:T(8,128)(2,1)} async-done(((bf16[3072,768]{1,0:T(8,128)(2,1)}), bf16[3072,768]{1,0:T(8,128)(2,1)}) %all-reduce.6.cloned.1.call-update) | async-done | bytes 4718608 | tf_op jit(solution)/shard_map/psum | solution.py:143
  275.1 5.5 fusion.42
  284.9 28.7 %multiply_convert_fusion.1 = (bf16[3072,768]{1,0:T(8,128)(2,1)}, f32[3072,768]{1,0:T(8,128)}, f32[3072,768]{1,0:T(8,128)}) fusion(f32[768]{0:T(1024)S(1)} %copy-done.44, bf16[768,768]{1,0:T(8,128)(2,1)} %all-gather.3.cloned.1.call-done, f32[768]{0:T(1024)S(1)} %get-tuple-element.333, f32[768]{0:T(1024)S(1)} %get-tuple-element.334, ...), kind=kOutput, calls=%fused_computation.61 | convolution fusion | flops 3800825856 | bytes 34246656 | tf_op jit(solution)/shard_map/dot_general | solution.py:150
  313.6 8.9 convolution_convert_fusion.1
  323.2 12.0 %psum.63 = s32[]{:T(128)} all-reduce(s32[]{:T(128)} %reduce_sum.243), channel_id=1, replica_groups=mesh['dp'=8,'mp'=4] {'dp'}, use_global_device_ids=true, to_apply=%region_1.0 | all-reduce | flops 1 | bytes 8 | tf_op jit(solution)/shard_map/psum | solution.py:100
  337.7 11.7 %scatter_custom_fusion = f32[3072,768]{1,0:T(8,128)} fusion(s32[768]{0:T(1024)} %fusion.80, f32[768,768]{1,0:T(8,128)S(1)} %bitcast.173, f32[]{:T(128)} %constant.75.clone.1), kind=kCustom, calls=%fused_computation.91 | custom fusion | flops 589824 | bytes 9437696 | tf_op jit(solution)/shard_map/scatter-add | solution.py:164
  349.4 67.5 %all-reduce.8.cloned.1.call-done = bf16[3072,768]{1,0:T(8,128)(2,1)} async-done(((bf16[3072,768]{1,0:T(8,128)(2,1)}), bf16[3072,768]{1,0:T(8,128)(2,1)}) %all-reduce.8.cloned.1.call-update) | async-done | bytes 4718608 | tf_op jit(solution)/shard_map/psum | solution.py:152
  416.9 8.5 fusion.95
  427.8 5.5 multiply_reduce_fusion.2
  433.3 8.4 subtract_multiply_fusion.1
  441.7 15.6 %fusion.99 = (f32[768]{0:T(1024)}, bf16[3072,768]{1,0:T(8,128)(2,1)S(1)}) fusion(f32[3072,768]{1,0:T(8,128)} %get-tuple-element.402, bf16[768,768]{0,1:T(8,128)(2,1)S(1)} %copy-done.50, f32[3072,768]{1,0:T(8,128)} %get-tuple-element.407, f32[3072,768]{1,0:T(8,128)} %get-tuple-element.413, f32[768]{0:T(1024)S(1)} %copy-done.45), kind=kOutput, calls=%fused_computation.191 | convolution fusion | flops 3663985920 | bytes 34215936 | tf_op jit(solution)/shard_map/dot_general | solution.py:24
  459.5 5.6 convolution_convert_fusion
  465.2 94.3 %all-reduce.10.cloned.1.call-done = bf16[3072,768]{1,0:T(8,128)(2,1)} async-done(((bf16[3072,768]{1,0:T(8,128)(2,1)}), bf16[3072,768]{1,0:T(8,128)(2,1)}) %all-reduce.10.cloned.1.call-update) | async-done | bytes 4718608 | tf_op jit(solution)/shard_map/psum | solution.py:173
  559.5 12.0 %multiply_reduce_fusion.3 = (f32[768]{0:T(1024)}, f32[3072]{0:T(1024)S(1)}, f32[3072]{0:T(1024)S(1)}, f32[768]{0:T(1024)}, f32[768]{0:T(1024)}) fusion(f32[3072,768]{1,0:T(8,128)} %get-tuple-element.407, bf16[3072,768]{1,0:T(8,128)(2,1)} %all-reduce.10.cloned.1.call-done, f32[3072]{0:T(1024)S(1)} %copy-done.33, f32[3072]{0:T(1024)S(1)} %broadcast_multiply_fusion.5, ...), kind=kLoop, calls=%fused_computation.51 | loop fusion | flops 37740288 | bytes 23657472 | tf_op jit(solution)/shard_map/reduce_sum | solution.py:48
  571.5 10.0 %fusion.94 = (f32[768]{0:T(1024)}, f32[3072,768]{1,0:T(8,128)S(1)}) fusion(f32[3072]{0:T(1024)S(1)} %broadcast_multiply_fusion, f32[3072]{0:T(1024)S(1)} %broadcast_multiply_fusion.5, f32[768]{0:T(1024)S(1)} %get-tuple-element.335, bf16[3072,768]{1,0:T(8,128)(2,1)} %all-reduce.6.cloned.1.call-done, bf16[3072,768]{1,0:T(8,128)(2,1)} %param.30, ...), kind=kLoop, calls=%fused_computation.187 | loop fusion | flops 33029376 | bytes 33088512 | tf_op jit(solution)/shard_map/reduce_sum | solution.py:182
  588.1 10.4 %fusion.55 = f32[768,768]{0,1:T(8,128)} fusion(bf16[3072,768]{1,0:T(8,128)(2,1)} %get-tuple-element.401, f32[3072,768]{1,0:T(8,128)} %get-tuple-element.407), kind=kOutput, calls=%fused_computation.106 | convolution fusion | flops 3626237952 | bytes 16515072 | tf_op jit(solution)/shard_map/dot_general | solution.py:18
  598.7 11.5 %fusion.52 = f32[768,768]{1,0:T(8,128)} fusion(bf16[3072,768]{1,0:T(8,128)(2,1)} %copy-done.52, f32[768]{0:T(1024)S(1)} %copy-done.41, f32[768]{0:T(1024)S(1)} %copy-done.36, bf16[3072,768]{1,0:T(8,128)(2,1)} %all-reduce.6.cloned.1.call-done, bf16[3072,768]{1,0:T(8,128)(2,1)} %param.30, f32[3072]{0:T(1024)S(1)} %copy-done.33, ...), kind=kOutput, calls=%fused_computation.103 | convolution fusion | flops 3645112320 | bytes 16548864 | tf_op jit(solution)/shard_map/dot_general | solution.py:18
  610.3 5.4 convolution_convert_fusion.3
  617.9 101.9 %while.30 = (s32[]{:T(128)}, f32[3,1024,3,64]{1,3,2,0:T(8,128)}, f32[3,1024,3,64]{1,3,2,0:T(8,128)}, f32[2,3,512,3,64]{2,4,3,1,0:T(8,128)}, bf16[2,3,512,3,64]{2...) while((s32[]{:T(128)}, f32[3,1024,3,64]{1,3,2,0:T(8,128)}, ...), condition=%wide.region_20.21_spmd.clone.clone, body=%wide.region_18.20_spmd.clone.sunk.clone | while | flops 3079761408 | bytes 262011152 | solution.py:230
  618.1 4.1 fusion.164
  622.2 6.5 copy-done
  628.7 6.0 bitcast_add_fusion.7
  634.7 13.3 %multiply_reduce_fusion.23 = (f32[3,3,512]{2,1,0:T(4,128)S(1)}, f32[3,3,512,1024]{3,2,1,0:T(8,128)}) fusion(f32[3,3,512,1024]{3,2,1,0:T(8,128)} %copy-done, f32[3,3,512]{2,1,0:T(4,128)S(1)} %dynamic-slice_bitcast_fusion.3, bf16[3,1024,3,64]{1,3,2,0:T(8,128)(2,1)} %get-tuple-element.603, bf16[2,3,512,3,64]{2,4,3,1,0:T(8,128)(2,1)} %get-tuple-element.602, ...), kind=kOutput, calls=%fused_computation.15.clone.1.clone | convolution fusion | flops 622849536 | bytes 39555076 | tf_op jit(solution)/shard_map/while/body/eval_jaxpr/sbhe,slhe->shbl/dot_general | solution.py:210
  648.0 14.1 %multiply_convert_fusion.4 = bf16[3,3,512,1024]{3,2,1,0:T(8,128)(2,1)S(1)} fusion(f32[3,3,512,1024]{3,2,1,0:T(8,128)} %get-tuple-element.546, f32[3,3,512,1024]{3,2,1,0:T(8,128)} %copy-done, f32[3,3,512]{2,1,0:T(4,128)S(1)} %get-tuple-element.547, f32[3,3,512]{2,1,0:T(4,128)S(1)} %dynamic-slice_bitcast_fusion.3), kind=kLoop, calls=%fused_computation.14.clone.1.clone | loop fusion | flops 23592960 | bytes 47222784 | tf_op jit(solution)/shard_map/while/body/eval_jaxpr/convert_element_type | solution.py:217
  672.3 6.6 copy-done
  678.9 6.8 bitcast_add_fusion.7
  685.7 13.5 %multiply_reduce_fusion.23 = (f32[3,3,512]{2,1,0:T(4,128)S(1)}, f32[3,3,512,1024]{3,2,1,0:T(8,128)}) fusion(f32[3,3,512,1024]{3,2,1,0:T(8,128)} %copy-done, f32[3,3,512]{2,1,0:T(4,128)S(1)} %dynamic-slice_bitcast_fusion.3, bf16[3,1024,3,64]{1,3,2,0:T(8,128)(2,1)} %get-tuple-element.603, bf16[2,3,512,3,64]{2,4,3,1,0:T(8,128)(2,1)} %get-tuple-element.602, ...), kind=kOutput, calls=%fused_computation.15.clone.1.clone | convolution fusion | flops 622849536 | bytes 39555076 | tf_op jit(solution)/shard_map/while/body/eval_jaxpr/sbhe,slhe->shbl/dot_general | solution.py:210
  699.2 14.3 %multiply_convert_fusion.4 = bf16[3,3,512,1024]{3,2,1,0:T(8,128)(2,1)S(1)} fusion(f32[3,3,512,1024]{3,2,1,0:T(8,128)} %get-tuple-element.546, f32[3,3,512,1024]{3,2,1,0:T(8,128)} %copy-done, f32[3,3,512]{2,1,0:T(4,128)S(1)} %get-tuple-element.547, f32[3,3,512]{2,1,0:T(4,128)S(1)} %dynamic-slice_bitcast_fusion.3), kind=kLoop, calls=%fused_computation.14.clone.1.clone | loop fusion | flops 23592960 | bytes 47222784 | tf_op jit(solution)/shard_map/while/body/eval_jaxpr/convert_element_type | solution.py:217
  733.7 4.2 stack_reshape.13
  747.1 6.6 fusion.61
  760.0 8.9 bitcast_convert_fusion
  774.0 37.1 %all-reduce = (f32[2,192]{1,0:T(2,128)S(1)}, f32[768]{0:T(1024)S(1)}, f32[6,768]{1,0:T(8,128)S(1)}) all-reduce(f32[2,192]{1,0:T(2,128)S(1)} %pad_maximum_fusion, f32[768]{0:T(1024)} %get-tuple-element.414, f32[6,768]{1,0:T(8,128)S(1)} %stack.44), channel_id=1, replica_groups=mesh['dp'=8,'mp'=4] {'dp'}, use_global_device_ids=true, to_apply=%region_32.33 | all-reduce | flops 5760 | bytes 46080 | tf_op jit(solution)/shard_map/psum | solution.py:249
  819.8 47.2 %reduce-scatter.13.cloned.1.call-done = f32[96,576]{1,0:T(8,128)} async-done(((f32[768,576]{1,0:T(8,128)}), f32[96,576]{1,0:T(8,128)}) %reduce-scatter.13.cloned.1.call-update) | async-done | bytes 221200
  871.6 12.5 %convert_add_fusion.2 = f32[3072,768]{1,0:T(8,128)} fusion(bf16[3072,768]{1,0:T(8,128)(2,1)} %all-reduce.12.cloned.1.call-done, f32[3072,768]{1,0:T(8,128)} %copy-done.3, f32[3072,768]{1,0:T(8,128)} %scatter_custom_fusion, f32[3072]{0:T(1024)S(1)} %broadcast_subtract_fusion), kind=kLoop, calls=%fused_computation.52 | loop fusion | flops 9437184 | bytes 33042432 | tf_op jit(solution)/shard_map/add | solution.py:242
  884.2 39.5 %psum.71 = f32[]{:T(128)} all-reduce(f32[]{:T(128)S(6)} %add.340), channel_id=1, replica_groups=mesh['dp'=8,'mp'=4] {'dp','mp'}, use_global_device_ids=true, to_apply=%region_45.46 | all-reduce | flops 1 | bytes 8 | tf_op jit(solution)/shard_map/psum | solution.py:262
  (268 shorter events, 122.4 us)
Async XLA Ops:
  8.0 267.0 %all-reduce.6.cloned.1.call-start = ((), (), s32[]{:S(2)}) async-start(), calls=%async_computation.4 | async-start | bytes 9437184 | tf_op jit(solution)/shard_map/psum | solution.py:143
  157.4 9.4 copy-start.25
  167.8 13.4 %copy-start.1 = (bf16[3,1024,3,64]{1,3,2,0:T(8,128)(2,1)}, bf16[3,1024,3,64]{1,3,2,0:T(8,128)(2,1)S(1)}, u32[]{:S(2)}) copy-start(bf16[3,1024,3,64]{1,3,2,0:T(8,128)(2,1)S(1)} %get-tuple-element.614) | copy-start | bytes 3538948
  167.9 13.4 %copy-start.10 = (bf16[3,1024,3,64]{1,3,2,0:T(8,128)(2,1)}, bf16[3,1024,3,64]{1,3,2,0:T(8,128)(2,1)S(1)}, u32[]{:S(2)}) copy-start(bf16[3,1024,3,64]{1,3,2,0:T(8,128)(2,1)S(1)} %get-tuple-element.617) | copy-start | bytes 3538948
  181.2 99.4 %slice-start = ((s8[4718592]{0:T(1024)(128)(4,1)}), s8[524288]{0:T(1024)(128)(4,1)S(1)}, s32[]{:S(2)}) async-start(s8[4718592]{0:T(1024)(128)(4,1)} %bitcast.164), calls=%async_computation.14 | async-start | bytes 1048576
  181.2 103.6 %all-gather.3.cloned.1.call-start = ((), (), s32[]{:S(2)}) async-start(), calls=%async_computation.5 | async-start | bytes 1327104 | tf_op jit(solution)/shard_map/all_gather | solution.py:107
  183.0 130.6 %all-gather.5.cloned.1.call-start = ((), (), s32[]{:S(2)}) async-start(), calls=%async_computation.6 | async-start | bytes 1327104 | tf_op jit(solution)/shard_map/all_gather | solution.py:108
  184.7 232.1 %all-reduce.8.cloned.1.call-start = ((), (), s32[]{:S(2)}) async-start(), calls=%async_computation.7 | async-start | bytes 9437184 | tf_op jit(solution)/shard_map/psum | solution.py:152
  186.4 98.5 %copy-start.35 = (f32[768]{0:T(1024)}, f32[768]{0:T(1024)S(1)}, u32[]{:S(2)}) copy-start(f32[768]{0:T(1024)S(1)} %get-tuple-element.334) | copy-start | bytes 9220
  186.4 98.5 %copy-start.40 = (f32[768]{0:T(1024)}, f32[768]{0:T(1024)S(1)}, u32[]{:S(2)}) copy-start(f32[768]{0:T(1024)S(1)} %get-tuple-element.333) | copy-start | bytes 9220
  275.1 9.8 %copy-start.44 = (f32[768]{0:T(1024)S(1)}, f32[768]{0:T(1024)}, u32[]{:S(2)}) copy-start(f32[768]{0:T(1024)} %param.40) | copy-start | bytes 9220
  284.8 28.7 %copy-start.32 = (f32[3072]{0:T(1024)}, f32[3072]{0:T(1024)S(1)}, u32[]{:S(2)}) copy-start(f32[3072]{0:T(1024)S(1)} %add_rsqrt_fusion.1) | copy-start | bytes 36868
  313.6 22.3 %copy-start.47 = (s32[3,256]{1,0:T(4,128)S(1)}, s32[3,256]{1,0:T(4,128)}, u32[]{:S(2)}) copy-start(s32[3,256]{1,0:T(4,128)} %param.33) | copy-start | bytes 9220
  313.6 23.6 %copy-start.48 = (s32[3]{0:T(128)S(1)}, s32[3]{0:T(128)}, u32[]{:S(2)}) copy-start(s32[3]{0:T(128)} %param.32) | copy-start | bytes 40
  313.6 23.7 %copy-start.23 = (bf16[3,256,768]{2,1,0:T(8,128)(2,1)S(1)}, bf16[3,256,768]{2,1,0:T(8,128)(2,1)}, u32[]{:S(2)}) copy-start(bf16[3,256,768]{2,1,0:T(8,128)(2,1)} %param.34) | copy-start | bytes 3538948
  322.5 237.0 %all-reduce.10.cloned.1.call-start = ((), (), s32[]{:S(2)}) async-start(), calls=%async_computation.8 | async-start | bytes 9437184 | tf_op jit(solution)/shard_map/psum | solution.py:173
  416.8 10.9 %slice-start.4 = ((s8[9437184]{0:T(1024)(128)(4,1)}), s8[4194304]{0:T(1024)(128)(4,1)S(1)}, s32[]{:S(2)}) async-start(s8[9437184]{0:T(1024)(128)(4,1)} %bitcast.168), calls=%async_computation.18 | async-start | bytes 8388608
  416.8 10.9 %slice-start.5 = ((s8[9437184]{0:T(1024)(128)(4,1)}), s8[4194304]{0:T(1024)(128)(4,1)S(1)}, s32[]{:S(2)}) async-start(s8[9437184]{0:T(1024)(128)(4,1)} %bitcast.168), calls=%async_computation.19 | async-start | bytes 8388608
  416.8 10.9 %slice-start.6 = ((s8[9437184]{0:T(1024)(128)(4,1)}), s8[1048576]{0:T(1024)(128)(4,1)S(1)}, s32[]{:S(2)}) async-start(s8[9437184]{0:T(1024)(128)(4,1)} %bitcast.168), calls=%async_computation.20 | async-start | bytes 2097152
  441.7 17.8 %copy-start.49 = (bf16[768,768]{1,0:T(8,128)(2,1)S(1)}, bf16[768,768]{1,0:T(8,128)(2,1)}, u32[]{:S(2)}) copy-start(bf16[768,768]{1,0:T(8,128)(2,1)} %all-gather.3.cloned.1.call-done) | copy-start | bytes 3538948
  459.5 100.0 %copy-start.33 = (f32[3072]{0:T(1024)S(1)}, f32[3072]{0:T(1024)}, u32[]{:S(2)}) copy-start(f32[3072]{0:T(1024)} %copy-done.32) | copy-start | bytes 36868
  459.5 100.0 %copy-start.36 = (f32[768]{0:T(1024)S(1)}, f32[768]{0:T(1024)}, u32[]{:S(2)}) copy-start(f32[768]{0:T(1024)} %copy-done.35) | copy-start | bytes 9220
  465.2 349.7 %reduce-scatter.15.cloned.1.call-start = ((), (), s32[]{:S(2)}) async-start(), calls=%async_computation.13 | async-start | bytes 884736
  559.5 12.0 %copy-start.11 = (bf16[3072,768]{1,0:T(8,128)(2,1)S(1)}, bf16[3072,768]{1,0:T(8,128)(2,1)}, u32[]{:S(2)}) copy-start(bf16[3072,768]{1,0:T(8,128)(2,1)} %all-reduce.10.cloned.1.call-done) | copy-start | bytes 14155780
  571.5 13.6 %copy-start.12 = (bf16[3072,192]{0,1:T(8,128)(2,1)S(1)}, bf16[3072,192]{0,1:T(8,128)(2,1)}, u32[]{:S(2)}) copy-start(bf16[3072,192]{0,1:T(8,128)(2,1)} %convert_element_type.129) | copy-start | bytes 3538948
  588.1 10.6 %copy-start.41 = (f32[768]{0:T(1024)S(1)}, f32[768]{0:T(1024)}, u32[]{:S(2)}) copy-start(f32[768]{0:T(1024)} %copy-done.40) | copy-start | bytes 9220
  588.1 228.4 %reduce-scatter.11.cloned.1.call-start = ((), (), s32[]{:S(2)}) async-start(), calls=%async_computation.11 | async-start | bytes 2654208 | tf_op jit(solution)/shard_map/reduce_scatter | solution.py:247
  598.6 219.5 %reduce-scatter.9.cloned.1.call-start = ((), (), s32[]{:S(2)}) async-start(), calls=%async_computation.10 | async-start | bytes 2654208 | tf_op jit(solution)/shard_map/reduce_scatter | solution.py:246
  598.7 11.6 %copy-start.15 = (bf16[192,768]{0,1:T(8,128)(2,1)S(1)}, bf16[192,768]{0,1:T(8,128)(2,1)}, u32[]{:S(2)}) copy-start(bf16[192,768]{0,1:T(8,128)(2,1)} %all_gather.13) | copy-start | bytes 884740
  610.2 256.7 %reduce-scatter.13.cloned.1.call-start = ((), (), s32[]{:S(2)}) async-start(), calls=%async_computation.12 | async-start | bytes 2211840
  648.0 14.1 %copy-start.6 = (bf16[2,3,512,3,64]{2,4,3,1,0:T(8,128)(2,1)S(1)}, bf16[2,3,512,3,64]{2,4,3,1,0:T(8,128)(2,1)}, u32[]{:S(2)}) copy-start(bf16[2,3,512,3,64]{2,4,3,1,0:T(8,128)(2,1)} %get-tuple-element.599) | copy-start | bytes 3538948 | tf_op jit(solution)/shard_map/while
  648.0 14.1 %copy-start.8 = (f32[3,1024,3,64]{1,3,2,0:T(8,128)S(1)}, f32[3,1024,3,64]{1,3,2,0:T(8,128)}, u32[]{:S(2)}) copy-start(f32[3,1024,3,64]{1,3,2,0:T(8,128)} %get-tuple-element.587) | copy-start | bytes 7077892 | tf_op jit(solution)/shard_map/while
  699.2 14.3 %copy-start.6 = (bf16[2,3,512,3,64]{2,4,3,1,0:T(8,128)(2,1)S(1)}, bf16[2,3,512,3,64]{2,4,3,1,0:T(8,128)(2,1)}, u32[]{:S(2)}) copy-start(bf16[2,3,512,3,64]{2,4,3,1,0:T(8,128)(2,1)} %get-tuple-element.599) | copy-start | bytes 3538948 | tf_op jit(solution)/shard_map/while
  699.2 14.3 %copy-start.8 = (f32[3,1024,3,64]{1,3,2,0:T(8,128)S(1)}, f32[3,1024,3,64]{1,3,2,0:T(8,128)}, u32[]{:S(2)}) copy-start(f32[3,1024,3,64]{1,3,2,0:T(8,128)} %get-tuple-element.587) | copy-start | bytes 7077892 | tf_op jit(solution)/shard_map/while
  719.8 18.2 %copy-start.7 = (f32[3,1024,3,64]{1,3,2,0:T(8,128)S(1)}, f32[3,1024,3,64]{1,3,2,0:T(8,128)}, u32[]{:S(2)}) copy-start(f32[3,1024,3,64]{1,3,2,0:T(8,128)} %get-tuple-element.115) | copy-start | bytes 7077892
  759.6 9.4 copy-start.28
  759.6 9.6 %copy-start.29 = (f32[3,96,192]{2,1,0:T(8,128)S(1)}, f32[3,96,192]{2,1,0:T(8,128)}, u32[]{:S(2)}) copy-start(f32[3,96,192]{2,1,0:T(8,128)} %param.43) | copy-start | bytes 663556
  759.6 9.7 %copy-start.31 = (f32[3072]{0:T(1024)S(1)}, f32[3072]{0:T(1024)}, u32[]{:S(2)}) copy-start(f32[3072]{0:T(1024)} %mul.529) | copy-start | bytes 36868
  759.7 10.4 %copy-start.38 = (f32[768]{0:T(1024)S(1)}, f32[768]{0:T(1024)}, u32[]{:S(2)}) copy-start(f32[768]{0:T(1024)} %get-tuple-element.329) | copy-start | bytes 9220
  759.7 13.2 %copy-start.13 = (f32[2,3,512,3,64]{2,4,3,1,0:T(8,128)S(1)}, f32[2,3,512,3,64]{2,4,3,1,0:T(8,128)}, u32[]{:S(2)}) copy-start(f32[2,3,512,3,64]{2,4,3,1,0:T(8,128)} %get-tuple-element.113) | copy-start | bytes 7077892
  759.7 111.9 %all-reduce.12.cloned.1.call-start = ((), (), s32[]{:S(2)}) async-start(), calls=%async_computation.9 | async-start | bytes 9437184 | tf_op jit(solution)/shard_map/psum | solution.py:242
  871.5 56.5 %copy-start.43 = (f32[2,192]{1,0:T(2,128)S(1)}, f32[2,192]{1,0:T(2,128)}, u32[]{:S(2)}) copy-start(f32[2,192]{1,0:T(2,128)} %param.39) | copy-start | bytes 4612
  871.5 57.8 %copy-start.46 = (f32[768]{0:T(1024)S(1)}, f32[768]{0:T(1024)}, u32[]{:S(2)}) copy-start(f32[768]{0:T(1024)} %param.40) | copy-start | bytes 9220
  871.5 59.2 %copy-start.34 = (f32[6,768]{1,0:T(8,128)S(1)}, f32[6,768]{1,0:T(8,128)}, u32[]{:S(2)}) copy-start(f32[6,768]{1,0:T(8,128)} %param.41) | copy-start | bytes 55300
  871.6 62.3 %copy-start.18 = (f32[768,96]{0,1:T(8,128)S(1)}, f32[768,96]{0,1:T(8,128)}, u32[]{:S(2)}) copy-start(f32[768,96]{0,1:T(8,128)} %param.38) | copy-start | bytes 884740
  871.6 62.3 %copy-start.20 = (f32[768,96]{0,1:T(8,128)S(1)}, f32[768,96]{0,1:T(8,128)}, u32[]{:S(2)}) copy-start(f32[768,96]{0,1:T(8,128)} %reduce-scatter.11.cloned.1.call-done) | copy-start | bytes 884740
  871.6 64.4 %copy-start.19 = (f32[96,768]{1,0:T(8,128)S(1)}, f32[96,768]{1,0:T(8,128)}, u32[]{:S(2)}) copy-start(f32[96,768]{1,0:T(8,128)} %param.37) | copy-start | bytes 884740
  871.6 64.4 %copy-start.21 = (f32[96,768]{1,0:T(8,128)S(1)}, f32[96,768]{1,0:T(8,128)}, u32[]{:S(2)}) copy-start(f32[96,768]{1,0:T(8,128)} %reduce-scatter.9.cloned.1.call-done) | copy-start | bytes 884740
  (31 other events, 176.0 us)
Sparse Core Ops, SparseCore 0:
  181.3 93.6 all-reduce.5
  322.7 94.1 all-reduce.7
  465.3 94.1 all-reduce.9
  769.0 94.0 all-reduce.11
Sparse Core Ops, SparseCore 1:
  184.5 40.8 all-gather.2
  228.0 39.6 all-gather.4
  588.2 63.4 reduce-scatter.14
  655.1 69.0 reduce-scatter.10
  727.7 69.2 reduce-scatter.8
  800.4 66.5 reduce-scatter.12
where the time goes:
time: 951 us; the launch traced here: 947 us
  waiting for transfers between devices  298 us (31%)
  matrix products  212 us (22%)
  other arithmetic  163 us (17%)
  blocking collectives  161 us (17%)
  local copies, waits for them, and re-layouts  88 us (9%)
  between operations  23.5 us (2%)
    psum x1, waiting for transfers between devices, shards(): lax.psum(col_contract(inner_grad_low, wexp).astype(jnp.bfloat16), 'mp')  94.3 us
    psum x1, waiting for transfers between devices, shards(): lax.psum(jnp.dot(outputs_low, wcomb, preferred_element_type=f32).astype(j...  88.7 us
    psum x1, waiting for transfers between devices, shards(): lax.psum(jnp.dot(hidden_low, wred, preferred_element_type=f32).astype(jnp...  67.5 us
    unnamed x12, waiting for transfers between devices  47.4 us
    psum x1, blocking collectives, shards(): total_squares = lax.psum(term, ('dp', 'mp'))  39.5 us
    all_gather x1, blocking collectives, shards(): lax.all_gather(projections.astype(bf16), 'dp', axis=1, tiled=True)  38.7 us
    psum x1, blocking collectives, shards(): lax.psum((grad_offsets, grad_shifts, grad_vectors), 'dp')  37.1 us
    all_gather x1, blocking collectives, shards(): lax.all_gather(combiner.astype(bf16), 'dp', axis=1, tiled=True)  33.3 us
  transfers between devices with their start and end apart: 10, of which 4 were waited for; matrix products, arithmetic and copies ran while one was open for 25% of the time, Pallas kernels for 0%

commit v1 on v0

v1 whole, which is shorter than its diff:
```python
import functools

import jax
import jax.numpy as jnp
from jax import lax
from jax.experimental import pallas as pl
from jax.experimental.pallas import tpu as pltpu
from jax.sharding import PartitionSpec as P

HD = 64
STEP = 10
LEN = 1024
WIDTH = 768
BLK = 256

clip_limit = 10.0
learn_rate = 0.05
vector_rate = 0.3
decay_rate = 0.01
adam_eps = 1e-06

MESH = pl.DeviceIdType.MESH
bf16 = jnp.bfloat16
f32 = jnp.float32
HBM = pl.BlockSpec(memory_space=pl.ANY)
VM = pl.BlockSpec(memory_space=pltpu.VMEM)
SM = pl.BlockSpec(memory_space=pltpu.SMEM)
DMA = pltpu.SemaphoreType.DMA
VMEM_CAP = 60 * 1024 * 1024


def dot(left, right):
    return jnp.dot(left, right, preferred_element_type=f32)


def dot_t(left, right):
    return lax.dot_general(left, right, (((1,), (1,)), ((), ())), preferred_element_type=f32)


def place():
    dp = lax.axis_index("dp")
    mp = lax.axis_index("mp")
    return dp // 2, lax.rem(dp, 2), mp // 2, lax.rem(mp, 2)


def dev(z, x, y, c):
    return {"dp": z * 2 + x, "mp": y * 2 + c}


def remote(src, dst, send, recv, where):
    return pltpu.make_async_remote_copy(
        src_ref=src, dst_ref=dst, send_sem=send, recv_sem=recv, device_id=where, device_id_type=MESH
    )


def greet(peers):
    barrier = pltpu.get_barrier_semaphore()
    for peer in peers:
        pl.semaphore_signal(barrier, inc=1, device_id=peer, device_id_type=MESH)
    pl.semaphore_wait(barrier, len(peers))


def start(copies):
    for copy in copies:
        copy.start()


def arrived(copies):
    for copy in copies:
        copy.wait_recv()


def sent(copies):
    for copy in copies:
        copy.wait_send()


def gather_kernel(nz, full, *refs):
    n = len(full)
    shards, (small, keep) = refs[:n], refs[n : n + 2]
    outs, (small_out, keep_out) = refs[n + 2 : 2 * n + 2], refs[2 * n + 2 : 2 * n + 4]
    zs, zr, two_s, two_r, three_s, three_r, core_s, core_r, local, small_s, small_r, keep_s, keep_r = refs[
        2 * n + 4 :
    ]
    z, x, y, c = place()
    others = [dev(lax.rem(z + d, nz), x, y, c) for d in range(1, nz)]
    along_x, along_y, along_c = dev(z, 1 - x, y, c), dev(z, x, 1 - y, c), dev(z, x, y, 1 - c)
    greet(others + [along_x, along_y, along_c])
    chunks = [(a, h) for a in range(n) for h in range(2)]
    own = [outs[a].at[c] if full[a] else outs[a] for a in range(n)]
    locals_ = [pltpu.make_async_copy(shards[a], own[a].at[y, z, x], local.at[a]) for a in range(n)]
    start(locals_)

    def stage_z(i):
        a, h = chunks[i]
        return [
            remote(shards[a].at[h], own[a].at[y, z, x, h], zs.at[i, d - 1], zr.at[i, d - 1], others[d - 1])
            for d in range(1, nz)
        ]

    def stage_two(i):
        a, h = chunks[i]
        block = own[a].at[y, :, x, h]
        return [remote(block, block, two_s.at[i], two_r.at[i], along_x if h == 0 else along_y)]

    def stage_three(i):
        a, h = chunks[i]
        block = own[a].at[y, :, :, h] if h == 0 else own[a].at[:, :, x, h]
        return [remote(block, block, three_s.at[i], three_r.at[i], along_y if h == 0 else along_x)]

    def stage_core(i):
        a, h = chunks[i]
        if not full[a]:
            return []
        block = own[a].at[:, :, :, h]
        return [remote(block, block, core_s.at[i], core_r.at[i], along_c)]

    total = len(chunks)
    first = [stage_z(i) for i in range(total)]
    keep_first = [
        remote(keep, keep_out.at[z, x], keep_s.at[d - 1], keep_r.at[d - 1], others[d - 1]) for d in range(1, nz)
    ]
    small_first = [remote(small, small_out.at[c, y], small_s.at[0], small_r.at[0], along_y)]
    own_small = [
        pltpu.make_async_copy(small, small_out.at[c, y], local.at[n]),
        pltpu.make_async_copy(keep, keep_out.at[z, x], local.at[n + 1]),
    ]
    start(own_small)
    start(first[0] + first[1] + keep_first + small_first)
    for i in range(2, total):
        start(first[i])
    for copy in locals_ + own_small:
        copy.wait()
    arrived(keep_first + small_first)
    keep_second = [remote(keep_out.at[:, x], keep_out.at[:, x], keep_s.at[nz - 1], keep_r.at[nz - 1], along_x)]
    small_second = [remote(small_out.at[c], small_out.at[c], small_s.at[1], small_r.at[1], along_c)]
    start(keep_second + small_second)
    second, third, fourth = [None] * total, [None] * total, [None] * total
    for step in range(total + 3):
        if step < total:
            arrived(first[step])
            second[step] = stage_two(step)
            start(second[step])
        if 0 <= step - 1 < total:
            arrived(second[step - 1])
            third[step - 1] = stage_three(step - 1)
            start(third[step - 1])
        if 0 <= step - 2 < total:
            arrived(third[step - 2])
            fourth[step - 2] = stage_core(step - 2)
            start(fourth[step - 2])
        if 0 <= step - 3 < total:
            arrived(fourth[step - 3])
    arrived(keep_second + small_second)
    for i in range(total):
        sent(first[i] + second[i] + third[i] + fourth[i])
    sent(keep_first + small_first + keep_second + small_second)


def gather(shards, full, small, keep, nz):
    n = len(shards)
    shapes = [
        jax.ShapeDtypeStruct(((2,) if f else ()) + (2, nz, 2) + s.shape, s.dtype) for s, f in zip(shards, full)
    ]
    shapes += [
        jax.ShapeDtypeStruct((2, 2) + small.shape, f32),
        jax.ShapeDtypeStruct((nz, 2) + keep.shape, f32),
    ]
    return pl.pallas_call(
        functools.partial(gather_kernel, nz, full),
        out_shape=shapes,
        in_specs=[VM] * (n + 2),
        out_specs=[HBM] * (n + 2),
        scratch_shapes=[DMA((2 * n, nz - 1)), DMA((2 * n, nz - 1))]
        + [DMA((2 * n,))] * 6
        + [DMA((n + 2,)), DMA((2,)), DMA((2,)), DMA((nz,)), DMA((nz,))],
        compiler_params=pltpu.CompilerParams(collective_id=1, has_side_effects=True),
        name="gather_weights",
    )(*shards, small, keep)


def attend_kernel(x_ref, w_ref, b_ref, qkv_ref, out_ref, lse_ref, rows, sem):
    y = lax.axis_index("mp") // 2
    copies = [
        pltpu.make_async_copy(x_ref.at[pl.ds(pl.multiple_of(y * LEN, LEN), LEN)], rows.at[pl.ds(0, LEN)], sem.at[0]),
        pltpu.make_async_copy(x_ref.at[pl.ds(2 * LEN, LEN)], rows.at[pl.ds(LEN, LEN)], sem.at[1]),
    ]
    start(copies)
    for copy in copies:
        copy.wait()

    def project(i, carry):
        at = pl.ds(pl.multiple_of(i * BLK, BLK), BLK)
        qkv_ref[at, :] = (dot(rows[at, :], w_ref[...]) + b_ref[...]).astype(bf16)
        return carry

    lax.fori_loop(0, 2 * LEN // BLK, project, 0)
    lane = lax.broadcasted_iota(jnp.int32, (BLK, 128), 1)
    ones = jnp.ones((LEN, 128), bf16)

    def unit(i, carry):
        u, p = i // 3, lax.rem(i, 3)
        shared = u >= LEN // BLK
        q_row = pl.multiple_of(jnp.where(shared, 512 * y, 0) + u * BLK, BLK)
        kv_row = pl.multiple_of(jnp.where(shared, LEN, 0), LEN)
        col = pl.multiple_of(p * 128, 128)
        query = qkv_ref[pl.ds(q_row, BLK), pl.ds(col, 128)]
        key = qkv_ref[pl.ds(kv_row, LEN), pl.ds(pl.multiple_of(col + 384, 128), 128)]
        value = qkv_ref[pl.ds(kv_row, LEN), pl.ds(pl.multiple_of(col + 768, 128), 128)]
        wide = jnp.concatenate([value, ones], axis=1)
        parts = []
        lse = jnp.where(p == 0, 0.0, lse_ref[pl.ds(pl.multiple_of(u * BLK, BLK), BLK), :])
        for h in range(2):
            mine = (lane < 64) if h == 0 else (lane >= 64)
            q_head = jnp.where(mine, query * bf16(0.125), bf16(0.0))
            scores = dot_t(q_head, key)
            top = jnp.max(scores, -1, keepdims=True)
            weight = jnp.exp(scores - top)
            both = dot(weight.astype(bf16), wide)
            total = both[:, 128:]
            parts.append(both[:, :128] / total)
            lse = jnp.where(lane == 2 * p + h, top + jnp.log(total), lse)
        out_ref[pl.ds(pl.multiple_of(u * BLK, BLK), BLK), pl.ds(col, 128)] = jnp.where(
            lane < 64, parts[0], parts[1]
        ).astype(bf16)
        lse_ref[pl.ds(pl.multiple_of(u * BLK, BLK), BLK), :] = lse
        return carry

    lax.fori_loop(0, 18, unit, 0)


def attend(activations, weights, bias):
    return pl.pallas_call(
        attend_kernel,
        out_shape=[
            jax.ShapeDtypeStruct((2 * LEN, 1152), bf16),
            jax.ShapeDtypeStruct((1536, 384), bf16),
            jax.ShapeDtypeStruct((1536, 128), f32),
        ],
        in_specs=[HBM, VM, VM],
        out_specs=[VM] * 3,
        scratch_shapes=[pltpu.VMEM((2 * LEN, WIDTH), bf16), DMA((2,))],
        compiler_params=pltpu.CompilerParams(vmem_limit_bytes=VMEM_CAP),
        name="attend",
    )(activations, weights, bias)


def rows_of(c):
    return [
        (pl.ds(pl.multiple_of(512 * c, 512), 512), pl.ds(0, 512)),
        (pl.ds(pl.multiple_of(LEN + 256 * c, 256), 256), pl.ds(512, 256)),
    ]


def to_rows_kernel(heads_ref, rows_ref, send, recv, local):
    z, x, y, c = place()
    peer = dev(z, x, y, 1 - c)
    greet([peer])
    out = [
        remote(heads_ref.at[there], rows_ref.at[c, here], send.at[i], recv.at[i], peer)
        for i, (there, here) in enumerate(rows_of(1 - c))
    ]
    start(out)
    kept = [
        pltpu.make_async_copy(heads_ref.at[there], rows_ref.at[c, here], local.at[i])
        for i, (there, here) in enumerate(rows_of(c))
    ]
    start(kept)
    for copy in kept + out:
        copy.wait()


def to_heads_kernel(rows_ref, heads_ref, send, recv, local):
    z, x, y, c = place()
    peer = dev(z, x, y, 1 - c)
    greet([peer])
    out = [
        remote(rows_ref.at[1 - c, here], heads_ref.at[there], send.at[i], recv.at[i], peer)
        for i, (there, here) in enumerate(rows_of(c))
    ]
    start(out)
    kept = [
        pltpu.make_async_copy(rows_ref.at[c, here], heads_ref.at[there], local.at[i])
        for i, (there, here) in enumerate(rows_of(c))
    ]
    start(kept)
    for copy in kept + out:
        copy.wait()


def exchange(kernel, value, shape, cid, name):
    return pl.pallas_call(
        kernel,
        out_shape=jax.ShapeDtypeStruct(shape, bf16),
        in_specs=[VM],
        out_specs=VM,
        scratch_shapes=[DMA((2,)), DMA((2,)), DMA((2,))],
        compiler_params=pltpu.CompilerParams(collective_id=cid, has_side_effects=True),
        name=name,
    )(value)


def erf_parts(value):
    size = jnp.abs(value)
    turn = 1.0 / (1.0 + (0.3275911 * 0.7071067811865476) * size)
    bell = jnp.exp(-0.5 * value * value)
    poly = turn * (
        0.5 * 0.254829592
        + turn
        * (
            0.5 * -0.284496736
            + turn * (0.5 * 1.421413741 + turn * (0.5 * -1.453152027 + turn * (0.5 * 1.061405429)))
        )
    )
    tail = poly * bell
    cdf = jnp.where(value >= 0.0, 1.0 - tail, tail)
    return cdf, bell


def norm(value):
    mean = jnp.mean(value, -1, keepdims=True)
    centered = value - mean
    rstd = lax.rsqrt(jnp.mean(centered * centered, -1, keepdims=True) + 1e-05)
    return centered * rstd, rstd


def norm_back(grad, unit, rstd, gain):
    scaled = grad * gain
    return rstd * (
        scaled - jnp.mean(scaled, -1, keepdims=True) - unit * jnp.mean(scaled * unit, -1, keepdims=True)
    )


def column(value):
    return jnp.sum(value, 0, keepdims=True)


def middle_kernel(
    share_ref,
    count_ref,
    att_ref,
    wo_ref,
    w1_ref,
    w2_ref,
    shift_ref,
    vec_ref,
    x_ref,
    pos_ref,
    cot_ref,
    out_ref,
    resid_ref,
    datt_ref,
    dwo_ref,
    dw1_ref,
    dw2_ref,
    dshift_ref,
    dvec_ref,
    x_own,
    cot_own,
    unit1,
    rstd1,
    norm1,
    low1,
    low1_t,
    hidden,
    slope,
    total,
    d2,
    d2_low,
    d2_low_t,
    inner_low,
    sem,
):
    dp = lax.axis_index("dp")
    mp = lax.axis_index("mp")
    y, c = mp // 2, lax.rem(mp, 2)
    copies = [
        pltpu.make_async_copy(
            x_ref.at[pl.ds(pl.multiple_of(y * LEN + 512 * c, 512), 512)], x_own.at[pl.ds(0, 512)], sem.at[0]
        ),
        pltpu.make_async_copy(
            x_ref.at[pl.ds(pl.multiple_of(2 * LEN + 512 * y + 256 * c, 256), 256)],
            x_own.at[pl.ds(512, 256)],
            sem.at[1],
        ),
        pltpu.make_async_copy(cot_ref.at[y], cot_own.at[0], sem.at[2]),
        pltpu.make_async_copy(cot_ref.at[2], cot_own.at[1], sem.at[3]),
    ]
    start(copies)
    for copy in copies:
        copy.wait()
    blocks = WIDTH // BLK

    def vec(i):
        return vec_ref[pl.ds(i, 1), :]

    def at(b):
        return pl.ds(pl.multiple_of(b * BLK, BLK), BLK)

    def one(b, carry):
        value = dot_t(att_ref[0, at(b), :], wo_ref[0]) + dot_t(att_ref[1, at(b), :], wo_ref[1])
        first = x_own[at(b), :].astype(f32) + (value + vec(0))
        unit, rstd = norm(first)
        unit1[at(b), :] = unit
        rstd1[at(b), :] = jnp.broadcast_to(rstd, (BLK, 128))
        normed = unit * vec(2) + vec(3)
        norm1[at(b), :] = normed
        low = normed.astype(bf16)
        low1[at(b), :] = low
        low1_t[:, at(b)] = low.T
        return carry

    lax.fori_loop(0, blocks, one, 0)

    def two(i, carry):
        j, b = i // blocks, lax.rem(i, blocks)
        inner = dot(low1[at(b), :], w1_ref[j]) + shift_ref[j]
        cdf, bell = erf_parts(inner)
        low = (inner * cdf).astype(bf16)
        hidden[j, at(b), :] = low
        slope[j, at(b), :] = cdf + inner * (bell * 0.3989422804014327)
        part = dot_t(low, w2_ref[j])
        total[at(b), :] = jnp.where(j == 0, part, total[at(b), :] + part)
        return carry

    lax.fori_loop(0, 4 * blocks, two, 0)
    dvec_ref[...] = jnp.zeros_like(dvec_ref)

    def three(b, carry):
        second = norm1[at(b), :] + (total[at(b), :] + vec(1))
        unit, rstd = norm(second)
        final = unit * vec(4) + vec(5)
        which = jnp.where(b == 2, 1, 0)
        seq = jnp.where(b == 2, 2, y)
        share = share_ref[seq]
        inputs = x_own[at(b), :].astype(f32)
        out_ref[at(b), :] = (inputs + share * (final - inputs)).astype(bf16)
        base = jnp.where(b == 2, 512 * y + 256 * c, 512 * c + b * BLK)
        slots = pos_ref.shape[1]
        row = lax.broadcasted_iota(jnp.int32, (BLK, slots), 0) + base
        slot = lax.broadcasted_iota(jnp.int32, (BLK, slots), 1)
        hit = (pos_ref[pl.ds(seq, 1), :] == row) & (slot < count_ref[seq])
        target = dot(jnp.where(hit, 1.0, 0.0).astype(bf16), cot_own[which])
        up = share * target
        resid_ref[at(b), :] = (1.0 - share) * target
        grad = norm_back(up, unit, rstd, vec(4))
        d2[at(b), :] = grad
        low = grad.astype(bf16)
        d2_low[at(b), :] = low
        d2_low_t[:, at(b)] = low.T
        dvec_ref[pl.ds(1, 1), :] += column(grad)
        dvec_ref[pl.ds(4, 1), :] += column(up * unit)
        dvec_ref[pl.ds(5, 1), :] += column(up)
        return carry

    lax.fori_loop(0, blocks, three, 0)
    dshift_ref[...] = jnp.zeros_like(dshift_ref)

    def four(j, carry):
        def rows(b, carry):
            grad = dot(d2_low[at(b), :], w2_ref[j]) * slope[j, at(b), :]
            low = grad.astype(bf16)
            inner_low[at(b), :] = low
            dshift_ref[j] += column(grad)
            part = dot_t(low, w1_ref[j])
            d2[at(b), :] += part
            return carry

        lax.fori_loop(0, blocks, rows, 0)

        def grads(b, carry):
            dw2_ref[j, at(b), :] = dot(d2_low_t[at(b), :], hidden[j]).astype(bf16)
            dw1_ref[j, at(b), :] = dot(low1_t[at(b), :], inner_low[...]).astype(bf16)
            return carry

        lax.fori_loop(0, blocks, grads, 0)
        return carry

    lax.fori_loop(0, 4, four, 0)

    def five(b, carry):
        grad = d2[at(b), :]
        unit = unit1[at(b), :]
        first = norm_back(grad, unit, rstd1[at(b), :][:, :1], vec(2))
        dvec_ref[pl.ds(0, 1), :] += column(first)
        dvec_ref[pl.ds(2, 1), :] += column(grad * unit)
        dvec_ref[pl.ds(3, 1), :] += column(grad)
        resid_ref[at(b), :] += first
        low = first.astype(bf16)
        d2_low_t[:, at(b)] = low.T
        for p in range(2):
            datt_ref[p, at(b), :] = dot(low, wo_ref[p]).astype(bf16)
        return carry

    lax.fori_loop(0, blocks, five, 0)

    def six(b, carry):
        for p in range(2):
            dwo_ref[p, at(b), :] = dot(d2_low_t[at(b), :], att_ref[p]).astype(bf16)
        return carry

    lax.fori_loop(0, blocks, six, 0)


def middle(shares, counts, att, wo, w1, w2, shifts, vectors, activations, positions, cotangents):
    slots = positions.shape[1]
    big = (WIDTH, WIDTH)
    return pl.pallas_call(
        middle_kernel,
        out_shape=[
            jax.ShapeDtypeStruct(big, bf16),
            jax.ShapeDtypeStruct(big, f32),
            jax.ShapeDtypeStruct((2, WIDTH, 384), bf16),
            jax.ShapeDtypeStruct((2, WIDTH, 384), bf16),
            jax.ShapeDtypeStruct((4,) + big, bf16),
            jax.ShapeDtypeStruct((4,) + big, bf16),
            jax.ShapeDtypeStruct((4, 1, WIDTH), f32),
            jax.ShapeDtypeStruct((8, WIDTH), f32),
        ],
        in_specs=[SM, SM, VM, VM, VM, VM, VM, VM, HBM, VM, HBM],
        out_specs=[VM] * 8,
        scratch_shapes=[
            pltpu.VMEM(big, bf16),
            pltpu.VMEM((2, slots, WIDTH), bf16),
            pltpu.VMEM(big, f32),
            pltpu.VMEM((WIDTH, 128), f32),
            pltpu.VMEM(big, f32),
            pltpu.VMEM(big, bf16),
            pltpu.VMEM(big, bf16),
            pltpu.VMEM((4,) + big, bf16),
            pltpu.VMEM((4,) + big, f32),
            pltpu.VMEM(big, f32),
            pltpu.VMEM(big, f32),
            pltpu.VMEM(big, bf16),
            pltpu.VMEM(big, bf16),
            pltpu.VMEM(big, bf16),
            DMA((4,)),
        ],
        compiler_params=pltpu.CompilerParams(vmem_limit_bytes=VMEM_CAP),
        name="middle",
    )(shares, counts, att, wo, w1, w2, shifts, vectors, activations, positions, cotangents)


def back_kernel(
    x_ref, w_ref, qkv_ref, out_ref, lse_ref, dout_ref, dw_ref, dx_ref, doff_ref, rows, rows_t, grads, key_t, stats, dk, dv, sem
):
    y = lax.axis_index("mp") // 2
    copies = [
        pltpu.make_async_copy(x_ref.at[pl.ds(pl.multiple_of(y * LEN, LEN), LEN)], rows.at[pl.ds(0, LEN)], sem.at[0]),
        pltpu.make_async_copy(x_ref.at[pl.ds(2 * LEN, LEN)], rows.at[pl.ds(LEN, LEN)], sem.at[1]),
    ]
    start(copies)
    for copy in copies:
        copy.wait()
    spot = lax.broadcasted_iota(jnp.int32, (8, 384), 0)
    head = (lax.broadcasted_iota(jnp.int32, (8, 384), 1)) // HD
    pick = jnp.where(spot == head, 1.0, 0.0).astype(bf16)

    def at(b):
        return pl.ds(pl.multiple_of(b * BLK, BLK), BLK)

    def prepare(u, carry):
        both = out_ref[at(u), :].astype(f32) * dout_ref[at(u), :].astype(f32)
        high = both.astype(bf16)
        low = (both - high.astype(f32)).astype(bf16)
        stats[0, u] = lse_ref[at(u), :].T[:8, :]
        stats[1, u] = dot_t(pick, high) + dot_t(pick, low)
        return carry

    lax.fori_loop(0, 6, prepare, 0)

    def turn(i, carry):
        rows_t[:, at(i)] = rows[at(i), :].T
        grads[at(i), :] = jnp.zeros((BLK, 1152), bf16)
        return carry

    lax.fori_loop(0, 2 * LEN // BLK, turn, 0)
    doff_ref[...] = jnp.zeros_like(doff_ref)
    lane = lax.broadcasted_iota(jnp.int32, (BLK, 128), 1)
    sub = lax.broadcasted_iota(jnp.int32, (128, BLK), 0)

    for s in range(2):
        n_units = 4 if s == 0 else 2
        kv_row = s * LEN

        def pair(p, carry, n_units=n_units, kv_row=kv_row, s=s):
            col = pl.multiple_of(p * 128, 128)
            k_col = pl.ds(pl.multiple_of(col + 384, 128), 128)
            v_col = pl.ds(pl.multiple_of(col + 768, 128), 128)
            key_t[...] = qkv_ref[pl.ds(kv_row, LEN), k_col].T
            dk[...] = jnp.zeros_like(dk)
            dv[...] = jnp.zeros_like(dv)

            def unit(i, carry):
                u = i + 4 * s
                q_row = pl.multiple_of((512 * y if s else 0) + u * BLK, BLK)
                query = qkv_ref[pl.ds(q_row, BLK), pl.ds(col, 128)] * bf16(0.125)
                grad = dout_ref[at(u), pl.ds(col, 128)]
                key = qkv_ref[pl.ds(kv_row, LEN), k_col]
                value = qkv_ref[pl.ds(kv_row, LEN), v_col]
                parts = []
                for h in range(2):
                    mine = (lane < 64) if h == 0 else (lane >= 64)
                    q_head = jnp.where(mine, query, bf16(0.0))
                    g_head = jnp.where(mine, grad, bf16(0.0))
                    lse = stats[0, u, pl.ds(2 * p + h, 1), :]
                    delta = stats[1, u, pl.ds(2 * p + h, 1), :]
                    probs = jnp.exp(dot_t(key, q_head) - lse)
                    slopes = dot_t(value, g_head)
                    dv[...] += dot(probs.astype(bf16), g_head)
                    low = (probs * (slopes - delta)).astype(bf16)
                    dk[...] += dot(low, q_head)
                    parts.append(dot(key_t[...], low))
                dq = (jnp.where(sub < 64, parts[0], parts[1]) * 0.125).T
                doff_ref[pl.ds(0, 1), pl.ds(col, 128)] += column(dq)
                grads[pl.ds(q_row, BLK), pl.ds(col, 128)] = dq.astype(bf16)
                return carry

            lax.fori_loop(0, n_units, unit, 0)
            grads[pl.ds(kv_row, LEN), k_col] = dk[...].astype(bf16)
            grads[pl.ds(kv_row, LEN), v_col] = dv[...].astype(bf16)
            doff_ref[pl.ds(1, 1), pl.ds(col, 128)] += column(dv[...])
            return carry

        lax.fori_loop(0, 3, pair, 0)

    def inputs(i, carry):
        dx_ref[at(i), :] = dot_t(grads[at(i), :], w_ref[...]).astype(bf16)
        return carry

    lax.fori_loop(0, 2 * LEN // BLK, inputs, 0)

    def weights(i, carry):
        b, k = i // 3, lax.rem(i, 3)
        col = pl.ds(pl.multiple_of(k * 384, 128), 384)
        dw_ref[at(b), col] = dot(rows_t[at(b), :], grads[:, col]).astype(bf16)
        return carry

    lax.fori_loop(0, 9, weights, 0)


def back(activations, weights, qkv, out, lse, dout):
    return pl.pallas_call(
        back_kernel,
        out_shape=[
            jax.ShapeDtypeStruct((WIDTH, 1152), bf16),
            jax.ShapeDtypeStruct((2 * LEN, WIDTH), bf16),
            jax.ShapeDtypeStruct((8, 384), f32),
        ],
        in_specs=[HBM] + [VM] * 5,
        out_specs=[VM] * 3,
        scratch_shapes=[
            pltpu.VMEM((2 * LEN, WIDTH), bf16),
            pltpu.VMEM((WIDTH, 2 * LEN), bf16),
            pltpu.VMEM((2 * LEN, 1152), bf16),
            pltpu.VMEM((128, LEN), bf16),
            pltpu.VMEM((2, 6, 8, BLK), f32),
            pltpu.VMEM((LEN, 128), f32),
            pltpu.VMEM((LEN, 128), f32),
            DMA((2,)),
        ],
        compiler_params=pltpu.CompilerParams(vmem_limit_bytes=VMEM_CAP),
        name="attend_back",
    )(activations, weights, qkv, out, lse, dout)


def tail_kernel(nz, full, *refs):
    n = len(full)
    refs = list(refs)

    def take(count):
        head = refs[:count]
        del refs[:count]
        return head

    partial = take(n)
    small, dx, resid, layer = take(4)
    outs = take(n)
    small_out, norm_out, layer_out, input_out = take(4)
    gap = take(2 * n)
    whole = take(2 * n)
    recv_two = take(2 * n)
    sum_two = take(2 * n)
    recv_three = take(2 * n)
    sum_three = take(2 * n)
    recv_z = take(2 * n)
    small_buf, small_in, small_z, norm_buf, norm_in, norm_z, dx_in, dx_sum, dx_y, mine = take(10)
    core_s, core_r, two_s, two_r, three_s, three_r, zs, zr, bs, br, bzs, bzr, os, orr, local = take(15)
    z, x, y, c = place()
    others = [dev(lax.rem(z + d, nz), x, y, c) for d in range(1, nz)]
    along_x, along_y, along_c = dev(z, 1 - x, y, c), dev(z, x, 1 - y, c), dev(z, x, y, 1 - c)
    greet(others + [along_x, along_y, along_c])
    chunks = [(a, h) for a in range(n) for h in range(2)]
    total = len(chunks)
    span = 2 * nz * 2

    def row_sets(yy, cc):
        return [
            (pl.ds(pl.multiple_of(yy * LEN + 512 * cc, 512), 512), pl.ds(0, 512)),
            (pl.ds(pl.multiple_of(2 * LEN + 512 * yy + 256 * cc, 256), 256), pl.ds(512, 256)),
        ]

    def spread(source, target, k):
        first = [
            remote(source.at[here], target.at[there], os.at[k + i], orr.at[k + i], along_y)
            for i, (there, here) in enumerate(row_sets(y, c))
        ]
        second = [
            remote(source.at[here], target.at[there], os.at[k + 2 + i], orr.at[k + 2 + i], along_c)
            for i, (there, here) in enumerate(row_sets(y, c))
        ]
        third = [
            remote(target.at[there], target.at[there], os.at[k + 4 + i], orr.at[k + 4 + i], along_c)
            for i, (there, here) in enumerate(row_sets(1 - y, c))
        ]
        kept = [
            pltpu.make_async_copy(source.at[here], target.at[there], local.at[k // 3 + i])
            for i, (there, here) in enumerate(row_sets(y, c))
        ]
        return first, second, third, kept

    dx_core = [
        remote(
            dx.at[pl.ds(pl.multiple_of(512 * (1 - c), 512), 512)], dx_in.at[pl.ds(0, 512)], os.at[12], orr.at[12], along_c
        )
    ] + [
        remote(
            dx.at[pl.ds(pl.multiple_of(LEN + 512 * yy + 256 * (1 - c), 256), 256)],
            dx_in.at[pl.ds(512 + 256 * yy, 256)],
            os.at[13 + yy],
            orr.at[13 + yy],
            along_c,
        )
        for yy in range(2)
    ]
    start(dx_core)

    def core_stage(i):
        a, h = chunks[i]
        if not full[a]:
            return []
        return [remote(partial[a].at[1 - c, :, :, :, h], gap[i], core_s.at[i], core_r.at[i], along_c)]

    first = [core_stage(i) for i in range(total)]
    for copies in first:
        start(copies)
    lay_first, lay_second, lay_third, lay_kept = spread(layer, layer_out, 0)
    start(lay_kept + lay_second)

    def butterfly(buf, inn, slots, k):
        for stage, peer in enumerate((along_c, along_y, along_x)):
            copy = remote(buf.at[stage], inn.at[stage], bs.at[k + stage], br.at[k + stage], peer)
            copy.start()
            copy.wait()
            buf[stage + 1] = buf[stage] + inn[stage]
        slots[z] = buf[3]
        copies = [
            remote(buf.at[3], slots.at[z], bzs.at[k // 3, d - 1], bzr.at[k // 3, d - 1], others[d - 1])
            for d in range(1, nz)
        ]
        start(copies)
        for copy in copies:
            copy.wait()
        acc = slots[0]
        for d in range(1, nz):
            acc = acc + slots[d]
        return acc

    def split(i):
        return i // (2 * nz), lax.rem(i // 2, nz), lax.rem(i, 2)

    def stage_two(i):
        a, h = chunks[i]
        if full[a]:
            arrived(first[i])

            def add(k, carry):
                yy, zz, xx = split(k)
                whole[i][yy, zz, xx] = (
                    partial[a][c, yy, zz, xx, h].astype(f32) + gap[i][yy, zz, xx].astype(f32)
                ).astype(bf16)
                return carry

            lax.fori_loop(0, span, add, 0)
            block = whole[i].at[1 - y] if h == 0 else whole[i].at[:, :, 1 - x]
        else:
            block = partial[a].at[1 - y, :, :, h] if h == 0 else partial[a].at[:, :, 1 - x, h]
        return [remote(block, recv_two[i], two_s.at[i], two_r.at[i], along_y if h == 0 else along_x)]

    def stage_three(i):
        a, h = chunks[i]

        def add(k, carry):
            hi, lo = (k // 2, lax.rem(k, 2)) if h == 0 else (k // nz, lax.rem(k, nz))
            yy, zz, xx = (y, hi, lo) if h == 0 else (hi, lo, x)
            own = whole[i][yy, zz, xx] if full[a] else partial[a][yy, zz, xx, h]
            sum_two[i][hi, lo] = (own.astype(f32) + recv_two[i][hi, lo].astype(f32)).astype(bf16)
            return carry

        lax.fori_loop(0, 2 * nz, add, 0)
        block = sum_two[i].at[:, 1 - x] if h == 0 else sum_two[i].at[1 - y]
        return [remote(block, recv_three[i], three_s.at[i], three_r.at[i], along_x if h == 0 else along_y)]

    def stage_z(i):
        a, h = chunks[i]

        def add(k, carry):
            own = sum_two[i][k, x] if h == 0 else sum_two[i][y, k]
            sum_three[i][k] = (own.astype(f32) + recv_three[i][k].astype(f32)).astype(bf16)
            return carry

        lax.fori_loop(0, nz, add, 0)
        return [
            remote(
                sum_three[i].at[lax.rem(z + d, nz)], recv_z[i].at[d - 1], zs.at[i, d - 1], zr.at[i, d - 1], others[d - 1]
            )
            for d in range(1, nz)
        ]

    def finish(i):
        a, h = chunks[i]
        acc = sum_three[i][z].astype(f32)
        for d in range(1, nz):
            acc = acc + recv_z[i][d - 1].astype(f32)
        outs[a][h] = acc

    small_buf[0] = small[...]
    second, third, fourth = [None] * total, [None] * total, [None] * total
    arrived(dx_core)
    own_rows = pl.ds(pl.multiple_of(512 * c, 512), 512)
    for yy in range(2):
        at_in = pl.ds(512 + 256 * yy, 256)
        at_dx = pl.ds(pl.multiple_of(LEN + 512 * yy + 256 * c, 256), 256)
        dx_sum[pl.ds(256 * yy, 256), :] = (dx[at_dx, :].astype(f32) + dx_in[at_in, :].astype(f32)).astype(bf16)
    dx_swap = remote(
        dx_sum.at[pl.ds(pl.multiple_of(256 * (1 - y), 256), 256)], dx_y, os.at[15], orr.at[15], along_y
    )
    dx_swap.start()
    mine[pl.ds(0, 512), :] = (
        resid[pl.ds(0, 512), :] + (dx[own_rows, :].astype(f32) + dx_in[pl.ds(0, 512), :].astype(f32))
    ).astype(bf16)
    dx_swap.wait_recv()
    mine[pl.ds(512, 256), :] = (
        resid[pl.ds(512, 256), :]
        + (dx_sum[pl.ds(pl.multiple_of(256 * y, 256), 256), :].astype(f32) + dx_y[...].astype(f32))
    ).astype(bf16)
    in_first, in_second, in_third, in_kept = spread(mine, input_out, 6)
    start(in_kept + in_second)
    for step in range(total + 3):
        if step < total:
            second[step] = stage_two(step)
            start(second[step])
        if 0 <= step - 1 < total:
            arrived(second[step - 1])
            third[step - 1] = stage_three(step - 1)
            start(third[step - 1])
        if 0 <= step - 2 < total:
            arrived(third[step - 2])
            fourth[step - 2] = stage_z(step - 2)
            start(fourth[step - 2])
        if 0 <= step - 3 < total:
            arrived(fourth[step - 3])
            finish(step - 3)
        if step == 0:
            start(lay_first)
        if step == 4:
            start(in_first)
    small_out[...] = butterfly(small_buf, small_in, small_z, 0)
    acc = jnp.float32(0.0)
    for a in range(n):
        for h in range(2):
            acc = acc + jnp.sum(outs[a][h] * outs[a][h])
    norm_buf[0] = jnp.broadcast_to(acc, (8, 128))
    norm_out[...] = butterfly(norm_buf, norm_in, norm_z, 3)
    arrived(lay_first)
    start(lay_third)
    arrived(in_first)
    start(in_third)
    arrived(lay_second + lay_third + in_second + in_third)
    for i in range(total):
        sent(first[i] + second[i] + third[i] + fourth[i])
    sent(dx_core + [dx_swap] + lay_first + lay_second + lay_third + in_first + in_second + in_third)
    for copy in lay_kept + in_kept:
        copy.wait()


def tail(partial, full, small, dx, resid, layer, nz):
    n = len(full)
    tiles = [p.shape[-2:] for p in partial]
    gap, whole, two, three, last, sum_two = [], [], [], [], [], []
    for tile, f in zip(tiles, full):
        for h in range(2):
            shape = (2, nz, 2) + tile if f else (8, 128)
            gap.append(pltpu.VMEM(shape, bf16))
            whole.append(pltpu.VMEM(shape, bf16))
            shape = ((nz, 2) if h == 0 else (2, nz)) + tile
            two.append(pltpu.VMEM(shape, bf16))
            sum_two.append(pltpu.VMEM(shape, bf16))
            three.append(pltpu.VMEM((nz,) + tile, bf16))
            last.append(pltpu.VMEM((nz - 1,) + tile, bf16))
    rows = 3 * LEN
    return pl.pallas_call(
        functools.partial(tail_kernel, nz, full),
        out_shape=[jax.ShapeDtypeStruct((2,) + tile, f32) for tile in tiles]
        + [
            jax.ShapeDtypeStruct(small.shape, f32),
            jax.ShapeDtypeStruct((8, 128), f32),
            jax.ShapeDtypeStruct((rows, WIDTH), bf16),
            jax.ShapeDtypeStruct((rows, WIDTH), bf16),
        ],
        in_specs=[VM] * (n + 4),
        out_specs=[VM] * (n + 2) + [HBM] * 2,
        scratch_shapes=gap
        + whole
        + two
        + sum_two
        + three
        + three
        + last
        + [
            pltpu.VMEM((4,) + small.shape, f32),
            pltpu.VMEM((3,) + small.shape, f32),
            pltpu.VMEM((nz,) + small.shape, f32),
            pltpu.VMEM((4, 8, 128), f32),
            pltpu.VMEM((3, 8, 128), f32),
            pltpu.VMEM((nz, 8, 128), f32),
            pltpu.VMEM((LEN, WIDTH), bf16),
            pltpu.VMEM((512, WIDTH), bf16),
            pltpu.VMEM((256, WIDTH), bf16),
            pltpu.VMEM((WIDTH, WIDTH), bf16),
        ]
        + [DMA((2 * n,))] * 6
        + [DMA((2 * n, nz - 1))] * 2
        + [DMA((6,))] * 2
        + [DMA((2, nz - 1))] * 2
        + [DMA((16,))] * 2
        + [DMA((4,))],
        compiler_params=pltpu.CompilerParams(collective_id=4, has_side_effects=True, vmem_limit_bytes=VMEM_CAP),
        name="reduce_gradients",
    )(*partial, small, dx, resid, layer)


def adamw_update_step(weight, first, second, grad, clip_factor, rate):
    clipped = grad * clip_factor
    averaged = 0.9 * first + 0.1 * clipped
    squared = 0.98 * second + 0.02 * clipped * clipped
    step_size = averaged / (1.0 - 0.9**STEP) / (jnp.sqrt(squared / (1.0 - 0.98**STEP)) + adam_eps)
    return (weight - rate * (step_size + decay_rate * weight), averaged, squared)


def shards(
    activations,
    keep_flags,
    mask_counts,
    mask_positions,
    cotangents,
    projections,
    combiner,
    expander,
    reducer,
    offsets,
    shifts,
    vectors,
    momentum_projections,
    variance_projections,
    momentum_combiner,
    variance_combiner,
    momentum_expander,
    variance_expander,
    momentum_reducer,
    variance_reducer,
    momentum_offsets,
    variance_offsets,
    first_moment_shifts,
    second_moment_shifts,
    momentum_vectors,
    variance_vectors,
):
    n_dp = lax.axis_size("dp")
    nz = n_dp // 2
    mp = lax.axis_index("mp")
    y, c = mp // 2, lax.rem(mp, 2)
    seq_dev = keep_flags.shape[0]
    r = projections.shape[1]
    half = r // 2
    cols = projections.shape[2]
    own = [
        projections.transpose(1, 0, 2).astype(bf16).reshape(2, half, 3 * cols),
        combiner.T.astype(bf16).reshape(2, half, cols),
        expander.astype(bf16).reshape(2, half, WIDTH),
        reducer.T.astype(bf16).reshape(2, half, WIDTH),
    ]
    full = (False, True, True, True)
    pad = jnp.zeros((2, WIDTH - cols), f32)
    small = jnp.concatenate(
        [shifts[None], jnp.concatenate([offsets, pad], 1), jnp.zeros((5, WIDTH), f32)], 0
    )
    keep = jnp.broadcast_to(jnp.sum(keep_flags).astype(f32), (8, 128))
    g_qkv, g_out, g_one, g_two, g_small, g_keep = gather(own, full, small, keep, nz)
    kept_float = jnp.sum(g_keep[:, :, 0, 0])
    kept_total = kept_float.astype(jnp.int32)
    shares = keep_flags.astype(f32) * jnp.float32(seq_dev * n_dp) / kept_float
    w_pair = g_qkv.reshape(2, WIDTH, 3, cols)
    w_qkv = w_pair.transpose(1, 2, 0, 3).reshape(WIDTH, 6 * cols)
    w_out = g_out.reshape(2, 2, WIDTH, cols).transpose(0, 2, 1, 3).reshape(2, WIDTH, 2 * cols)
    w_one = g_one.reshape(4, WIDTH, WIDTH)
    w_two = g_two.reshape(4, WIDTH, WIDTH)
    mine = lax.dynamic_index_in_dim(g_small, c, 0, False)
    bias = jnp.concatenate(
        [mine[:, 1, :cols].reshape(1, 2 * cols), jnp.zeros((1, 2 * cols), f32), mine[:, 2, :cols].reshape(1, 2 * cols)],
        1,
    )
    shift_rows = g_small[:, :, 0].reshape(4, 1, WIDTH)
    qkv, att, lse = attend(activations, w_qkv, bias)
    att_rows = exchange(to_rows_kernel, att, (2, WIDTH, 384), 2, "to_rows")
    layer, resid, d_att, dw_out, dw_one, dw_two, dshift, dvec = middle(
        shares, mask_counts, att_rows, w_out, w_one, w_two, shift_rows, vectors, activations, mask_positions, cotangents
    )
    d_heads = exchange(to_heads_kernel, d_att, (1536, 384), 3, "to_heads")
    dw_qkv, dx, doff = back(activations, w_qkv, qkv, att, lse, d_heads)
    p_qkv = dw_qkv.reshape(WIDTH, 3, 2, cols).transpose(2, 0, 1, 3).reshape(2, nz, 2, 2, half, 3 * cols)
    p_out = dw_out.reshape(2, WIDTH, 2, cols).transpose(0, 2, 1, 3).reshape(2, 2, nz, 2, 2, half, cols)
    p_one = dw_one.reshape(2, 2, nz, 2, 2, half, WIDTH)
    p_two = dw_two.reshape(2, 2, nz, 2, 2, half, WIDTH)
    blank = jnp.zeros((2, 384), f32)
    off = doff[:2]
    off_rows = jnp.where(c == 0, jnp.concatenate([off, blank], 1), jnp.concatenate([blank, off], 1))
    sums = jnp.concatenate([dvec[:6], dshift[:, 0], off_rows, jnp.zeros((4, WIDTH), f32)], 0)
    t_two, t_one, t_out, t_qkv, sums, squares, layer_output, input_low = tail(
        [p_two, p_one, p_out, p_qkv], (True, True, True, False), sums, dx, resid, layer, nz
    )
    share_proj = t_qkv.reshape(r, 3, cols).transpose(1, 0, 2)
    share_comb = t_out.reshape(r, cols).T
    share_expd = t_one.reshape(r, WIDTH)
    share_redc = t_two.reshape(r, WIDTH).T
    sum_vectors = sums[:6]
    total_squares = squares[0, 0] + jnp.sum(sums * sums)
    gradient_norm = jnp.sqrt(total_squares)
    clip_factor = clip_limit / jnp.maximum(gradient_norm, clip_limit)
    spot = 2 * c + y
    shifts_total = lax.dynamic_index_in_dim(sums[6:10], spot, 0, False)
    sum_offsets = lax.dynamic_index_in_dim(sums[10:12].reshape(2, 4, cols), spot, 1, False)
    next_projections = adamw_update_step(
        projections, momentum_projections, variance_projections, share_proj, clip_factor, learn_rate
    )
    next_combiner = adamw_update_step(
        combiner, momentum_combiner, variance_combiner, share_comb, clip_factor, learn_rate
    )
    next_expander = adamw_update_step(
        expander, momentum_expander, variance_expander, share_expd, clip_factor, learn_rate
    )
    next_reducer = adamw_update_step(
        reducer, momentum_reducer, variance_reducer, share_redc, clip_factor, learn_rate
    )
    next_offsets = adamw_update_step(
        offsets, momentum_offsets, variance_offsets, sum_offsets, clip_factor, vector_rate
    )
    next_shifts = adamw_update_step(
        shifts, first_moment_shifts, second_moment_shifts, shifts_total, clip_factor, vector_rate
    )
    next_vectors = adamw_update_step(
        vectors, momentum_vectors, variance_vectors, sum_vectors, clip_factor, vector_rate
    )
    return (
        layer_output,
        input_low.astype(f32),
        kept_total,
        gradient_norm,
        *next_projections,
        *next_combiner,
        *next_expander,
        *next_reducer,
        *next_offsets,
        *next_shifts,
        *next_vectors,
        next_projections[0].astype(bf16),
        next_combiner[0].astype(bf16),
        next_expander[0].astype(bf16),
        next_reducer[0].astype(bf16),
    )


def solution(mesh):
    placed = (
        P("dp", None),
        P("dp"),
        P("dp"),
        P("dp", None),
        P("dp", None, None),
        P(None, "dp", "mp"),
        P("mp", "dp"),
        P("dp", "mp"),
        P("mp", "dp"),
        P(None, "mp"),
        P("mp"),
        P(),
        P(None, "dp", "mp"),
        P(None, "dp", "mp"),
        P("mp", "dp"),
        P("mp", "dp"),
        P("dp", "mp"),
        P("dp", "mp"),
        P("mp", "dp"),
        P("mp", "dp"),
        P(None, "mp"),
        P(None, "mp"),
        P("mp"),
        P("mp"),
        P(),
        P(),
    )
    return jax.shard_map(
        shards,
        mesh=mesh,
        in_specs=placed,
        out_specs=(
            P("dp", None),
            P("dp", None),
            P(),
            P(),
            P(None, "dp", "mp"),
            P(None, "dp", "mp"),
            P(None, "dp", "mp"),
            P("mp", "dp"),
            P("mp", "dp"),
            P("mp", "dp"),
            P("dp", "mp"),
            P("dp", "mp"),
            P("dp", "mp"),
            P("mp", "dp"),
            P("mp", "dp"),
            P("mp", "dp"),
            P(None, "mp"),
            P(None, "mp"),
            P(None, "mp"),
            P("mp"),
            P("mp"),
            P("mp"),
            P(),
            P(),
            P(),
            P(None, "dp", "mp"),
            P("mp", "dp"),
            P("dp", "mp"),
            P("mp", "dp"),
        ),
        check_vma=False,
    )
```

time: 951 us -> 499 us (0.52)
  Pallas kernels: 0 us -> 421 us
  waiting for transfers between devices: 298 us -> 0 us
  matrix products: 212 us -> 0 us
  blocking collectives: 161 us -> 0 us
  other arithmetic: 163 us -> 26.4 us
  local copies, waits for them, and re-layouts: 88 us -> 43.6 us
  between operations: 23.5 us -> 6.06 us
    pallas_call x0 -> x7, Pallas kernels: none -> 421 us  [the longest x1 175 us: tail(): pl.pallas_call(functools.partial(tail_kernel, nz, full), out_shape=[jax.S...]
    psum x4 -> x0, waiting for transfers between devices: 250 us -> none  [the longest x1 94.3 us: shards(): lax.psum(col_contract(inner_grad_low, wexp).astype(jnp.bfloat16), 'mp')]
    dot_general x25 -> x0, matrix products: 209 us -> none  [the longest x1 28.7 us: shards(): inner = jnp.dot(normed_low, wexp, preferred_element_type=f32) + shifts]
    psum x3 -> x0, blocking collectives: 88.5 us -> none  [the longest x1 39.5 us: shards(): total_squares = lax.psum(term, ('dp', 'mp'))]
    all_gather x2 -> x0, blocking collectives: 72 us -> none  [the longest x1 38.7 us: shards(): lax.all_gather(projections.astype(bf16), 'dp', axis=1, tiled=True)]
    reduce_sum x19 -> x3, other arithmetic: 75.9 us -> 4.21 us  [the longest x1 1.5 us: shards(): total_squares = squares[0, 0] + jnp.sum(sums * sums)]
    unnamed x12 -> x0, waiting for transfers between devices: 47.4 us -> none
    convert_element_type x7 -> x5, other arithmetic: 35.2 us -> 8.67 us  [the longest x1 4.48 us: shards(): input_low.astype(f32)]
  transfers between devices with their start and end apart: 10 -> 0, of which waited for: 4 -> 0; matrix products, arithmetic and copies ran while one was open for 25% -> 0% of each run, Pallas kernels for 0% -> 0%
where the time goes in v1:
time: 499 us; the launch traced here: 497 us
  Pallas kernels  421 us (84%)
  local copies, waits for them, and re-layouts  43.6 us (9%)
  other arithmetic  26.4 us (5%)
  between operations  6.06 us (1%)
    pallas_call x1, Pallas kernels, tail(): pl.pallas_call(functools.partial(tail_kernel, nz, full), out_shape=[jax.S...  175 us
    pallas_call x1, Pallas kernels, gather(): pl.pallas_call(functools.partial(gather_kernel, nz, full), out_shape=shap...  97.8 us
    pallas_call x1, Pallas kernels, middle(): pl.pallas_call(middle_kernel, out_shape=[jax.ShapeDtypeStruct(big, bf16),...  58 us
    pallas_call x1, Pallas kernels, back(): pl.pallas_call(back_kernel, out_shape=[jax.ShapeDtypeStruct((WIDTH, 1152)...  51.1 us
    pallas_call x1, Pallas kernels, attend(): pl.pallas_call(attend_kernel, out_shape=[jax.ShapeDtypeStruct((2 * LEN, 1...  31.1 us

profile of v1, /device:TPU:0, one launch (start us, length us, event | category | flops | bytes accessed | tf_op | source)
XLA Modules:
  0.0 497.4 jit_solution(16733728194711294851)
XLA Ops:
  0.7 1.3 reduce_sum.27
  2.9 0.7 broadcast_in_dim.17
  4.2 1.4 fusion.9.refs_4_
  5.5 0.9 convert_bitcast_fusion.1
  6.4 0.7 copy.86
  7.1 1.0 convert_bitcast_fusion
  8.3 0.8 reshape.125.refs_0_
  9.1 1.6 convert_element_type.50
  10.7 0.7 convert_element_type.51
  11.4 97.8 %gather_weights.1 = (bf16[2,4,2,2,48,576]{5,4,3,2,1,0:T(8,128)(2,1)}, bf16[2,2,4,2,2,48,192]{6,5,4,3,2,1,0:T(8,128)(2,1)}, bf16[2,2,4,2,2,48,768]{6,5,4,3,2,1,0:...) custom-call(bf16[2,48,576]{2,1,0:T(8,128)(2,1)} %reshape.125.refs_0_,, ...), custom_call_target="tpu_custom_call" | custom-call | tf_op jit(solution)/shard_map/gather_weights/pallas_call | solution.py:169
  109.2 1.4 slice_reduce_fusion
  111.2 1.2 multiply_divide_fusion.share_ref
  112.4 1.5 slice.33
  113.9 0.8 dynamic-slice_bitcast_fusion
  115.4 1.7 copy.89
  117.1 1.4 copy.90.wo_ref
  118.6 5.9 %reshape.129 = bf16[2,768,3,192]{3,2,1,0:T(4,128)(2,1)S(1)} reshape(bf16[2,4,2,2,48,576]{5,4,3,2,1,0:T(8,128)(2,1)} %get-tuple-element.58) | data formatting | bytes 3538944 | tf_op jit(solution)/shard_map/reshape | solution.py:1003
  124.5 3.3 copy.87
  127.8 3.8 copy.88.w_ref
  131.6 31.1 %attend.1 = (bf16[2048,1152]{1,0:T(8,128)(2,1)}, bf16[1536,384]{1,0:T(8,128)(2,1)}, f32[1536,128]{1,0:T(8,128)}) custom-call(bf16[3072,768]{1,0:T(8,128)(2,1)} %x_ref.5, bf16[768,1152]{1,0:T(8,128)(2,1)} %copy.88.w_ref, f32[1,1152]{1,0:T(1,128)} %fusion.11.b_ref), custom_call_target="tpu_custom_call" | custom-call | tf_op jit(solution)/shard_map/attend/pallas_call | solution.py:233
  162.7 4.5 to_rows.1.att_ref
  167.3 58.0 %middle.1 = (bf16[768,768]{1,0:T(8,128)(2,1)}, f32[768,768]{1,0:T(8,128)}, bf16[2,768,384]{2,1,0:T(8,128)(2,1)}, bf16[2,768,384]{2,1,0:T(8,128)(2,1)}, bf16[4,76...) custom-call(f32[3]{0:T(128)} %multiply_divide_fusion.share_ref, ...), custom_call_target="tpu_custom_call" | custom-call | tf_op jit(solution)/shard_map/middle/pallas_call | solution.py:508
  225.3 0.7 copy.115
  226.0 1.6 copy.91
  227.6 1.6 copy.92
  229.1 4.4 to_heads.1.dout_ref
  233.5 51.1 %attend_back.1 = (bf16[768,1152]{1,0:T(8,128)(2,1)}, bf16[2048,768]{1,0:T(8,128)(2,1)}, f32[8,384]{1,0:T(8,128)}) custom-call(bf16[3072,768]{1,0:T(8,128)(2,1)} %x_ref.5, bf16[768,1152]{1,0:T(8,128)(2,1)} %copy.88.w_ref, bf16[2048,1152]{1,0:T(8,128)(2,1)} %get-tuple-element.67.qkv_ref, bf16[1536,384]{1,0:T(8,128)(2,1)} %get-tuple-element.60.heads_ref.out_ref, ...), custom_call_target="tpu_custom_call" | custom-call | tf_op jit(solution)/shard_map/attend_back/pallas_call | solution.py:643
  284.6 3.9 copy.94
  288.5 0.7 slice.35
  289.2 0.7 maximum_maximum_fusion.refs_4_
  289.9 4.2 copy.95
  294.1 3.8 reshape.140.refs_3_
  297.9 174.6 %reduce_gradients.1 = (f32[2,48,768]{2,1,0:T(8,128)}, f32[2,48,768]{2,1,0:T(8,128)}, f32[2,48,192]{2,1,0:T(8,128)}, f32[2,48,576]{2,1,0:T(8,128)}, f32[16,768]{1...) custom-call(bf16[2,2,4,2,2,48,768]{6,5,4,3,2,1,0:T(8,128)(2,1)} %bitcast.86, ...), custom_call_target="tpu_custom_call" | custom-call | tf_op jit(solution)/shard_map/reduce_gradients/pallas_call | solution.py:902
  472.5 1.5 multiply_reduce_fusion
  474.1 1.2 slice.36
  476.6 0.7 slice.37
  478.1 0.8 slice.38
  478.9 0.6 multiply_subtract_fusion.5
  479.6 1.4 multiply_subtract_fusion.4
  481.0 0.9 broadcast_multiply_fusion.3
  482.0 1.0 broadcast_multiply_fusion.2
  482.9 1.1 broadcast_multiply_fusion
  484.3 0.8 fusion.21
  485.1 1.1 fusion.24
  486.2 1.1 fusion.15
  487.3 1.1 fusion.18
  488.4 4.5 convert_element_type.54
  492.9 2.2 copy.117
  (72 shorter events, 2.8 us)
Async XLA Ops:
  0.7 10.0 %copy-start.2 = (f32[768,96]{0,1:T(8,128)S(1)}, f32[768,96]{0,1:T(8,128)}, u32[]{:S(2)}) copy-start(f32[768,96]{0,1:T(8,128)} %param.34) | copy-start | bytes 884740
  0.7 110.5 %copy-start.23 = (s32[3]{0:T(128)S(1)}, s32[3]{0:T(128)}, u32[]{:S(2)}) copy-start(s32[3]{0:T(128)} %param.27) | copy-start | bytes 40
  284.6 4.6 copy-start.14
  297.8 179.6 %copy-start.18 = (f32[2,192]{1,0:T(2,128)S(1)}, f32[2,192]{1,0:T(2,128)}, u32[]{:S(2)}) copy-start(f32[2,192]{1,0:T(2,128)} %param.35) | copy-start | bytes 4612
  297.8 179.6 %copy-start.21 = (f32[2,192]{1,0:T(2,128)S(1)}, f32[2,192]{1,0:T(2,128)}, u32[]{:S(2)}) copy-start(f32[2,192]{1,0:T(2,128)} %param.46) | copy-start | bytes 4612
  297.8 179.6 %copy-start.22 = (f32[2,192]{1,0:T(2,128)S(1)}, f32[2,192]{1,0:T(2,128)}, u32[]{:S(2)}) copy-start(f32[2,192]{1,0:T(2,128)} %param.47) | copy-start | bytes 4612
  297.9 181.1 %copy-start.17 = (f32[768]{0:T(1024)S(1)}, f32[768]{0:T(1024)}, u32[]{:S(2)}) copy-start(f32[768]{0:T(1024)} %param.36) | copy-start | bytes 9220
  297.9 181.1 %copy-start.19 = (f32[768]{0:T(1024)S(1)}, f32[768]{0:T(1024)}, u32[]{:S(2)}) copy-start(f32[768]{0:T(1024)} %param.48) | copy-start | bytes 9220
  297.9 181.1 %copy-start.20 = (f32[768]{0:T(1024)S(1)}, f32[768]{0:T(1024)}, u32[]{:S(2)}) copy-start(f32[768]{0:T(1024)} %param.49) | copy-start | bytes 9220
  297.9 181.7 %copy-start.11 = (f32[6,768]{1,0:T(8,128)S(1)}, f32[6,768]{1,0:T(8,128)}, u32[]{:S(2)}) copy-start(f32[6,768]{1,0:T(8,128)} %vec_ref.1) | copy-start | bytes 55300
  297.9 181.7 %copy-start.15 = (f32[6,768]{1,0:T(8,128)S(1)}, f32[6,768]{1,0:T(8,128)}, u32[]{:S(2)}) copy-start(f32[6,768]{1,0:T(8,128)} %param.50) | copy-start | bytes 55300
  297.9 181.7 %copy-start.16 = (f32[6,768]{1,0:T(8,128)S(1)}, f32[6,768]{1,0:T(8,128)}, u32[]{:S(2)}) copy-start(f32[6,768]{1,0:T(8,128)} %param.51) | copy-start | bytes 55300
  472.5 11.8 %copy-start.4 = (f32[192,96]{1,0:T(8,128)S(1)}, f32[192,96]{1,0:T(8,128)}, u32[]{:S(2)}) copy-start(f32[192,96]{1,0:T(8,128)} %param.32) | copy-start | bytes 221188
  472.5 11.8 %copy-start.12 = (f32[192,96]{1,0:T(8,128)S(1)}, f32[192,96]{1,0:T(8,128)}, u32[]{:S(2)}) copy-start(f32[192,96]{1,0:T(8,128)} %param.40) | copy-start | bytes 221188
  472.5 11.8 %copy-start.13 = (f32[192,96]{1,0:T(8,128)S(1)}, f32[192,96]{1,0:T(8,128)}, u32[]{:S(2)}) copy-start(f32[192,96]{1,0:T(8,128)} %param.41) | copy-start | bytes 221188
  472.5 12.5 %copy-start.1 = (f32[3,96,192]{2,1,0:T(8,128)S(1)}, f32[3,96,192]{2,1,0:T(8,128)}, u32[]{:S(2)}) copy-start(f32[3,96,192]{2,1,0:T(8,128)} %param.31) | copy-start | bytes 663556
  472.5 12.5 %copy-start.5 = (f32[3,96,192]{2,1,0:T(8,128)S(1)}, f32[3,96,192]{2,1,0:T(8,128)}, u32[]{:S(2)}) copy-start(f32[3,96,192]{2,1,0:T(8,128)} %param.38) | copy-start | bytes 663556
  472.5 12.5 %copy-start.6 = (f32[3,96,192]{2,1,0:T(8,128)S(1)}, f32[3,96,192]{2,1,0:T(8,128)}, u32[]{:S(2)}) copy-start(f32[3,96,192]{2,1,0:T(8,128)} %param.39) | copy-start | bytes 663556
  484.0 2.2 copy-start.7
  484.0 2.2 copy-start.8
  485.0 2.3 copy-start.3
  485.0 2.3 copy-start.9
  485.0 2.3 copy-start.10
  485.1 3.4 copy-start
  487.3 5.6 %slice-start = ((s8[4718592]{0:T(1024)(128)(4,1)}), s8[4194304]{0:T(1024)(128)(4,1)S(1)}, s32[]{:S(2)}) async-start(s8[4718592]{0:T(1024)(128)(4,1)} %bitcast.79), calls=%async_computation | async-start | bytes 8388608
  488.4 4.5 slice-start.1

commit v2 on v1

--- a/solution.py
+++ b/solution.py
@@ -26,7 +26,7 @@
 VM = pl.BlockSpec(memory_space=pltpu.VMEM)
 SM = pl.BlockSpec(memory_space=pltpu.SMEM)
 DMA = pltpu.SemaphoreType.DMA
-VMEM_CAP = 60 * 1024 * 1024
+VMEM_CAP = 63 * 1024 * 1024
 
 
 def dot(left, right):
@@ -662,6 +662,1150 @@
         compiler_params=pltpu.CompilerParams(vmem_limit_bytes=VMEM_CAP),
         name="attend_back",
     )(activations, weights, qkv, out, lse, dout)
+
+
+def core_kernel(
+    share_ref,
+    count_ref,
+    att_ref,
+    go_ref,
+    g1_ref,
+    g2_ref,
+    shift_ref,
+    vec_ref,
+    x_ref,
+    pos_ref,
+    cot_ref,
+    layer_ref,
+    resid_ref,
+    datt_ref,
+    dwo_ref,
+    o1_ref,
+    o2_ref,
+    dshift_ref,
+    dvec_ref,
+    x_own,
+    cot_own,
+    unit1,
+    rstd1,
+    norm1,
+    low1,
+    low1_t,
+    hidden,
+    slope,
+    total,
+    d2,
+    d2_low,
+    d2_low_t,
+    inner_low,
+    wo_ref,
+    w1_ref,
+    w2_ref,
+    dw1_ref,
+    dw2_ref,
+    out_ref,
+    sem,
+    store,
+    give_s,
+    give_r,
+    local,
+):
+    z, x, y, c = place()
+    along_y, along_c = dev(z, x, 1 - y, c), dev(z, x, y, 1 - c)
+    copies = [
+        pltpu.make_async_copy(
+            x_ref.at[pl.ds(pl.multiple_of(y * LEN + 512 * c, 512), 512)], x_own.at[pl.ds(0, 512)], sem.at[0]
+        ),
+        pltpu.make_async_copy(
+            x_ref.at[pl.ds(pl.multiple_of(2 * LEN + 512 * y + 256 * c, 256), 256)],
+            x_own.at[pl.ds(512, 256)],
+            sem.at[1],
+        ),
+        pltpu.make_async_copy(cot_ref.at[y], cot_own.at[0], sem.at[2]),
+        pltpu.make_async_copy(cot_ref.at[2], cot_own.at[1], sem.at[3]),
+    ]
+    start(copies)
+    big = [
+        pltpu.make_async_copy(g1_ref, w1_ref, sem.at[4]),
+        pltpu.make_async_copy(g2_ref, w2_ref, sem.at[5]),
+    ]
+    start(big)
+    greet([along_y, along_c])
+
+    def own_set(k, yy):
+        if k == 1:
+            return pl.ds(pl.multiple_of(2 * LEN + 512 * yy + 256 * c, 256), 256), pl.ds(512, 256)
+        return pl.ds(pl.multiple_of(yy * LEN + 512 * c, 512), 512), pl.ds(0, 512)
+
+    def give(k, stage):
+        there, here = own_set(k, 1 - y if stage == 2 else y)
+        source = layer_ref.at[there] if stage == 2 else out_ref.at[here]
+        peer = along_y if stage == 0 else along_c
+        return remote(source, layer_ref.at[there], give_s.at[k, stage], give_r.at[k, stage], peer)
+
+    def keep(k):
+        there, here = own_set(k, y)
+        return pltpu.make_async_copy(out_ref.at[here], layer_ref.at[there], local.at[k])
+
+    for copy in copies:
+        copy.wait()
+    blocks = WIDTH // BLK
+    for p in range(2):
+        wo_ref[p, :, 0:128] = go_ref[p, 0, :, 0:128]
+        wo_ref[p, :, 128:256] = go_ref[p, 1, :, 0:128]
+        wo_ref[p, :, 256:384] = go_ref[p, 0, :, 128:256] + go_ref[p, 1, :, 128:256]
+
+    def vec(i):
+        return vec_ref[pl.ds(i, 1), :]
+
+    def at(b):
+        return pl.ds(pl.multiple_of(b * BLK, BLK), BLK)
+
+    def one(b, carry):
+        value = dot_t(att_ref[0, at(b), :], wo_ref[0]) + dot_t(att_ref[1, at(b), :], wo_ref[1])
+        first = x_own[at(b), :].astype(f32) + (value + vec(0))
+        unit, rstd = norm(first)
+        unit1[at(b), :] = unit
+        rstd1[at(b), :] = jnp.broadcast_to(rstd, (BLK, 128))
+        normed = unit * vec(2) + vec(3)
+        norm1[at(b), :] = normed
+        low = normed.astype(bf16)
+        low1[at(b), :] = low
+        low1_t[:, at(b)] = low.T
+        return carry
+
+    lax.fori_loop(0, blocks, one, 0)
+    for copy in big:
+        copy.wait()
+
+    def two(i, carry):
+        j, b = i // blocks, lax.rem(i, blocks)
+        inner = dot(low1[at(b), :], w1_ref[j]) + shift_ref[j]
+        cdf, bell = erf_parts(inner)
+        low = (inner * cdf).astype(bf16)
+        hidden[j, at(b), :] = low
+        slope[j, at(b), :] = cdf + inner * (bell * 0.3989422804014327)
+        part = dot_t(low, w2_ref[j])
+        total[at(b), :] = jnp.where(j == 0, part, total[at(b), :] + part)
+        return carry
+
+    lax.fori_loop(0, 4 * blocks, two, 0)
+    dvec_ref[...] = jnp.zeros_like(dvec_ref)
+
+    def three(b, carry):
+        second = norm1[at(b), :] + (total[at(b), :] + vec(1))
+        unit, rstd = norm(second)
+        final = unit * vec(4) + vec(5)
+        which = jnp.where(b == 2, 1, 0)
+        seq = jnp.where(b == 2, 2, y)
+        share = share_ref[seq]
+        inputs = x_own[at(b), :].astype(f32)
+        out_ref[at(b), :] = (inputs + share * (final - inputs)).astype(bf16)
+        base = jnp.where(b == 2, 512 * y + 256 * c, 512 * c + b * BLK)
+        slots = pos_ref.shape[1]
+        row = lax.broadcasted_iota(jnp.int32, (BLK, slots), 0) + base
+        slot = lax.broadcasted_iota(jnp.int32, (BLK, slots), 1)
+        hit = (pos_ref[pl.ds(seq, 1), :] == row) & (slot < count_ref[seq])
+        target = dot(jnp.where(hit, 1.0, 0.0).astype(bf16), cot_own[which])
+        up = share * target
+        resid_ref[at(b), :] = (1.0 - share) * target
+        grad = norm_back(up, unit, rstd, vec(4))
+        d2[at(b), :] = grad
+        low = grad.astype(bf16)
+        d2_low[at(b), :] = low
+        d2_low_t[:, at(b)] = low.T
+        dvec_ref[pl.ds(1, 1), :] += column(grad)
+        dvec_ref[pl.ds(4, 1), :] += column(up * unit)
+        dvec_ref[pl.ds(5, 1), :] += column(up)
+        return carry
+
+    lax.fori_loop(0, blocks, three, 0)
+    for k in range(2):
+        start([give(k, 0), give(k, 1), keep(k)])
+    dshift_ref[...] = jnp.zeros_like(dshift_ref)
+
+    def four(j, carry):
+        def rows(b, carry):
+            grad = dot(d2_low[at(b), :], w2_ref[j]) * slope[j, at(b), :]
+            low = grad.astype(bf16)
+            inner_low[at(b), :] = low
+            dshift_ref[j] += column(grad)
+            part = dot_t(low, w1_ref[j])
+            d2[at(b), :] += part
+            return carry
+
+        lax.fori_loop(0, blocks, rows, 0)
+
+        def grads(b, carry):
+            dw2_ref[j, at(b), :] = dot(d2_low_t[at(b), :], hidden[j]).astype(bf16)
+            dw1_ref[j, at(b), :] = dot(low1_t[at(b), :], inner_low[...]).astype(bf16)
+            return carry
+
+        lax.fori_loop(0, blocks, grads, 0)
+        pltpu.make_async_copy(dw2_ref.at[j], o2_ref.at[j], store.at[0, j]).start()
+        pltpu.make_async_copy(dw1_ref.at[j], o1_ref.at[j], store.at[1, j]).start()
+        return carry
+
+    lax.fori_loop(0, 4, four, 0)
+
+    def five(b, carry):
+        grad = d2[at(b), :]
+        unit = unit1[at(b), :]
+        first = norm_back(grad, unit, rstd1[at(b), :][:, :1], vec(2))
+        dvec_ref[pl.ds(0, 1), :] += column(first)
+        dvec_ref[pl.ds(2, 1), :] += column(grad * unit)
+        dvec_ref[pl.ds(3, 1), :] += column(grad)
+        resid_ref[at(b), :] += first
+        low = first.astype(bf16)
+        d2_low_t[:, at(b)] = low.T
+        for p in range(2):
+            datt_ref[p, at(b), :] = dot(low, wo_ref[p]).astype(bf16)
+        return carry
+
+    lax.fori_loop(0, blocks, five, 0)
+    for k in range(2):
+        give(k, 0).wait_recv()
+        give(k, 2).start()
+
+    def six(b, carry):
+        for p in range(2):
+            grad = dot(d2_low_t[at(b), :], att_ref[p]).astype(bf16)
+            for yy in range(2):
+                dwo_ref[p, yy, at(b), 0:128] = grad[:, 128 * yy : 128 * yy + 128]
+                dwo_ref[p, yy, at(b), 128:256] = grad[:, 256:384]
+        return carry
+
+    lax.fori_loop(0, blocks, six, 0)
+    for j in range(4):
+        pltpu.make_async_copy(dw2_ref.at[j], o2_ref.at[j], store.at[0, j]).wait()
+        pltpu.make_async_copy(dw1_ref.at[j], o1_ref.at[j], store.at[1, j]).wait()
+    for k in range(2):
+        keep(k).wait()
+        arrived([give(k, 1), give(k, 2)])
+        sent([give(k, 0), give(k, 1), give(k, 2)])
+
+
+def core(shares, counts, att, wo, w1, w2, shifts, vectors, activations, positions, cotangents):
+    slots = positions.shape[1]
+    big = (WIDTH, WIDTH)
+    return pl.pallas_call(
+        core_kernel,
+        out_shape=[
+            jax.ShapeDtypeStruct((3 * LEN, WIDTH), bf16),
+            jax.ShapeDtypeStruct(big, f32),
+            jax.ShapeDtypeStruct((2, WIDTH, 384), bf16),
+            jax.ShapeDtypeStruct((2, 2, WIDTH, 256), bf16),
+            jax.ShapeDtypeStruct((4,) + big, bf16),
+            jax.ShapeDtypeStruct((4,) + big, bf16),
+            jax.ShapeDtypeStruct((4, 1, WIDTH), f32),
+            jax.ShapeDtypeStruct((8, WIDTH), f32),
+        ],
+        in_specs=[SM, SM, VM, VM, HBM, HBM, VM, VM, HBM, VM, HBM],
+        out_specs=[HBM, VM, VM, VM, HBM, HBM, VM, VM],
+        scratch_shapes=[
+            pltpu.VMEM(big, bf16),
+            pltpu.VMEM((2, slots, WIDTH), bf16),
+            pltpu.VMEM(big, f32),
+            pltpu.VMEM((WIDTH, 128), f32),
+            pltpu.VMEM(big, f32),
+            pltpu.VMEM(big, bf16),
+            pltpu.VMEM(big, bf16),
+            pltpu.VMEM((4,) + big, bf16),
+            pltpu.VMEM((4,) + big, f32),
+            pltpu.VMEM(big, f32),
+            pltpu.VMEM(big, f32),
+            pltpu.VMEM(big, bf16),
+            pltpu.VMEM(big, bf16),
+            pltpu.VMEM(big, bf16),
+            pltpu.VMEM((2, WIDTH, 384), bf16),
+            pltpu.VMEM((4,) + big, bf16),
+            pltpu.VMEM((4,) + big, bf16),
+            pltpu.VMEM((4,) + big, bf16),
+            pltpu.VMEM((4,) + big, bf16),
+            pltpu.VMEM(big, bf16),
+            DMA((6,)),
+            DMA((2, 4)),
+            DMA((2, 3)),
+            DMA((2, 3)),
+            DMA((2,)),
+        ],
+        compiler_params=pltpu.CompilerParams(collective_id=7, has_side_effects=True, vmem_limit_bytes=VMEM_CAP),
+        name="core",
+    )(shares, counts, att, wo, w1, w2, shifts, vectors, activations, positions, cotangents)
+
+
+def front_kernel(
+    nz,
+    half,
+    cols,
+    x_ref,
+    proj_ref,
+    comb_ref,
+    exp_ref,
+    red_ref,
+    off_ref,
+    shift_ref,
+    keep_ref,
+    w_ref,
+    g_out,
+    g_one,
+    g_two,
+    small_ref,
+    kept_ref,
+    qkv_ref,
+    att_ref,
+    rows_ref,
+    lse_ref,
+    rows,
+    sh_qa,
+    sh_qb,
+    sh_out,
+    sh_one,
+    sh_two,
+    sh_small,
+    sh_keep,
+    qa,
+    qb,
+    small_in,
+    keep_in,
+    bias,
+    zs,
+    zr,
+    two_s,
+    two_r,
+    three_s,
+    three_r,
+    core_s,
+    core_r,
+    local,
+    small_s,
+    small_r,
+    keep_s,
+    keep_r,
+    row_s,
+    row_r,
+):
+    z, x, y, c = place()
+    others = [dev(lax.rem(z + d, nz), x, y, c) for d in range(1, nz)]
+    along_x, along_y, along_c = dev(z, 1 - x, y, c), dev(z, x, 1 - y, c), dev(z, x, y, 1 - c)
+    loads = [
+        pltpu.make_async_copy(x_ref.at[pl.ds(pl.multiple_of(y * LEN, LEN), LEN)], rows.at[pl.ds(0, LEN)], local.at[0]),
+        pltpu.make_async_copy(x_ref.at[pl.ds(2 * LEN, LEN)], rows.at[pl.ds(LEN, LEN)], local.at[1]),
+    ]
+    start(loads)
+    barrier = pltpu.get_barrier_semaphore()
+    peers = others + [along_x, along_y, along_c]
+    for peer in peers:
+        pl.semaphore_signal(barrier, inc=1, device_id=peer, device_id_type=MESH)
+    lane = lax.broadcasted_iota(jnp.int32, (half, 128), 1)
+    for h in range(2):
+        span = pl.ds(h * half, half)
+        for k in range(3):
+            sh_qa[h, :, 128 * k : 128 * k + 128] = proj_ref[k, span, 0:128].astype(bf16)
+        third = [proj_ref[k, span, 128:192] for k in range(3)]
+        sh_qb[h, :, 0:128] = jnp.concatenate([third[0], third[1]], 1).astype(bf16)
+        sh_qb[h, :, 128:256] = jnp.concatenate([third[2], third[2]], 1).astype(bf16)
+    turned = comb_ref[...].T
+    for h in range(2):
+        piece = turned[h * half : (h + 1) * half]
+        sh_out[h, :, 0:128] = piece[:, 0:128].astype(bf16)
+        last = jnp.concatenate([piece[:, 128:192], piece[:, 128:192]], 1)
+        sh_out[h, :, 128:256] = jnp.where(lane // 64 == y, last, 0.0).astype(bf16)
+        sh_one[h] = exp_ref[pl.ds(h * half, half), :].astype(bf16)
+    turned = red_ref[...].T
+    for h in range(2):
+        sh_two[h] = turned[h * half : (h + 1) * half].astype(bf16)
+    sh_small[...] = jnp.zeros_like(sh_small)
+    sh_small[0:1, :] = shift_ref[...]
+    pick = lax.broadcasted_iota(jnp.int32, (2, 128), 1)
+    off = off_ref[...]
+    sh_small[1:3, 0:128] = off[:, 0:128]
+    last = jnp.concatenate([off[:, 128:192], off[:, 128:192]], 1)
+    sh_small[1:3, 128:256] = jnp.where(pick // 64 == y, last, 0.0)
+    count = jnp.float32(0.0)
+    for s in range(keep_ref.shape[0]):
+        count = count + keep_ref[s].astype(f32)
+    sh_keep[...] = jnp.full((8, 128), count, f32)
+    pl.semaphore_wait(barrier, len(peers))
+
+    shards = [sh_qa, sh_qb, sh_out, sh_one, sh_two]
+    own = [qa, qb, g_out.at[c], g_one.at[c], g_two.at[c]]
+    chunks = [(a, h) for a in range(5) for h in range(2)]
+    total = len(chunks)
+
+    def stage_z(i):
+        a, h = chunks[i]
+        return [
+            remote(shards[a].at[h], own[a].at[y, z, x, h], zs.at[i, d - 1], zr.at[i, d - 1], others[d - 1])
+            for d in range(1, nz)
+        ]
+
+    def stage_two(i):
+        a, h = chunks[i]
+        block = own[a].at[y, :, x, h]
+        return [remote(block, block, two_s.at[i], two_r.at[i], along_x if h == 0 else along_y)]
+
+    def stage_three(i):
+        a, h = chunks[i]
+        block = own[a].at[y, :, :, h] if h == 0 else own[a].at[:, :, x, h]
+        return [remote(block, block, three_s.at[i], three_r.at[i], along_y if h == 0 else along_x)]
+
+    def stage_core(i):
+        a, h = chunks[i]
+        block = own[a].at[:, :, :, h]
+        return [remote(block, block, core_s.at[i], core_r.at[i], along_c)]
+
+    keep_first = [
+        remote(sh_keep, keep_in.at[z, x], keep_s.at[d - 1], keep_r.at[d - 1], others[d - 1]) for d in range(1, nz)
+    ]
+    small_first = [remote(sh_small, small_in.at[c, y], small_s.at[0], small_r.at[0], along_y)]
+    keep_second = [remote(keep_in.at[:, x], keep_in.at[:, x], keep_s.at[nz - 1], keep_r.at[nz - 1], along_x)]
+    small_second = [remote(small_in.at[c], small_in.at[c], small_s.at[1], small_r.at[1], along_c)]
+    kept = [pltpu.make_async_copy(shards[a], own[a].at[y, z, x], local.at[2 + a]) for a in range(5)]
+    kept += [
+        pltpu.make_async_copy(sh_small, small_in.at[c, y], local.at[7]),
+        pltpu.make_async_copy(sh_keep, keep_in.at[z, x], local.at[8]),
+    ]
+    start(kept)
+    start(stage_z(0) + stage_z(1) + small_first + keep_first)
+    for i in range(2, total):
+        start(stage_z(i))
+    for copy in kept + loads:
+        copy.wait()
+
+    def s1(i):
+        arrived(stage_z(i))
+        start(stage_two(i))
+
+    def s2(i):
+        arrived(stage_two(i))
+        start(stage_three(i))
+
+    def s3(i):
+        arrived(stage_three(i))
+        start(stage_core(i))
+
+    s1(0)
+    s1(1)
+    arrived(keep_first + small_first)
+    start(keep_second + small_second)
+    s2(0)
+    s1(2)
+    s2(1)
+    s1(3)
+    arrived(keep_second + small_second)
+    for yy in range(2):
+        bias[yy] = jnp.zeros((1, 384), f32)
+        bias[yy, :, 0:128] = small_in[c, yy, 1:2, 0:128]
+        bias[yy, :, 256:384] = small_in[c, yy, 2:3, 0:128]
+    bias[2] = jnp.zeros((1, 384), f32)
+    bias[2, :, 0:128] = small_in[c, 0, 1:2, 128:256] + small_in[c, 1, 1:2, 128:256]
+    bias[2, :, 256:384] = small_in[c, 0, 2:3, 128:256] + small_in[c, 1, 2:3, 128:256]
+    small_ref[...] = small_in[:, :, 0:1, :]
+    acc = jnp.zeros((8, 128), f32)
+    for zz in range(nz):
+        for xx in range(2):
+            acc = acc + keep_in[zz, xx]
+    kept_ref[...] = acc
+    arrived(stage_three(0) + stage_three(1))
+
+    def place_pair(i, carry):
+        yy, k = i // (4 * nz), lax.rem(i, 4 * nz)
+        zz, xx, h = k // 4, lax.rem(k // 2, 2), lax.rem(k, 2)
+        w_ref[yy, pl.ds(pl.multiple_of(k * half, half), half), :] = qa[yy, zz, xx, h]
+        return carry
+
+    lax.fori_loop(0, 8 * nz, place_pair, 0)
+
+    def row_copies(p):
+        col = pl.ds(pl.multiple_of(p * 128, 128), 128)
+        return [
+            remote(
+                att_ref.at[there, col], rows_ref.at[c, here, col], row_s.at[p, i], row_r.at[p, i], along_c
+            )
+            for i, (there, here) in enumerate(rows_of(1 - c))
+        ]
+
+    def row_kept(p):
+        col = pl.ds(pl.multiple_of(p * 128, 128), 128)
+        return [
+            pltpu.make_async_copy(att_ref.at[there, col], rows_ref.at[c, here, col], local.at[9 + i])
+            for i, (there, here) in enumerate(rows_of(c))
+        ]
+
+    hooks = {
+        0: [lambda: s2(2), lambda: s2(3)],
+        1: [lambda: s1(4), lambda: s1(5)],
+        3: [lambda: s2(4), lambda: s2(5)],
+        4: [lambda: s1(6), lambda: s1(7)],
+        9: [lambda: s3(4), lambda: s3(5)],
+        10: [lambda: s2(6), lambda: s2(7)],
+        11: [lambda: s1(8), lambda: s1(9)],
+    }
+    lanes = lax.broadcasted_iota(jnp.int32, (BLK, 128), 1)
+    ones = jnp.ones((LEN, 128), bf16)
+
+    def pair(p, carry):
+        @pl.when(p == 2)
+        def _():
+            arrived(stage_three(2) + stage_three(3))
+
+            def place_last(k, carry):
+                zz, xx, h = k // 4, lax.rem(k // 2, 2), lax.rem(k, 2)
+                at = pl.ds(pl.multiple_of(k * half, half), half)
+                near, far = qb[0, zz, xx, h], qb[1, zz, xx, h]
+                w_ref[2, at, 0:128] = jnp.concatenate([near[:, 0:64], far[:, 0:64]], 1)
+                w_ref[2, at, 128:256] = jnp.concatenate([near[:, 64:128], far[:, 64:128]], 1)
+                w_ref[2, at, 256:384] = jnp.concatenate([near[:, 128:192], far[:, 128:192]], 1)
+                return carry
+
+            lax.fori_loop(0, 4 * nz, place_last, 0)
+
+        def project(i, carry):
+            at = pl.ds(pl.multiple_of(i * BLK, BLK), BLK)
+            qkv_ref[p, at, :] = (dot(rows[at, :], w_ref[p]) + bias[p]).astype(bf16)
+            return carry
+
+        lax.fori_loop(0, 2 * LEN // BLK, project, 0)
+
+        def unit(u, carry):
+            for when, todo in hooks.items():
+
+                @pl.when(p * 6 + u == when)
+                def _(todo=todo):
+                    for step in todo:
+                        step()
+
+            shared = u >= LEN // BLK
+            at = pl.ds(pl.multiple_of(u * BLK, BLK), BLK)
+            q_row = pl.ds(pl.multiple_of(jnp.where(shared, 512 * y, 0) + u * BLK, BLK), BLK)
+            kv_row = pl.ds(pl.multiple_of(jnp.where(shared, LEN, 0), LEN), LEN)
+            query = qkv_ref[p, q_row, 0:128] * bf16(0.125)
+            key = qkv_ref[p, kv_row, 128:256]
+            wide = jnp.concatenate([qkv_ref[p, kv_row, 256:384], ones], axis=1)
+            parts = []
+            lse = jnp.where(p == 0, 0.0, lse_ref[at, :])
+            for h in range(2):
+                mine = (lanes < 64) if h == 0 else (lanes >= 64)
+                scores = dot_t(jnp.where(mine, query, bf16(0.0)), key)
+                top = jnp.max(scores, -1, keepdims=True)
+                weight = jnp.exp(scores - top)
+                both = dot(weight.astype(bf16), wide)
+                total_weight = both[:, 128:]
+                parts.append(both[:, :128] / total_weight)
+                lse = jnp.where(lanes == 2 * p + h, top + jnp.log(total_weight), lse)
+            att_ref[at, pl.ds(pl.multiple_of(p * 128, 128), 128)] = jnp.where(
+                lanes < 64, parts[0], parts[1]
+            ).astype(bf16)
+            lse_ref[at, :] = lse
+            return carry
+
+        lax.fori_loop(0, 6, unit, 0)
+        start(row_copies(p) + row_kept(p))
+        for copy in row_kept(p):
+            copy.wait()
+        return carry
+
+    lax.fori_loop(0, 3, pair, 0)
+    s3(6)
+    s3(7)
+    s2(8)
+    s2(9)
+    s3(8)
+    s3(9)
+    for p in range(3):
+        arrived(row_copies(p))
+    for i in range(4, total):
+        arrived(stage_core(i))
+    for p in range(3):
+        sent(row_copies(p))
+    for i in range(total):
+        sent(stage_z(i) + stage_two(i) + stage_three(i))
+    for i in range(4, total):
+        sent(stage_core(i))
+    sent(keep_first + small_first + keep_second + small_second)
+
+
+def front(activations, projections, combiner, expander, reducer, offsets, shifts, keep_flags, nz):
+    r, cols = projections.shape[1:]
+    half = r // 2
+    wide = (2, 2, nz, 2, 2, half)
+    return pl.pallas_call(
+        functools.partial(front_kernel, nz, half, cols),
+        out_shape=[
+            jax.ShapeDtypeStruct((3, WIDTH, 384), bf16),
+            jax.ShapeDtypeStruct(wide + (256,), bf16),
+            jax.ShapeDtypeStruct(wide + (WIDTH,), bf16),
+            jax.ShapeDtypeStruct(wide + (WIDTH,), bf16),
+            jax.ShapeDtypeStruct((2, 2, 1, WIDTH), f32),
+            jax.ShapeDtypeStruct((8, 128), f32),
+            jax.ShapeDtypeStruct((3, 2 * LEN, 384), bf16),
+            jax.ShapeDtypeStruct((1536, 384), bf16),
+            jax.ShapeDtypeStruct((2, WIDTH, 384), bf16),
+            jax.ShapeDtypeStruct((1536, 128), f32),
+        ],
+        in_specs=[HBM] + [VM] * 6 + [SM],
+        out_specs=[VM, HBM, HBM, HBM, VM, VM, VM, VM, VM, VM],
+        scratch_shapes=[
+            pltpu.VMEM((2 * LEN, WIDTH), bf16),
+            pltpu.VMEM((2, half, 384), bf16),
+            pltpu.VMEM((2, half, 256), bf16),
+            pltpu.VMEM((2, half, 256), bf16),
+            pltpu.VMEM((2, half, WIDTH), bf16),
+            pltpu.VMEM((2, half, WIDTH), bf16),
+            pltpu.VMEM((8, WIDTH), f32),
+            pltpu.VMEM((8, 128), f32),
+            pltpu.VMEM((2, nz, 2, 2, half, 384), bf16),
+            pltpu.VMEM((2, nz, 2, 2, half, 256), bf16),
+            pltpu.VMEM((2, 2, 8, WIDTH), f32),
+            pltpu.VMEM((nz, 2, 8, 128), f32),
+            pltpu.VMEM((3, 1, 384), f32),
+            DMA((10, nz - 1)),
+            DMA((10, nz - 1)),
+        ]
+        + [DMA((10,))] * 6
+        + [DMA((11,)), DMA((2,)), DMA((2,)), DMA((nz,)), DMA((nz,)), DMA((3, 2)), DMA((3, 2))],
+        compiler_params=pltpu.CompilerParams(collective_id=5, has_side_effects=True, vmem_limit_bytes=VMEM_CAP),
+        name="front",
+    )(activations, projections, combiner, expander, reducer, offsets, shifts.reshape(1, WIDTH), keep_flags)
+
+
+def rear_kernel(
+    nz,
+    half,
+    x_ref,
+    w_ref,
+    qkv_ref,
+    out_ref,
+    lse_ref,
+    datt_ref,
+    p_two,
+    p_one,
+    p_out,
+    resid_ref,
+    dvec_ref,
+    dshift_ref,
+    t_two,
+    t_one,
+    t_out,
+    t_a,
+    t_b,
+    sums_ref,
+    norm_ref,
+    input_ref,
+    dout,
+    rows,
+    rows_t,
+    grads,
+    key_t,
+    stats,
+    dk,
+    dv,
+    dx,
+    dqa,
+    dqb,
+    doff,
+    *refs,
+):
+    refs = list(refs)
+
+    def take(count):
+        head = refs[:count]
+        del refs[:count]
+        return head
+
+    n = 5
+    own, gap = take(6), take(6)
+    recv_two, recv_three, recv_z = take(10), take(10), take(10)
+    small_buf, small_in, small_z, norm_buf, norm_in, norm_z, dx_in, dx_sum, dx_y, mine = take(10)
+    (core_s, core_r, two_s, two_r, three_s, three_r, zs, zr, bs, br, bzs, bzr, os, orr, load, local, head_s, head_r) = take(18)
+    z, x, y, c = place()
+    others = [dev(lax.rem(z + d, nz), x, y, c) for d in range(1, nz)]
+    along_x, along_y, along_c = dev(z, 1 - x, y, c), dev(z, x, 1 - y, c), dev(z, x, y, 1 - c)
+    partial = [p_two, p_one, p_out, dqa, dqb]
+    outs = [t_two, t_one, t_out, t_a, t_b]
+    chunks = [(a, h) for a in range(n) for h in range(2)]
+    y_first = [a == 1 and h == 0 or a >= 2 and h == 0 for a, h in chunks]
+
+    def at(b):
+        return pl.ds(pl.multiple_of(b * BLK, BLK), BLK)
+
+    def load_own(i):
+        a, h = chunks[i]
+        return pltpu.make_async_copy(partial[a].at[c, :, :, :, h], own[i], load.at[i])
+
+    def load_rows(i):
+        base = jnp.where(i < 4, y * LEN, 2 * LEN - LEN) + i * BLK
+        return pltpu.make_async_copy(
+            x_ref.at[pl.ds(pl.multiple_of(base, BLK), BLK)], rows.at[lax.rem(i, 2)], local.at[lax.rem(i, 2)]
+        )
+
+    load_rows(0).start()
+    load_rows(1).start()
+    for i in range(6):
+        load_own(i).start()
+    greet(others + [along_x, along_y, along_c])
+    heads = [
+        remote(datt_ref.at[1 - c, here], dout.at[there], head_s.at[i], head_r.at[i], along_c)
+        for i, (there, here) in enumerate(rows_of(c))
+    ]
+    heads_kept = [
+        pltpu.make_async_copy(datt_ref.at[c, here], dout.at[there], local.at[2 + i])
+        for i, (there, here) in enumerate(rows_of(c))
+    ]
+    start(heads + heads_kept)
+
+    def core_stage(i):
+        a, h = chunks[i]
+        return [remote(partial[a].at[1 - c, :, :, :, h], gap[i], core_s.at[i], core_r.at[i], along_c)]
+
+    for i in range(6):
+        start(core_stage(i))
+
+    def cell(i, yy, zz, xx):
+        a, h = chunks[i]
+        return own[i][yy, zz, xx] if i < 6 else partial[a][yy, zz, xx, h]
+
+    def add(left, right):
+        return (left.astype(f32) + right.astype(f32)).astype(bf16)
+
+    def copy_two(i):
+        a, h = chunks[i]
+        ref = own[i] if i < 6 else partial[a].at[:, :, :, h]
+        block = ref.at[1 - y] if y_first[i] else ref.at[:, :, 1 - x]
+        return [remote(block, recv_two[i], two_s.at[i], two_r.at[i], along_y if y_first[i] else along_x)]
+
+    def copy_three(i):
+        block = recv_two[i].at[:, 1 - x] if y_first[i] else recv_two[i].at[1 - y]
+        return [remote(block, recv_three[i], three_s.at[i], three_r.at[i], along_x if y_first[i] else along_y)]
+
+    def copy_z(i):
+        return [
+            remote(
+                recv_three[i].at[lax.rem(z + d, nz)],
+                recv_z[i].at[d - 1],
+                zs.at[i, d - 1],
+                zr.at[i, d - 1],
+                others[d - 1],
+            )
+            for d in range(1, nz)
+        ]
+
+    def r1(i):
+        if i < 6:
+            load_own(i).wait()
+            arrived(core_stage(i))
+
+            def body(k, carry):
+                yy, zz, xx = k // (2 * nz), lax.rem(k // 2, nz), lax.rem(k, 2)
+                own[i][yy, zz, xx] = add(own[i][yy, zz, xx], gap[i][yy, zz, xx])
+                return carry
+
+            lax.fori_loop(0, 4 * nz, body, 0)
+        start(copy_two(i))
+
+    def r2(i):
+        arrived(copy_two(i))
+
+        def body(k, carry):
+            if y_first[i]:
+                hi, lo = k // 2, lax.rem(k, 2)
+                mine_too = cell(i, y, hi, lo)
+            else:
+                hi, lo = k // nz, lax.rem(k, nz)
+                mine_too = cell(i, hi, lo, x)
+            recv_two[i][hi, lo] = add(mine_too, recv_two[i][hi, lo])
+            return carry
+
+        lax.fori_loop(0, 2 * nz, body, 0)
+        start(copy_three(i))
+
+    def r3(i):
+        arrived(copy_three(i))
+
+        def body(k, carry):
+            mine_too = recv_two[i][k, x] if y_first[i] else recv_two[i][y, k]
+            recv_three[i][k] = add(mine_too, recv_three[i][k])
+            return carry
+
+        lax.fori_loop(0, nz, body, 0)
+        start(copy_z(i))
+
+    lane_256 = lax.broadcasted_iota(jnp.int32, (half, 256), 1)
+
+    def r4(i):
+        a, h = chunks[i]
+        arrived(copy_z(i))
+        acc = recv_three[i][z].astype(f32)
+        for d in range(1, nz):
+            acc = acc + recv_z[i][d - 1].astype(f32)
+        if a == 2:
+            acc = jnp.where((lane_256 < 128) | ((lane_256 - 128) // 64 == y), acc, 0.0)
+        outs[a][h] = acc
+
+    spot = lax.broadcasted_iota(jnp.int32, (8, 384), 0)
+    head = (lax.broadcasted_iota(jnp.int32, (8, 384), 1)) // HD
+    pick = jnp.where(spot == head, 1.0, 0.0).astype(bf16)
+
+    def turn(i, carry):
+        load_rows(i).wait()
+        rows_t[:, at(i)] = rows[lax.rem(i, 2)].T
+
+        @pl.when(i < 6)
+        def _():
+            load_rows(i + 2).start()
+
+        for p in range(3):
+            grads[p, at(i), 0:128] = jnp.zeros((BLK, 128), bf16)
+        return carry
+
+    lax.fori_loop(0, 2 * LEN // BLK, turn, 0)
+    doff[...] = jnp.zeros_like(doff)
+    arrived(heads)
+    for copy in heads_kept:
+        copy.wait()
+
+    def prepare(u, carry):
+        both = out_ref[at(u), :].astype(f32) * dout[at(u), :].astype(f32)
+        high = both.astype(bf16)
+        low = (both - high.astype(f32)).astype(bf16)
+        stats[0, u] = lse_ref[at(u), :].T[:8, :]
+        stats[1, u] = dot_t(pick, high) + dot_t(pick, low)
+        return carry
+
+    lax.fori_loop(0, 6, prepare, 0)
+    lane = lax.broadcasted_iota(jnp.int32, (BLK, 128), 1)
+    sub = lax.broadcasted_iota(jnp.int32, (128, BLK), 0)
+
+    def attention(s, hooks, before):
+        n_units = 4 if s == 0 else 2
+        kv = pl.ds(s * LEN, LEN)
+
+        def pair(p, carry):
+            for when, todo in before.items():
+
+                @pl.when(p == when)
+                def _(todo=todo):
+                    todo()
+
+            col = pl.multiple_of(p * 128, 128)
+            key_t[...] = qkv_ref[p, kv, 128:256].T
+            dk[...] = jnp.zeros_like(dk)
+            dv[...] = jnp.zeros_like(dv)
+
+            def unit(i, carry):
+                for when, todo in hooks.items():
+
+                    @pl.when(p * n_units + i == when)
+                    def _(todo=todo):
+                        for step in todo:
+                            step()
+
+                u = i + 4 * s
+                q_row = pl.ds(pl.multiple_of((512 * y if s else 0) + u * BLK, BLK), BLK)
+                query = qkv_ref[p, q_row, 0:128] * bf16(0.125)
+                grad = dout[at(u), pl.ds(col, 128)]
+                key = qkv_ref[p, kv, 128:256]
+                value = qkv_ref[p, kv, 256:384]
+                parts = []
+                for h in range(2):
+                    mine_too = (lane < 64) if h == 0 else (lane >= 64)
+                    q_head = jnp.where(mine_too, query, bf16(0.0))
+                    g_head = jnp.where(mine_too, grad, bf16(0.0))
+                    lse = stats[0, u, pl.ds(2 * p + h, 1), :]
+                    delta = stats[1, u, pl.ds(2 * p + h, 1), :]
+                    probs = jnp.exp(dot_t(key, q_head) - lse)
+                    slopes = dot_t(value, g_head)
+                    dv[...] += dot(probs.astype(bf16), g_head)
+                    low = (probs * (slopes - delta)).astype(bf16)
+                    dk[...] += dot(low, q_head)
+                    parts.append(dot(key_t[...], low))
+                dq = (jnp.where(sub < 64, parts[0], parts[1]) * 0.125).T
+                doff[pl.ds(0, 1), pl.ds(col, 128)] += column(dq)
+                grads[p, q_row, 0:128] = dq.astype(bf16)
+                return carry
+
+            lax.fori_loop(0, n_units, unit, 0)
+            grads[p, kv, 128:256] = dk[...].astype(bf16)
+            grads[p, kv, 256:384] = dv[...].astype(bf16)
+            doff[pl.ds(1, 1), pl.ds(col, 128)] += column(dv[...])
+            return carry
+
+        lax.fori_loop(0, 3, pair, 0)
+
+    def inputs(i, carry):
+        acc = dot_t(grads[0, at(i), :], w_ref[0]) + dot_t(grads[1, at(i), :], w_ref[1])
+        dx[at(i), :] = (acc + dot_t(grads[2, at(i), :], w_ref[2])).astype(bf16)
+        return carry
+
+    def swap_core(yy):
+        return remote(
+            dx.at[pl.ds(pl.multiple_of(LEN + 512 * yy + 256 * (1 - c), 256), 256)],
+            dx_in.at[pl.ds(512 + 256 * yy, 256)],
+            os.at[yy],
+            orr.at[yy],
+            along_c,
+        )
+
+    def swap_y():
+        return remote(
+            dx_sum.at[pl.ds(pl.multiple_of(256 * (1 - y), 256), 256)], dx_y, os.at[2], orr.at[2], along_y
+        )
+
+    def swap_own():
+        return remote(
+            dx.at[pl.ds(pl.multiple_of(512 * (1 - c), 512), 512)], dx_in.at[pl.ds(0, 512)], os.at[3], orr.at[3], along_c
+        )
+
+    def own_set(k, yy):
+        if k == 2:
+            return pl.ds(pl.multiple_of(2 * LEN + 512 * yy + 256 * c, 256), 256), pl.ds(512, 256)
+        return pl.ds(pl.multiple_of(yy * LEN + 512 * c + 256 * k, 256), 256), pl.ds(256 * k, 256)
+
+    def give_y(k):
+        there, here = own_set(k, y)
+        return remote(mine.at[here], input_ref.at[there], os.at[4 + k], orr.at[4 + k], along_y)
+
+    def give_c(k):
+        there, here = own_set(k, y)
+        return remote(mine.at[here], input_ref.at[there], os.at[7 + k], orr.at[7 + k], along_c)
+
+    def pass_on(k):
+        there, here = own_set(k, 1 - y)
+        return remote(input_ref.at[there], input_ref.at[there], os.at[10 + k], orr.at[10 + k], along_c)
+
+    def keep(k):
+        there, here = own_set(k, y)
+        return pltpu.make_async_copy(mine.at[here], input_ref.at[there], local.at[4 + k])
+
+    def shared_sum():
+        for yy in range(2):
+            swap_core(yy).wait_recv()
+            at_dx = pl.ds(pl.multiple_of(LEN + 512 * yy + 256 * c, 256), 256)
+            dx_sum[pl.ds(256 * yy, 256), :] = add(dx[at_dx, :], dx_in[pl.ds(512 + 256 * yy, 256), :])
+        swap_y().start()
+
+    def shared_done():
+        swap_y().wait_recv()
+        mine[pl.ds(512, 256), :] = (
+            resid_ref[pl.ds(512, 256), :]
+            + (dx_sum[pl.ds(pl.multiple_of(256 * y, 256), 256), :].astype(f32) + dx_y[...].astype(f32))
+        ).astype(bf16)
+        give_y(2).start()
+        give_c(2).start()
+        keep(2).start()
+
+    def shared_pass():
+        give_y(2).wait_recv()
+        pass_on(2).start()
+
+    attention(1, shared_hooks(r1, r2, r3, r4), {})
+    lax.fori_loop(4, 8, inputs, 0)
+    for yy in range(2):
+        swap_core(yy).start()
+
+    def weights(p, split):
+        def body(zz, carry):
+            at_zz = pl.ds(pl.multiple_of(zz * 4 * half, 4 * half), 4 * half)
+            value = dot(rows_t[at_zz, :], grads[p]).astype(bf16)
+            for k in range(4):
+                xx, h = k // 2, k % 2
+                part = value[k * half : (k + 1) * half]
+                if not split:
+                    dqa[p, zz, xx, h] = part
+                    continue
+                for yy in range(2):
+                    lo, hi = 64 * yy, 64 * yy + 64
+                    dqb[yy, zz, xx, h, :, 0:128] = jnp.concatenate([part[:, lo:hi], part[:, 128 + lo : 128 + hi]], 1)
+                    dqb[yy, zz, xx, h, :, 128:256] = jnp.concatenate(
+                        [part[:, 256 + lo : 256 + hi], jnp.zeros((half, 64), bf16)], 1
+                    )
+            return carry
+
+        lax.fori_loop(0, nz, body, 0)
+
+    def send_a():
+        weights(0, False)
+        weights(1, False)
+        r1(6)
+        r1(7)
+
+    attention(0, whole_hooks(r1, r2, r3, r4, shared_sum, shared_done, shared_pass), {2: send_a})
+    lax.fori_loop(0, 2, lambda i, carry: inputs(2 * (1 - c) + i, carry), 0)
+    swap_own().start()
+    weights(2, True)
+    r1(8)
+    r1(9)
+    lax.fori_loop(0, 2, lambda i, carry: inputs(2 * c + i, carry), 0)
+    swap_own().wait_recv()
+    own_rows = pl.ds(pl.multiple_of(512 * c, 512), 512)
+    mine[pl.ds(0, 512), :] = (
+        resid_ref[pl.ds(0, 512), :] + (dx[own_rows, :].astype(f32) + dx_in[pl.ds(0, 512), :].astype(f32))
+    ).astype(bf16)
+    give_y(0).start()
+    for k in range(2):
+        give_c(k).start()
+        keep(k).start()
+    small_buf[0] = jnp.zeros_like(sums_ref)
+    small_buf[0, 0:6, :] = dvec_ref[0:6, :]
+    for j in range(4):
+        small_buf[0, 6 + j : 7 + j, :] = dshift_ref[j]
+    small_buf[0, 10:12, pl.ds(pl.multiple_of(384 * c, 128), 384)] = doff[0:2, :]
+
+    def swap(buf, inn, k, stage):
+        peer = (along_c, along_y, along_x)[stage]
+        return remote(buf.at[stage], inn.at[stage], bs.at[k + stage], br.at[k + stage], peer)
+
+    def swap_z(buf, slots, k):
+        return [
+            remote(buf.at[3], slots.at[z], bzs.at[k // 3, d - 1], bzr.at[k // 3, d - 1], others[d - 1])
+            for d in range(1, nz)
+        ]
+
+    def merge(buf, inn, slots, k, stage):
+        copy = swap(buf, inn, k, stage)
+        copy.wait()
+        buf[stage + 1] = buf[stage] + inn[stage]
+        if stage < 2:
+            swap(buf, inn, k, stage + 1).start()
+        else:
+            slots[z] = buf[3]
+            start(swap_z(buf, slots, k))
+
+    def total(buf, slots, k):
+        for copy in swap_z(buf, slots, k):
+            copy.wait()
+        acc = slots[0]
+        for d in range(1, nz):
+            acc = acc + slots[d]
+        return acc
+
+    swap(small_buf, small_in, 0, 0).start()
+    r3(6)
+    r3(7)
+    merge(small_buf, small_in, small_z, 0, 0)
+    r2(8)
+    r2(9)
+    give_y(1).start()
+    merge(small_buf, small_in, small_z, 0, 1)
+    r4(6)
+    r4(7)
+    merge(small_buf, small_in, small_z, 0, 2)
+    r3(8)
+    r3(9)
+    sums_ref[...] = total(small_buf, small_z, 0)
+    r4(8)
+    r4(9)
+    acc = jnp.float32(0.0)
+    for a in range(n):
+        for h in range(2):
+            acc = acc + jnp.sum(outs[a][h] * outs[a][h])
+    norm_buf[0] = jnp.broadcast_to(acc, (8, 128))
+    swap(norm_buf, norm_in, 3, 0).start()
+    for stage in range(3):
+        merge(norm_buf, norm_in, norm_z, 3, stage)
+    norm_ref[...] = total(norm_buf, norm_z, 3)
+    for k in range(2):
+        give_y(k).wait_recv()
+        pass_on(k).start()
+    for k in range(3):
+        keep(k).wait()
+        give_c(k).wait_recv()
+        pass_on(k).wait_recv()
+    for k in range(3):
+        sent([give_y(k), give_c(k), pass_on(k)])
+    sent([swap_core(0), swap_core(1), swap_y(), swap_own()] + heads)
+    for i in range(2 * n):
+        sent((core_stage(i) if i < 6 else []) + copy_two(i) + copy_three(i) + copy_z(i))
+
+
+def shared_hooks(r1, r2, r3, r4):
+    return {
+        0: [lambda: r1(0), lambda: r1(1)],
+        1: [lambda: r1(2), lambda: r1(3)],
+        2: [lambda: r1(4), lambda: r1(5)],
+        5: [lambda: r2(0), lambda: r2(1)],
+    }
+
+
+def whole_hooks(r1, r2, r3, r4, shared_sum, shared_done, shared_pass):
+    return {
+        0: [shared_sum, lambda: r2(2), lambda: r2(3)],
+        2: [lambda: r3(0), lambda: r3(1)],
+        4: [shared_done, lambda: r2(4), lambda: r2(5)],
+        5: [lambda: r3(2), lambda: r3(3)],
+        6: [lambda: r4(0), lambda: r4(1)],
+        7: [lambda: r3(4), lambda: r3(5)],
+        8: [shared_pass],
+        9: [lambda: r4(2), lambda: r4(3)],
+        10: [lambda: r4(4), lambda: r4(5)],
+        11: [lambda: r2(6), lambda: r2(7)],
+    }
+
+
+def rear(activations, weights, qkv, out, lse, datt, p_two, p_one, p_out, resid, dvec, dshift, nz):
+    half = p_two.shape[-2]
+    widths = [WIDTH, WIDTH, 256, 384, 256]
+    chunks = [(a, h) for a in range(5) for h in range(2)]
+    y_first = [a == 1 and h == 0 or a >= 2 and h == 0 for a, h in chunks]
+    own = [pltpu.VMEM((2, nz, 2, half, widths[a]), bf16) for a, h in chunks[:6]]
+    two = [
+        pltpu.VMEM(((nz, 2) if first else (2, nz)) + (half, widths[a]), bf16) for (a, h), first in zip(chunks, y_first)
+    ]
+    three = [pltpu.VMEM((nz, half, widths[a]), bf16) for a, h in chunks]
+    last = [pltpu.VMEM((nz - 1, half, widths[a]), bf16) for a, h in chunks]
+    small = (16, WIDTH)
+    return pl.pallas_call(
+        functools.partial(rear_kernel, nz, half),
+        out_shape=[jax.ShapeDtypeStruct((2, half, w), f32) for w in widths]
+        + [
+            jax.ShapeDtypeStruct(small, f32),
+            jax.ShapeDtypeStruct((8, 128), f32),
+            jax.ShapeDtypeStruct((3 * LEN, WIDTH), bf16),
+        ],
+        in_specs=[HBM] + [VM] * 5 + [HBM] * 3 + [VM] * 3,
+        out_specs=[VM] * 7 + [HBM],
+        scratch_shapes=[
+            pltpu.VMEM((1536, 384), bf16),
+            pltpu.VMEM((2, BLK, WIDTH), bf16),
+            pltpu.VMEM((WIDTH, 2 * LEN), bf16),
+            pltpu.VMEM((3, 2 * LEN, 384), bf16),
+            pltpu.VMEM((128, LEN), bf16),
+            pltpu.VMEM((2, 6, 8, BLK), f32),
+            pltpu.VMEM((LEN, 128), f32),
+            pltpu.VMEM((LEN, 128), f32),
+            pltpu.VMEM((2 * LEN, WIDTH), bf16),
+            pltpu.VMEM((2, nz, 2, 2, half, 384), bf16),
+            pltpu.VMEM((2, nz, 2, 2, half, 256), bf16),
+            pltpu.VMEM((8, 384), f32),
+        ]
+        + own
+        + own
+        + two
+        + three
+        + last
+        + [
+            pltpu.VMEM((4,) + small, f32),
+            pltpu.VMEM((3,) + small, f32),
+            pltpu.VMEM((nz,) + small, f32),
+            pltpu.VMEM((4, 8, 128), f32),
+            pltpu.VMEM((3, 8, 128), f32),
+            pltpu.VMEM((nz, 8, 128), f32),
+            pltpu.VMEM((LEN, WIDTH), bf16),
+            pltpu.VMEM((512, WIDTH), bf16),
+            pltpu.VMEM((256, WIDTH), bf16),
+            pltpu.VMEM((WIDTH, WIDTH), bf16),
+        ]
+        + [DMA((6,))] * 2
+        + [DMA((10,))] * 4
+        + [DMA((10, nz - 1))] * 2
+        + [DMA((6,))] * 2
+        + [DMA((2, nz - 1))] * 2
+        + [DMA((13,))] * 2
+        + [DMA((6,)), DMA((7,)), DMA((2,)), DMA((2,))],
+        compiler_params=pltpu.CompilerParams(collective_id=6, has_side_effects=True, vmem_limit_bytes=VMEM_CAP),
+        name="rear",
+    )(activations, weights, qkv, out, lse, datt, p_two, p_one, p_out, resid, dvec, dshift)
 
 
 def tail_kernel(nz, full, *refs):
@@ -948,7 +2092,8 @@
     return (weight - rate * (step_size + decay_rate * weight), averaged, squared)
 
 
-def shards(
+def general_step(
+    slices,
     activations,
     keep_flags,
     mask_counts,
@@ -961,29 +2106,9 @@
     offsets,
     shifts,
     vectors,
-    momentum_projections,
-    variance_projections,
-    momentum_combiner,
-    variance_combiner,
-    momentum_expander,
-    variance_expander,
-    momentum_reducer,
-    variance_reducer,
-    momentum_offsets,
-    variance_offsets,
-    first_moment_shifts,
-    second_moment_shifts,
-    momentum_vectors,
-    variance_vectors,
 ):
-    n_dp = lax.axis_size("dp")
-    nz = n_dp // 2
-    mp = lax.axis_index("mp")
-    y, c = mp // 2, lax.rem(mp, 2)
+    n_dp, nz, c, r, half, cols = slices
     seq_dev = keep_flags.shape[0]
-    r = projections.shape[1]
-    half = r // 2
-    cols = projections.shape[2]
     own = [
         projections.transpose(1, 0, 2).astype(bf16).reshape(2, half, 3 * cols),
         combiner.T.astype(bf16).reshape(2, half, cols),
@@ -1033,6 +2158,133 @@
     share_comb = t_out.reshape(r, cols).T
     share_expd = t_one.reshape(r, WIDTH)
     share_redc = t_two.reshape(r, WIDTH).T
+    return share_proj, share_comb, share_expd, share_redc, sums, squares, layer_output, input_low, kept_total
+
+
+def fused_step(
+    slices,
+    activations,
+    keep_flags,
+    mask_counts,
+    mask_positions,
+    cotangents,
+    projections,
+    combiner,
+    expander,
+    reducer,
+    offsets,
+    shifts,
+    vectors,
+):
+    n_dp, nz, c, r, half, cols = slices
+    seq_dev = keep_flags.shape[0]
+    w_qkv, g_out, g_one, g_two, shift_rows, kept, qkv, att, att_rows, lse = front(
+        activations, projections, combiner, expander, reducer, offsets, shifts, keep_flags, nz
+    )
+    kept_float = kept[0, 0]
+    kept_total = kept_float.astype(jnp.int32)
+    shares = keep_flags.astype(f32) * jnp.float32(seq_dev * n_dp) / kept_float
+    layer_output, resid, d_att, dw_out, dw_one, dw_two, dshift, dvec = core(
+        shares,
+        mask_counts,
+        att_rows,
+        g_out.reshape(2, 2, WIDTH, 256),
+        g_one.reshape(4, WIDTH, WIDTH),
+        g_two.reshape(4, WIDTH, WIDTH),
+        shift_rows.reshape(4, 1, WIDTH),
+        vectors,
+        activations,
+        mask_positions,
+        cotangents,
+    )
+    block = (2, 2, nz, 2, 2, half)
+    t_two, t_one, t_out, t_a, t_b, sums, squares, input_low = rear(
+        activations,
+        w_qkv,
+        qkv,
+        att,
+        lse,
+        d_att,
+        dw_two.reshape(block + (WIDTH,)),
+        dw_one.reshape(block + (WIDTH,)),
+        dw_out.reshape(block + (256,)),
+        resid,
+        dvec,
+        dshift,
+        nz,
+    )
+    off = sums[10:12].reshape(4, 384)
+    off = jnp.concatenate([off[:, 0:128], off[:, 256:320], off[:, 128:256], off[:, 320:384]], 1)
+    sums = jnp.concatenate([sums[:10], off.reshape(2, WIDTH), sums[12:]], 0)
+    y = lax.axis_index("mp") // 2
+    t_a = t_a.reshape(r, 3, 128).transpose(1, 0, 2)
+    t_b = t_b.reshape(r, 256)[:, :192].reshape(r, 3, 64).transpose(1, 0, 2)
+    share_proj = jnp.concatenate([t_a, t_b], 2)
+    t_out = t_out.reshape(r, 256)
+    third = lax.dynamic_slice_in_dim(t_out, 128 + 64 * y, 64, 1)
+    share_comb = jnp.concatenate([t_out[:, :128], third], 1).T
+    share_expd = t_one.reshape(r, WIDTH)
+    share_redc = t_two.reshape(r, WIDTH).T
+    return share_proj, share_comb, share_expd, share_redc, sums, squares, layer_output, input_low, kept_total
+
+
+def shards(
+    activations,
+    keep_flags,
+    mask_counts,
+    mask_positions,
+    cotangents,
+    projections,
+    combiner,
+    expander,
+    reducer,
+    offsets,
+    shifts,
+    vectors,
+    momentum_projections,
+    variance_projections,
+    momentum_combiner,
+    variance_combiner,
+    momentum_expander,
+    variance_expander,
+    momentum_reducer,
+    variance_reducer,
+    momentum_offsets,
+    variance_offsets,
+    first_moment_shifts,
+    second_moment_shifts,
+    momentum_vectors,
+    variance_vectors,
+):
+    n_dp = lax.axis_size("dp")
+    nz = n_dp // 2
+    mp = lax.axis_index("mp")
+    y, c = mp // 2, lax.rem(mp, 2)
+    seq_dev = keep_flags.shape[0]
+    r = projections.shape[1]
+    half = r // 2
+    cols = projections.shape[2]
+    slices = (n_dp, nz, c, r, half, cols)
+    if half % 16 == 0 and cols == 192:
+        step = fused_step
+    else:
+        step = general_step
+    outs = step(
+        slices,
+        activations,
+        keep_flags,
+        mask_counts,
+        mask_positions,
+        cotangents,
+        projections,
+        combiner,
+        expander,
+        reducer,
+        offsets,
+        shifts,
+        vectors,
+    )
+    share_proj, share_comb, share_expd, share_redc, sums, squares, layer_output, input_low, kept_total = outs
     sum_vectors = sums[:6]
     total_squares = squares[0, 0] + jnp.sum(sums * sums)
     gradient_norm = jnp.sqrt(total_squares)

time: 499 us -> 331 us (0.66)
  Pallas kernels: 421 us -> 293 us
  local copies, waits for them, and re-layouts: 43.6 us -> 12.9 us
  other arithmetic: 26.4 us -> 19.3 us
    pallas_call x7 -> x3, Pallas kernels: 421 us -> 293 us  [the longest x1 141 us: rear(): pl.pallas_call(functools.partial(rear_kernel, nz, half), out_shape=[jax.S...]
    reshape x7 -> x6, local copies, waits for them, and re-layouts: 17.6 us -> 1.49 us  [the longest x1 1.27 us: front(): shifts.reshape(1, WIDTH)]
    transpose x3 -> x0, local copies, waits for them, and re-layouts: 9.06 us -> none  [the longest x1 4.19 us: shards(): dw_qkv.reshape(WIDTH, 3, 2, cols).transpose(2, 0, 1, 3)]
    pallas_call x2 -> x0, local copies, waits for them, and re-layouts: 5.42 us -> none  [the longest x1 3.86 us: back(): pl.pallas_call(back_kernel, out_shape=[jax.ShapeDtypeStruct((WIDTH, 1152)...]
where the time goes in v2:
time: 331 us
  Pallas kernels  293 us (89%)
  other arithmetic  19.3 us (6%)
  local copies, waits for them, and re-layouts  12.9 us (4%)
  between operations  5.36 us (2%)
    pallas_call x1, Pallas kernels, rear(): pl.pallas_call(functools.partial(rear_kernel, nz, half), out_shape=[jax.S...  141 us
    pallas_call x1, Pallas kernels, front(): pl.pallas_call(functools.partial(front_kernel, nz, half, cols), out_shape...  94.9 us
    pallas_call x1, Pallas kernels, core(): pl.pallas_call(core_kernel, out_shape=[jax.ShapeDtypeStruct((3 * LEN, WID...  56.8 us
    unnamed x49, local copies, waits for them, and re-layouts  7.09 us
    convert_element_type x1, other arithmetic, shards(): input_low.astype(f32)  6.82 us

profile of v2, /device:TPU:0, one launch (start us, length us, event | category | flops | bytes accessed | tf_op | source)
XLA Modules:
  0.0 330.6 jit_solution(5498275463468070815)
XLA Ops:
  0.7 0.0 copy-start.21
  0.7 1.9 copy.72.red_ref
  2.6 1.3 reshape.110.shift_ref
  3.8 94.9 %front.1 = (bf16[3,768,384]{2,1,0:T(8,128)(2,1)}, bf16[2,2,4,2,2,48,256]{6,5,4,3,2,1,0:T(8,128)(2,1)}, bf16[2,2,4,2,2,48,768]{6,5,4,3,2,1,0:T(8,128)(2,1)}, bf16...) custom-call(bf16[3072,768]{1,0:T(8,128)(2,1)} %x_ref.5, ...), custom_call_target="tpu_custom_call" | custom-call | tf_op jit(solution)/shard_map/front/pallas_call | solution.py:1233
  98.8 1.2 slice.41
  100.0 1.2 multiply_divide_fusion.share_ref
  101.1 56.8 %core.1 = (bf16[3072,768]{1,0:T(8,128)(2,1)}, f32[768,768]{1,0:T(8,128)}, bf16[2,768,384]{2,1,0:T(8,128)(2,1)}, bf16[2,2,768,256]{3,2,1,0:T(8,128)(2,1)}, bf16[4...) custom-call(f32[3]{0:T(128)} %multiply_divide_fusion.share_ref, ...), custom_call_target="tpu_custom_call" | custom-call | tf_op jit(solution)/shard_map/core/pallas_call | solution.py:891
  157.9 0.0 copy-start.8
  157.9 0.0 copy-start.13
  158.0 0.0 copy-start.14
  158.0 0.0 copy-start.15
  158.0 0.0 copy-start.17
  158.0 0.0 copy-start.18
  158.0 0.0 copy-start.16
  158.0 0.0 copy-start.19
  158.0 0.0 copy-start.20
  158.0 0.0 copy-start
  158.1 0.0 copy-start.4
  158.1 0.0 copy-start.2
  158.1 141.2 %rear.1 = (f32[2,48,768]{2,1,0:T(8,128)}, f32[2,48,768]{2,1,0:T(8,128)}, f32[2,48,256]{2,1,0:T(8,128)}, f32[2,48,384]{2,1,0:T(8,128)}, f32[2,48,256]{2,1,0:T(8,1...) custom-call(bf16[3072,768]{1,0:T(8,128)(2,1)} %x_ref.5, ...), custom_call_target="tpu_custom_call" | custom-call | tf_op jit(solution)/shard_map/rear/pallas_call | solution.py:1758
  299.4 0.0 copy-start.3
  299.4 0.0 copy-start.9
  299.4 0.0 copy-start.10
  299.4 0.0 copy-start.1
  299.4 0.0 copy-start.5
  299.4 0.9 slice.44
  300.4 0.1 fusion.28
  300.4 0.1 pad_maximum_fusion
  300.5 0.8 fusion.26
  301.3 1.4 fusion.7
  302.8 1.2 slice.42
  305.4 1.4 multiply_subtract_fusion.4
  306.8 0.6 multiply_subtract_fusion.5
  307.4 0.1 reshape_reshape.3
  307.5 0.6 multiply_subtract_fusion.6
  308.1 1.1 broadcast_multiply_fusion
  309.3 2.1 fusion.15
  311.3 2.2 fusion.12
  313.5 0.1 constant_dynamic-slice_fusion
  313.6 0.1 copy.81
  313.7 0.1 copy.80
  313.8 0.8 fusion.18
  314.6 0.1 reshape.120
  314.7 0.1 copy.79
  314.8 0.1 copy.75
  314.9 1.1 fusion.20
  316.0 6.8 %convert_element_type.22 = f32[3072,768]{1,0:T(8,128)} convert(bf16[3072,768]{1,0:T(8,128)(2,1)} %get-tuple-element.73) | non-fusion elementwise | flops 2359296 | bytes 14155776 | tf_op jit(solution)/shard_map/convert_element_type | solution.py:2318
  323.5 4.8 %copy.89 = bf16[3072,768]{1,0:T(8,128)(2,1)} copy(bf16[3072,768]{1,0:T(8,128)(2,1)} %get-tuple-element.172) | data formatting | bytes 9437184
  (33 shorter events, 0.2 us)
Async XLA Ops:
  0.7 99.3 %copy-start.21 = (s32[3]{0:T(128)S(1)}, s32[3]{0:T(128)}, u32[]{:S(2)}) copy-start(s32[3]{0:T(128)} %keep_ref.1) | copy-start | bytes 40
  157.9 147.4 %copy-start.8 = (f32[6,768]{1,0:T(8,128)S(1)}, f32[6,768]{1,0:T(8,128)}, u32[]{:S(2)}) copy-start(f32[6,768]{1,0:T(8,128)} %vec_ref.1) | copy-start | bytes 55300
  157.9 147.4 %copy-start.13 = (f32[6,768]{1,0:T(8,128)S(1)}, f32[6,768]{1,0:T(8,128)}, u32[]{:S(2)}) copy-start(f32[6,768]{1,0:T(8,128)} %param.50) | copy-start | bytes 55300
  158.0 147.4 %copy-start.14 = (f32[6,768]{1,0:T(8,128)S(1)}, f32[6,768]{1,0:T(8,128)}, u32[]{:S(2)}) copy-start(f32[6,768]{1,0:T(8,128)} %param.51) | copy-start | bytes 55300
  158.0 148.8 %copy-start.15 = (f32[768]{0:T(1024)S(1)}, f32[768]{0:T(1024)}, u32[]{:S(2)}) copy-start(f32[768]{0:T(1024)} %param.36) | copy-start | bytes 9220
  158.0 148.8 %copy-start.17 = (f32[768]{0:T(1024)S(1)}, f32[768]{0:T(1024)}, u32[]{:S(2)}) copy-start(f32[768]{0:T(1024)} %param.48) | copy-start | bytes 9220
  158.0 148.8 %copy-start.18 = (f32[768]{0:T(1024)S(1)}, f32[768]{0:T(1024)}, u32[]{:S(2)}) copy-start(f32[768]{0:T(1024)} %param.49) | copy-start | bytes 9220
  158.0 149.5 %copy-start.16 = (f32[2,192]{1,0:T(2,128)S(1)}, f32[2,192]{1,0:T(2,128)}, u32[]{:S(2)}) copy-start(f32[2,192]{1,0:T(2,128)} %off_ref.1) | copy-start | bytes 4612
  158.0 149.5 %copy-start.19 = (f32[2,192]{1,0:T(2,128)S(1)}, f32[2,192]{1,0:T(2,128)}, u32[]{:S(2)}) copy-start(f32[2,192]{1,0:T(2,128)} %param.46) | copy-start | bytes 4612
  158.0 149.5 %copy-start.20 = (f32[2,192]{1,0:T(2,128)S(1)}, f32[2,192]{1,0:T(2,128)}, u32[]{:S(2)}) copy-start(f32[2,192]{1,0:T(2,128)} %param.47) | copy-start | bytes 4612
  158.0 151.2 %copy-start = (f32[96,768]{1,0:T(8,128)S(1)}, f32[96,768]{1,0:T(8,128)}, u32[]{:S(2)}) copy-start(f32[96,768]{1,0:T(8,128)} %exp_ref.1) | copy-start | bytes 884740
  158.1 151.2 %copy-start.4 = (f32[96,768]{1,0:T(8,128)S(1)}, f32[96,768]{1,0:T(8,128)}, u32[]{:S(2)}) copy-start(f32[96,768]{1,0:T(8,128)} %param.42) | copy-start | bytes 884740
  158.1 153.3 %copy-start.2 = (f32[768,96]{0,1:T(8,128)S(1)}, f32[768,96]{0,1:T(8,128)}, u32[]{:S(2)}) copy-start(f32[768,96]{0,1:T(8,128)} %param.34) | copy-start | bytes 884740
  299.3 14.2 %copy-start.12 = (f32[2,48,256]{2,1,0:T(8,128)S(1)}, f32[2,48,256]{2,1,0:T(8,128)}, u32[]{:S(2)}) copy-start(f32[2,48,256]{2,1,0:T(8,128)} %get-tuple-element.78) | copy-start | bytes 294916
  299.4 14.4 %copy-start.3 = (f32[192,96]{1,0:T(8,128)S(1)}, f32[192,96]{1,0:T(8,128)}, u32[]{:S(2)}) copy-start(f32[192,96]{1,0:T(8,128)} %comb_ref.1) | copy-start | bytes 221188
  299.4 14.4 %copy-start.9 = (f32[192,96]{1,0:T(8,128)S(1)}, f32[192,96]{1,0:T(8,128)}, u32[]{:S(2)}) copy-start(f32[192,96]{1,0:T(8,128)} %param.40) | copy-start | bytes 221188
  299.4 14.4 %copy-start.10 = (f32[192,96]{1,0:T(8,128)S(1)}, f32[192,96]{1,0:T(8,128)}, u32[]{:S(2)}) copy-start(f32[192,96]{1,0:T(8,128)} %param.41) | copy-start | bytes 221188
  299.4 15.2 %copy-start.7 = (f32[2,48,384]{2,1,0:T(8,128)S(1)}, f32[2,48,384]{2,1,0:T(8,128)}, u32[]{:S(2)}) copy-start(f32[2,48,384]{2,1,0:T(8,128)} %get-tuple-element.76) | copy-start | bytes 442372
  299.4 15.3 %copy-start.11 = (f32[2,48,256]{2,1,0:T(8,128)S(1)}, f32[2,48,256]{2,1,0:T(8,128)}, u32[]{:S(2)}) copy-start(f32[2,48,256]{2,1,0:T(8,128)} %get-tuple-element.77) | copy-start | bytes 294916
  299.4 15.5 %copy-start.1 = (f32[3,96,192]{2,1,0:T(8,128)S(1)}, f32[3,96,192]{2,1,0:T(8,128)}, u32[]{:S(2)}) copy-start(f32[3,96,192]{2,1,0:T(8,128)} %proj_ref.1) | copy-start | bytes 663556
  299.4 15.5 %copy-start.5 = (f32[3,96,192]{2,1,0:T(8,128)S(1)}, f32[3,96,192]{2,1,0:T(8,128)}, u32[]{:S(2)}) copy-start(f32[3,96,192]{2,1,0:T(8,128)} %param.38) | copy-start | bytes 663556
  299.4 15.5 %copy-start.6 = (f32[3,96,192]{2,1,0:T(8,128)S(1)}, f32[3,96,192]{2,1,0:T(8,128)}, u32[]{:S(2)}) copy-start(f32[3,96,192]{2,1,0:T(8,128)} %param.39) | copy-start | bytes 663556

commit v3 on v2

--- a/solution.py
+++ b/solution.py
@@ -665,7 +665,9 @@
 
 
 def core_kernel(
-    share_ref,
+    seqs,
+    keep_ref,
+    kept_ref,
     count_ref,
     att_ref,
     go_ref,
@@ -798,7 +800,7 @@
         final = unit * vec(4) + vec(5)
         which = jnp.where(b == 2, 1, 0)
         seq = jnp.where(b == 2, 2, y)
-        share = share_ref[seq]
+        share = keep_ref[seq].astype(f32) * jnp.float32(seqs) / kept_ref[0:1, 0:1]
         inputs = x_own[at(b), :].astype(f32)
         out_ref[at(b), :] = (inputs + share * (final - inputs)).astype(bf16)
         base = jnp.where(b == 2, 512 * y + 256 * c, 512 * c + b * BLK)
@@ -885,11 +887,11 @@
         sent([give(k, 0), give(k, 1), give(k, 2)])
 
 
-def core(shares, counts, att, wo, w1, w2, shifts, vectors, activations, positions, cotangents):
+def core(seqs, keep_flags, kept, counts, att, wo, w1, w2, shifts, vectors, activations, positions, cotangents):
     slots = positions.shape[1]
     big = (WIDTH, WIDTH)
     return pl.pallas_call(
-        core_kernel,
+        functools.partial(core_kernel, seqs),
         out_shape=[
             jax.ShapeDtypeStruct((3 * LEN, WIDTH), bf16),
             jax.ShapeDtypeStruct(big, f32),
@@ -900,7 +902,7 @@
             jax.ShapeDtypeStruct((4, 1, WIDTH), f32),
             jax.ShapeDtypeStruct((8, WIDTH), f32),
         ],
-        in_specs=[SM, SM, VM, VM, HBM, HBM, VM, VM, HBM, VM, HBM],
+        in_specs=[SM, VM, SM, VM, VM, HBM, HBM, VM, VM, HBM, VM, HBM],
         out_specs=[HBM, VM, VM, VM, HBM, HBM, VM, VM],
         scratch_shapes=[
             pltpu.VMEM(big, bf16),
@@ -931,7 +933,7 @@
         ],
         compiler_params=pltpu.CompilerParams(collective_id=7, has_side_effects=True, vmem_limit_bytes=VMEM_CAP),
         name="core",
-    )(shares, counts, att, wo, w1, w2, shifts, vectors, activations, positions, cotangents)
+    )(keep_flags, kept, counts, att, wo, w1, w2, shifts, vectors, activations, positions, cotangents)
 
 
 def front_kernel(
@@ -1012,11 +1014,9 @@
         last = jnp.concatenate([piece[:, 128:192], piece[:, 128:192]], 1)
         sh_out[h, :, 128:256] = jnp.where(lane // 64 == y, last, 0.0).astype(bf16)
         sh_one[h] = exp_ref[pl.ds(h * half, half), :].astype(bf16)
-    turned = red_ref[...].T
-    for h in range(2):
-        sh_two[h] = turned[h * half : (h + 1) * half].astype(bf16)
+        sh_two[h] = red_ref[pl.ds(h * half, half), :].astype(bf16)
     sh_small[...] = jnp.zeros_like(sh_small)
-    sh_small[0:1, :] = shift_ref[...]
+    sh_small[0, :] = shift_ref[...]
     pick = lax.broadcasted_iota(jnp.int32, (2, 128), 1)
     off = off_ref[...]
     sh_small[1:3, 0:128] = off[:, 0:128]
@@ -1267,7 +1267,7 @@
         + [DMA((11,)), DMA((2,)), DMA((2,)), DMA((nz,)), DMA((nz,)), DMA((3, 2)), DMA((3, 2))],
         compiler_params=pltpu.CompilerParams(collective_id=5, has_side_effects=True, vmem_limit_bytes=VMEM_CAP),
         name="front",
-    )(activations, projections, combiner, expander, reducer, offsets, shifts.reshape(1, WIDTH), keep_flags)
+    )(activations, projections, combiner, expander, reducer.T, offsets, shifts, keep_flags)
 
 
 def rear_kernel(
@@ -2090,6 +2090,147 @@
     squared = 0.98 * second + 0.02 * clipped * clipped
     step_size = averaged / (1.0 - 0.9**STEP) / (jnp.sqrt(squared / (1.0 - 0.98**STEP)) + adam_eps)
     return (weight - rate * (step_size + decay_rate * weight), averaged, squared)
+
+
+def finish_kernel(half, *refs):
+    refs = list(refs)
+
+    def take(count):
+        head = refs[:count]
+        del refs[:count]
+        return head
+
+    low, layer = take(2)
+    t_two, t_one, t_out, t_a, t_b, sums, squares, kept = take(8)
+    mats = [take(3) for _ in range(4)]
+    smalls = [take(3) for _ in range(3)]
+    grad_out, layer_out, norm_out, kept_out = take(4)
+    mats_out = [take(4) for _ in range(4)]
+    smalls_out = [take(3) for _ in range(3)]
+    low_buf, wide_buf, layer_buf = take(3)
+    held = [take(3) for _ in range(4)]
+    made = [take(4) for _ in range(4)]
+    low_sem, layer_sem, wide_sem, back_sem, mat_sem, made_sem = take(6)
+    z, x, y, c = place()
+    parts = low.shape[0] // 512
+
+    def at(k):
+        return pl.ds(k * 512, 512)
+
+    low_in = [pltpu.make_async_copy(low.at[at(k)], low_buf.at[at(k)], low_sem.at[k]) for k in range(parts)]
+    layer_in = [pltpu.make_async_copy(layer.at[at(k)], layer_buf.at[at(k)], layer_sem.at[k]) for k in range(parts)]
+    wide_to = [pltpu.make_async_copy(wide_buf.at[at(k)], grad_out.at[at(k)], wide_sem.at[k]) for k in range(parts)]
+    layer_to = [pltpu.make_async_copy(layer_buf.at[at(k)], layer_out.at[at(k)], back_sem.at[k]) for k in range(parts)]
+    mats_in = [
+        pltpu.make_async_copy(mats[a][i], held[a][i], mat_sem.at[3 * a + i]) for a in range(4) for i in range(3)
+    ]
+    mats_to = [
+        [pltpu.make_async_copy(made[a][i], mats_out[a][i], made_sem.at[4 * a + i]) for i in range(4)]
+        for a in range(4)
+    ]
+    start(low_in[:2] + mats_in + low_in[2:] + layer_in)
+    squared_sums = sums[...] * sums[...]
+    total = jnp.sum(jnp.sum(squared_sums, 1, keepdims=True), 0, keepdims=True) + squares[0:1, 0:1]
+    gradient_norm = jnp.sqrt(total)
+    clip_factor = clip_limit / jnp.maximum(gradient_norm, clip_limit)
+    norm_out[0] = jnp.max(jnp.broadcast_to(gradient_norm, (8, 128)))
+    kept_out[0] = jnp.max(kept[...]).astype(jnp.int32)
+    for k in range(parts):
+        low_in[k].wait()
+        wide_buf[at(k), :] = low_buf[at(k), :].astype(f32)
+        wide_to[k].start()
+    for copy in mats_in:
+        copy.wait()
+
+    def update(a, index, grad):
+        new = adamw_update_step(
+            held[a][0][index], held[a][1][index], held[a][2][index], grad, clip_factor, learn_rate
+        )
+        for i in range(3):
+            made[a][i][index] = new[i]
+        made[a][3][index] = new[0].astype(bf16)
+
+    def third(value):
+        return jnp.where(y == 0, value[:, 0:64], value[:, 64:128])
+
+    for h in range(2):
+        span = slice(h * half, (h + 1) * half)
+        update(2, (span, slice(None)), t_one[h])
+        update(3, (span, slice(None)), t_two[h])
+    start(mats_to[2] + mats_to[3])
+    for h in range(2):
+        span = slice(h * half, (h + 1) * half)
+        for k in range(3):
+            wide = jnp.concatenate([t_a[h, :, 128 * k : 128 * k + 128], t_b[h, :, 64 * k : 64 * k + 64]], 1)
+            update(0, (k, span, slice(None)), wide)
+    start(mats_to[0])
+    halves = [jnp.concatenate([t_out[h, :, 0:128], third(t_out[h, :, 128:256])], 1) for h in range(2)]
+    update(1, (slice(None), slice(None)), jnp.concatenate(halves, 0).T)
+    start(mats_to[1])
+    for k in range(parts):
+        layer_in[k].wait()
+        layer_to[k].start()
+    spot = 2 * c + y
+    near = sums[10:12, pl.ds(pl.multiple_of(384 * c + 128 * y, 128), 128)]
+    far = third(sums[10:12, pl.ds(pl.multiple_of(384 * c + 256, 128), 128)])
+    slopes = [jnp.concatenate([near, far], 1), sums[pl.ds(6 + spot, 1), :], sums[0:6, :]]
+    for a in range(3):
+        shape = slopes[a].shape
+        new = adamw_update_step(*(ref[...].reshape(shape) for ref in smalls[a]), slopes[a], clip_factor, vector_rate)
+        for i in range(3):
+            smalls_out[a][i][...] = new[i].reshape(smalls_out[a][i].shape)
+    for copy in wide_to + layer_to + sum(mats_to, []):
+        copy.wait()
+
+
+def finish(low, layer, shares, sums, squares, kept, states):
+    half = shares[0].shape[1]
+    rows = low.shape[0]
+    parts = rows // 512
+    turned = tuple(value.T for value in states[3])
+    mats = (states[0], states[1], states[2], turned)
+    smalls = states[4:]
+    shape = jax.ShapeDtypeStruct
+    outs = pl.pallas_call(
+        functools.partial(finish_kernel, half),
+        out_shape=[shape((rows, WIDTH), f32), shape((rows, WIDTH), bf16), shape((1,), f32), shape((1,), jnp.int32)]
+        + [shape(m[0].shape, d) for m in mats for d in (f32, f32, f32, bf16)]
+        + [shape(m[0].shape, f32) for m in smalls for _ in range(3)],
+        in_specs=[HBM] * 2 + [VM] * 8 + [HBM] * 12 + [VM] * 9,
+        out_specs=[HBM] * 2 + [SM] * 2 + [HBM] * 16 + [VM] * 9,
+        scratch_shapes=[
+            pltpu.VMEM((rows, WIDTH), bf16),
+            pltpu.VMEM((rows, WIDTH), f32),
+            pltpu.VMEM((rows, WIDTH), bf16),
+        ]
+        + [pltpu.VMEM(m[0].shape, f32) for m in mats for _ in range(3)]
+        + [pltpu.VMEM(m[0].shape, d) for m in mats for d in (f32, f32, f32, bf16)]
+        + [DMA((parts,))] * 4
+        + [DMA((12,)), DMA((16,))],
+        compiler_params=pltpu.CompilerParams(vmem_limit_bytes=VMEM_CAP),
+        name="finish",
+    )(low, layer, *shares, sums, squares, kept, *(v for m in mats for v in m), *(v for m in smalls for v in m))
+    grad, layer_output, norm_value, kept_value = outs[:4]
+    proj, comb, expd, redc = (outs[4 + 4 * a : 8 + 4 * a] for a in range(4))
+    redc = [value.T for value in redc]
+    offs, shif, vecs = (outs[20 + 3 * a : 23 + 3 * a] for a in range(3))
+    return (
+        layer_output,
+        grad,
+        kept_value.reshape(()),
+        norm_value.reshape(()),
+        *proj[:3],
+        *comb[:3],
+        *expd[:3],
+        *redc[:3],
+        *offs,
+        *shif,
+        *vecs,
+        proj[3],
+        comb[3],
+        expd[3],
+        redc[3],
+    )
 
 
 def general_step(
@@ -2175,17 +2316,17 @@
     offsets,
     shifts,
     vectors,
+    states,
 ):
     n_dp, nz, c, r, half, cols = slices
     seq_dev = keep_flags.shape[0]
     w_qkv, g_out, g_one, g_two, shift_rows, kept, qkv, att, att_rows, lse = front(
         activations, projections, combiner, expander, reducer, offsets, shifts, keep_flags, nz
     )
-    kept_float = kept[0, 0]
-    kept_total = kept_float.astype(jnp.int32)
-    shares = keep_flags.astype(f32) * jnp.float32(seq_dev * n_dp) / kept_float
     layer_output, resid, d_att, dw_out, dw_one, dw_two, dshift, dvec = core(
-        shares,
+        seq_dev * n_dp,
+        keep_flags,
+        kept,
         mask_counts,
         att_rows,
         g_out.reshape(2, 2, WIDTH, 256),
@@ -2213,19 +2354,7 @@
         dshift,
         nz,
     )
-    off = sums[10:12].reshape(4, 384)
-    off = jnp.concatenate([off[:, 0:128], off[:, 256:320], off[:, 128:256], off[:, 320:384]], 1)
-    sums = jnp.concatenate([sums[:10], off.reshape(2, WIDTH), sums[12:]], 0)
-    y = lax.axis_index("mp") // 2
-    t_a = t_a.reshape(r, 3, 128).transpose(1, 0, 2)
-    t_b = t_b.reshape(r, 256)[:, :192].reshape(r, 3, 64).transpose(1, 0, 2)
-    share_proj = jnp.concatenate([t_a, t_b], 2)
-    t_out = t_out.reshape(r, 256)
-    third = lax.dynamic_slice_in_dim(t_out, 128 + 64 * y, 64, 1)
-    share_comb = jnp.concatenate([t_out[:, :128], third], 1).T
-    share_expd = t_one.reshape(r, WIDTH)
-    share_redc = t_two.reshape(r, WIDTH).T
-    return share_proj, share_comb, share_expd, share_redc, sums, squares, layer_output, input_low, kept_total
+    return finish(input_low, layer_output, (t_two, t_one, t_out, t_a, t_b), sums, squares, kept, states)
 
 
 def shards(
@@ -2266,10 +2395,32 @@
     cols = projections.shape[2]
     slices = (n_dp, nz, c, r, half, cols)
     if half % 16 == 0 and cols == 192:
-        step = fused_step
-    else:
-        step = general_step
-    outs = step(
+        states = (
+            (projections, momentum_projections, variance_projections),
+            (combiner, momentum_combiner, variance_combiner),
+            (expander, momentum_expander, variance_expander),
+            (reducer, momentum_reducer, variance_reducer),
+            (offsets, momentum_offsets, variance_offsets),
+            (shifts, first_moment_shifts, second_moment_shifts),
+            (vectors, momentum_vectors, variance_vectors),
+        )
+        return fused_step(
+            slices,
+            activations,
+            keep_flags,
+            mask_counts,
+            mask_positions,
+            cotangents,
+            projections,
+            combiner,
+            expander,
+            reducer,
+            offsets,
+            shifts,
+            vectors,
+            states,
+        )
+    outs = general_step(
         slices,
         activations,
         keep_flags,

time: 331 us -> 307 us (0.927)
  other arithmetic: 19.3 us -> 0 us
  Pallas kernels: 293 us -> 306 us
  local copies, waits for them, and re-layouts: 12.9 us -> 0 us
  between operations: 5.36 us -> 0.85 us
    convert_element_type x5 -> x0, other arithmetic: 12.9 us -> none  [the longest x1 6.82 us: shards(): input_low.astype(f32)]
    pallas_call x1 -> x2, Pallas kernels: 56.8 us -> 69.7 us  [the longest x1 56.9 us: core(): pl.pallas_call(functools.partial(core_kernel, seqs), out_shape=[jax.Shape...]
    unnamed x49 -> x0, local copies, waits for them, and re-layouts: 7.09 us -> none
    slice x7 -> x0, local copies, waits for them, and re-layouts: 4.18 us -> none  [the longest x1 1.19 us: shards(): total_squares = squares[0, 0] + jnp.sum(sums * sums)]
where the time goes in v3:
time: 307 us
  Pallas kernels  306 us (100%)
    pallas_call x1, Pallas kernels, rear(): pl.pallas_call(functools.partial(rear_kernel, nz, half), out_shape=[jax.S...  141 us
    pallas_call x1, Pallas kernels, front(): pl.pallas_call(functools.partial(front_kernel, nz, half, cols), out_shape...  95 us
    pallas_call x1, Pallas kernels, core(): pl.pallas_call(functools.partial(core_kernel, seqs), out_shape=[jax.Shape...  56.9 us
    pallas_call x1, Pallas kernels, finish(): pl.pallas_call(functools.partial(finish_kernel, half), out_shape=[shape((...  12.8 us

profile of v3, /device:TPU:0, one launch (start us, length us, event | category | flops | bytes accessed | tf_op | source)
XLA Modules:
  0.0 306.7 jit_solution(1798926483967640687)
XLA Ops:
  0.7 95.0 %front.1 = (bf16[3,768,384]{2,1,0:T(8,128)(2,1)}, bf16[2,2,4,2,2,48,256]{6,5,4,3,2,1,0:T(8,128)(2,1)}, bf16[2,2,4,2,2,48,768]{6,5,4,3,2,1,0:T(8,128)(2,1)}, bf16...) custom-call(bf16[3072,768]{1,0:T(8,128)(2,1)} %x_ref.5, ...), custom_call_target="tpu_custom_call" | custom-call | tf_op jit(solution)/shard_map/front/pallas_call | solution.py:1233
  95.7 56.9 %core.1 = (bf16[3072,768]{1,0:T(8,128)(2,1)}, f32[768,768]{1,0:T(8,128)}, bf16[2,768,384]{2,1,0:T(8,128)(2,1)}, bf16[2,2,768,256]{3,2,1,0:T(8,128)(2,1)}, bf16[4...) custom-call(s32[3]{0:T(128)} %keep_ref.3, ...), custom_call_target="tpu_custom_call" | custom-call | tf_op jit(solution)/shard_map/core/pallas_call | solution.py:893
  152.6 141.1 %rear.1 = (f32[2,48,768]{2,1,0:T(8,128)}, f32[2,48,768]{2,1,0:T(8,128)}, f32[2,48,256]{2,1,0:T(8,128)}, f32[2,48,384]{2,1,0:T(8,128)}, f32[2,48,256]{2,1,0:T(8,1...) custom-call(bf16[3072,768]{1,0:T(8,128)(2,1)} %x_ref.5, ...), custom_call_target="tpu_custom_call" | custom-call | tf_op jit(solution)/shard_map/rear/pallas_call | solution.py:1758
  293.7 12.8 %finish.1 = (f32[3072,768]{1,0:T(8,128)}, bf16[3072,768]{1,0:T(8,128)(2,1)}, f32[1]{0:T(128)}, s32[1]{0:T(128)}, f32[3,96,192]{2,1,0:T(8,128)}, /*index=5*/f32[3...) custom-call(bf16[3072,768]{1,0:T(8,128)(2,1)} %get-tuple-element.101, ...), custom_call_target="tpu_custom_call" | custom-call | tf_op jit(solution)/shard_map/finish/pallas_call | solution.py:2194

commit v4 on v3

--- a/solution.py
+++ b/solution.py
@@ -1270,6 +1270,50 @@
     )(activations, projections, combiner, expander, reducer.T, offsets, shifts, keep_flags)
 
 
+Y_FIRST = (False, False, True, False, True, False, False, True, False, False)
+CORE_ORDER = (5, 4, 1, 2, 0, 3)
+SHARED_STEPS = {
+    0: [(1, 5), (1, 4)],
+    1: [(1, 1)],
+    2: [(1, 2), (1, 0)],
+    3: [(2, 5), (2, 4), (1, 3)],
+}
+WHOLE_STEPS = {
+    1: [(2, 1)],
+    2: ["sum", (2, 2)],
+    3: [(3, 5)],
+    6: [(4, 5), (3, 1)],
+    7: [(2, 0)],
+    8: ["done", (3, 4), (1, 6), (1, 7)],
+    10: [(4, 1)],
+    11: [(4, 4), (3, 0)],
+}
+LATE_STEPS = [(2, 3), (1, 8), (1, 9)]
+TAIL_STEPS = [
+    "pass",
+    (3, 2),
+    (4, 0),
+    (2, 7),
+    (2, 6),
+    (2, 8),
+    (4, 2),
+    (3, 3),
+    "small",
+    (2, 9),
+    "give",
+    (3, 6),
+    (3, 7),
+    (3, 8),
+    "small z",
+    (3, 9),
+    (4, 3),
+    (4, 6),
+    (4, 7),
+    (4, 8),
+    (4, 9),
+]
+
+
 def rear_kernel(
     nz,
     half,
@@ -1325,7 +1369,7 @@
     partial = [p_two, p_one, p_out, dqa, dqb]
     outs = [t_two, t_one, t_out, t_a, t_b]
     chunks = [(a, h) for a in range(n) for h in range(2)]
-    y_first = [a == 1 and h == 0 or a >= 2 and h == 0 for a, h in chunks]
+    y_first = Y_FIRST
 
     def at(b):
         return pl.ds(pl.multiple_of(b * BLK, BLK), BLK)
@@ -1342,7 +1386,7 @@
 
     load_rows(0).start()
     load_rows(1).start()
-    for i in range(6):
+    for i in CORE_ORDER:
         load_own(i).start()
     greet(others + [along_x, along_y, along_c])
     heads = [
@@ -1359,7 +1403,7 @@
         a, h = chunks[i]
         return [remote(partial[a].at[1 - c, :, :, :, h], gap[i], core_s.at[i], core_r.at[i], along_c)]
 
-    for i in range(6):
+    for i in CORE_ORDER:
         start(core_stage(i))
 
     def cell(i, yy, zz, xx):
@@ -1477,7 +1521,7 @@
     lane = lax.broadcasted_iota(jnp.int32, (BLK, 128), 1)
     sub = lax.broadcasted_iota(jnp.int32, (128, BLK), 0)
 
-    def attention(s, hooks, before):
+    def attention(s, hooks, before, run):
         n_units = 4 if s == 0 else 2
         kv = pl.ds(s * LEN, LEN)
 
@@ -1498,8 +1542,7 @@
 
                     @pl.when(p * n_units + i == when)
                     def _(todo=todo):
-                        for step in todo:
-                            step()
+                        run(todo)
 
                 u = i + 4 * s
                 q_row = pl.ds(pl.multiple_of((512 * y if s else 0) + u * BLK, BLK), BLK)
@@ -1599,7 +1642,17 @@
         give_y(2).wait_recv()
         pass_on(2).start()
 
-    attention(1, shared_hooks(r1, r2, r3, r4), {})
+    stages = {1: r1, 2: r2, 3: r3, 4: r4}
+    named = {"sum": shared_sum, "done": shared_done, "pass": shared_pass}
+
+    def run(steps):
+        for step in steps:
+            if step in named:
+                named[step]()
+            else:
+                stages[step[0]](step[1])
+
+    attention(1, SHARED_STEPS, {}, run)
     lax.fori_loop(4, 8, inputs, 0)
     for yy in range(2):
         swap_core(yy).start()
@@ -1624,34 +1677,13 @@
 
         lax.fori_loop(0, nz, body, 0)
 
-    def send_a():
+    def weights_a():
         weights(0, False)
         weights(1, False)
-        r1(6)
-        r1(7)
-
-    attention(0, whole_hooks(r1, r2, r3, r4, shared_sum, shared_done, shared_pass), {2: send_a})
-    lax.fori_loop(0, 2, lambda i, carry: inputs(2 * (1 - c) + i, carry), 0)
-    swap_own().start()
+
+    attention(0, WHOLE_STEPS, {2: weights_a}, run)
     weights(2, True)
-    r1(8)
-    r1(9)
-    lax.fori_loop(0, 2, lambda i, carry: inputs(2 * c + i, carry), 0)
-    swap_own().wait_recv()
-    own_rows = pl.ds(pl.multiple_of(512 * c, 512), 512)
-    mine[pl.ds(0, 512), :] = (
-        resid_ref[pl.ds(0, 512), :] + (dx[own_rows, :].astype(f32) + dx_in[pl.ds(0, 512), :].astype(f32))
-    ).astype(bf16)
-    give_y(0).start()
-    for k in range(2):
-        give_c(k).start()
-        keep(k).start()
-    small_buf[0] = jnp.zeros_like(sums_ref)
-    small_buf[0, 0:6, :] = dvec_ref[0:6, :]
-    for j in range(4):
-        small_buf[0, 6 + j : 7 + j, :] = dshift_ref[j]
-    small_buf[0, 10:12, pl.ds(pl.multiple_of(384 * c, 128), 384)] = doff[0:2, :]
-
+    run(LATE_STEPS)
     def swap(buf, inn, k, stage):
         peer = (along_c, along_y, along_x)[stage]
         return remote(buf.at[stage], inn.at[stage], bs.at[k + stage], br.at[k + stage], peer)
@@ -1680,34 +1712,70 @@
             acc = acc + slots[d]
         return acc
 
+    lax.fori_loop(0, 2, lambda i, carry: inputs(2 * (1 - c) + i, carry), 0)
+    swap_own().start()
+    small_buf[0] = jnp.zeros_like(sums_ref)
+    small_buf[0, 0:6, :] = dvec_ref[0:6, :]
+    for j in range(4):
+        small_buf[0, 6 + j : 7 + j, :] = dshift_ref[j]
+    small_buf[0, 10:12, pl.ds(pl.multiple_of(384 * c, 128), 384)] = doff[0:2, :]
     swap(small_buf, small_in, 0, 0).start()
-    r3(6)
-    r3(7)
+    lax.fori_loop(0, 2, lambda i, carry: inputs(2 * c + i, carry), 0)
+    swap_own().wait_recv()
+    own_rows = pl.ds(pl.multiple_of(512 * c, 512), 512)
+    mine[pl.ds(0, 512), :] = (
+        resid_ref[pl.ds(0, 512), :] + (dx[own_rows, :].astype(f32) + dx_in[pl.ds(0, 512), :].astype(f32))
+    ).astype(bf16)
     merge(small_buf, small_in, small_z, 0, 0)
-    r2(8)
-    r2(9)
-    give_y(1).start()
-    merge(small_buf, small_in, small_z, 0, 1)
-    r4(6)
-    r4(7)
-    merge(small_buf, small_in, small_z, 0, 2)
-    r3(8)
-    r3(9)
+    for k in range(2):
+        give_c(k).start()
+        keep(k).start()
+
+    def give_own():
+        give_y(0).start()
+        give_y(1).start()
+
+    named["small"] = lambda: merge(small_buf, small_in, small_z, 0, 1)
+    named["small z"] = lambda: merge(small_buf, small_in, small_z, 0, 2)
+    named["give"] = give_own
+    run(TAIL_STEPS)
     sums_ref[...] = total(small_buf, small_z, 0)
-    r4(8)
-    r4(9)
     acc = jnp.float32(0.0)
     for a in range(n):
         for h in range(2):
             acc = acc + jnp.sum(outs[a][h] * outs[a][h])
     norm_buf[0] = jnp.broadcast_to(acc, (8, 128))
-    swap(norm_buf, norm_in, 3, 0).start()
-    for stage in range(3):
-        merge(norm_buf, norm_in, norm_z, 3, stage)
-    norm_ref[...] = total(norm_buf, norm_z, 3)
-    for k in range(2):
-        give_y(k).wait_recv()
-        pass_on(k).start()
+
+    def norm_swap(stage):
+        peer = (along_c, along_x, along_y)[stage]
+        return remote(
+            norm_buf.at[stage if stage < 2 else 3], norm_in.at[stage], bs.at[3 + stage], br.at[3 + stage], peer
+        )
+
+    norm_swap(0).start()
+    give_y(0).wait_recv()
+    pass_on(0).start()
+    norm_swap(0).wait()
+    norm_buf[1] = norm_buf[0] + norm_in[0]
+    norm_swap(1).start()
+    norm_swap(1).wait()
+    norm_buf[2] = norm_buf[1] + norm_in[1]
+    norm_z[z] = norm_buf[2]
+    over_z = [
+        remote(norm_buf.at[2], norm_z.at[z], bzs.at[1, d - 1], bzr.at[1, d - 1], others[d - 1]) for d in range(1, nz)
+    ]
+    start(over_z)
+    for copy in over_z:
+        copy.wait()
+    squares = norm_z[0]
+    for d in range(1, nz):
+        squares = squares + norm_z[d]
+    norm_buf[3] = squares
+    norm_swap(2).start()
+    give_y(1).wait_recv()
+    pass_on(1).start()
+    norm_swap(2).wait()
+    norm_ref[...] = norm_buf[3] + norm_in[2]
     for k in range(3):
         keep(k).wait()
         give_c(k).wait_recv()
@@ -1719,35 +1787,11 @@
         sent((core_stage(i) if i < 6 else []) + copy_two(i) + copy_three(i) + copy_z(i))
 
 
-def shared_hooks(r1, r2, r3, r4):
-    return {
-        0: [lambda: r1(0), lambda: r1(1)],
-        1: [lambda: r1(2), lambda: r1(3)],
-        2: [lambda: r1(4), lambda: r1(5)],
-        5: [lambda: r2(0), lambda: r2(1)],
-    }
-
-
-def whole_hooks(r1, r2, r3, r4, shared_sum, shared_done, shared_pass):
-    return {
-        0: [shared_sum, lambda: r2(2), lambda: r2(3)],
-        2: [lambda: r3(0), lambda: r3(1)],
-        4: [shared_done, lambda: r2(4), lambda: r2(5)],
-        5: [lambda: r3(2), lambda: r3(3)],
-        6: [lambda: r4(0), lambda: r4(1)],
-        7: [lambda: r3(4), lambda: r3(5)],
-        8: [shared_pass],
-        9: [lambda: r4(2), lambda: r4(3)],
-        10: [lambda: r4(4), lambda: r4(5)],
-        11: [lambda: r2(6), lambda: r2(7)],
-    }
-
-
 def rear(activations, weights, qkv, out, lse, datt, p_two, p_one, p_out, resid, dvec, dshift, nz):
     half = p_two.shape[-2]
     widths = [WIDTH, WIDTH, 256, 384, 256]
     chunks = [(a, h) for a in range(5) for h in range(2)]
-    y_first = [a == 1 and h == 0 or a >= 2 and h == 0 for a, h in chunks]
+    y_first = Y_FIRST
     own = [pltpu.VMEM((2, nz, 2, half, widths[a]), bf16) for a, h in chunks[:6]]
     two = [
         pltpu.VMEM(((nz, 2) if first else (2, nz)) + (half, widths[a]), bf16) for (a, h), first in zip(chunks, y_first)

time: 307 us -> 278 us (0.906)
  Pallas kernels: 306 us -> 277 us
    pallas_call x1, Pallas kernels: 141 us -> 113 us  [rear(): pl.pallas_call(functools.partial(rear_kernel, nz, half), out_shape=[jax.S...]
where the time goes in v4:
time: 278 us
  Pallas kernels  277 us (100%)
    pallas_call x1, Pallas kernels, rear(): pl.pallas_call(functools.partial(rear_kernel, nz, half), out_shape=[jax.S...  113 us
    pallas_call x1, Pallas kernels, front(): pl.pallas_call(functools.partial(front_kernel, nz, half, cols), out_shape...  95 us
    pallas_call x1, Pallas kernels, core(): pl.pallas_call(functools.partial(core_kernel, seqs), out_shape=[jax.Shape...  56.9 us
    pallas_call x1, Pallas kernels, finish(): pl.pallas_call(functools.partial(finish_kernel, half), out_shape=[shape((...  12.8 us

profile of v4, /device:TPU:0, one launch (start us, length us, event | category | flops | bytes accessed | tf_op | source)
XLA Modules:
  0.0 278.2 jit_solution(17717819326006595681)
XLA Ops:
  0.7 95.0 %front.1 = (bf16[3,768,384]{2,1,0:T(8,128)(2,1)}, bf16[2,2,4,2,2,48,256]{6,5,4,3,2,1,0:T(8,128)(2,1)}, bf16[2,2,4,2,2,48,768]{6,5,4,3,2,1,0:T(8,128)(2,1)}, bf16...) custom-call(bf16[3072,768]{1,0:T(8,128)(2,1)} %x_ref.5, ...), custom_call_target="tpu_custom_call" | custom-call | tf_op jit(solution)/shard_map/front/pallas_call | solution.py:1233
  95.7 56.9 %core.1 = (bf16[3072,768]{1,0:T(8,128)(2,1)}, f32[768,768]{1,0:T(8,128)}, bf16[2,768,384]{2,1,0:T(8,128)(2,1)}, bf16[2,2,768,256]{3,2,1,0:T(8,128)(2,1)}, bf16[4...) custom-call(s32[3]{0:T(128)} %keep_ref.3, ...), custom_call_target="tpu_custom_call" | custom-call | tf_op jit(solution)/shard_map/core/pallas_call | solution.py:893
  152.6 112.6 %rear.1 = (f32[2,48,768]{2,1,0:T(8,128)}, f32[2,48,768]{2,1,0:T(8,128)}, f32[2,48,256]{2,1,0:T(8,128)}, f32[2,48,384]{2,1,0:T(8,128)}, f32[2,48,256]{2,1,0:T(8,1...) custom-call(bf16[3072,768]{1,0:T(8,128)(2,1)} %x_ref.5, ...), custom_call_target="tpu_custom_call" | custom-call | tf_op jit(solution)/shard_map/rear/pallas_call | solution.py:1802
  265.2 12.8 %finish.1 = (f32[3072,768]{1,0:T(8,128)}, bf16[3072,768]{1,0:T(8,128)(2,1)}, f32[1]{0:T(128)}, s32[1]{0:T(128)}, f32[3,96,192]{2,1,0:T(8,128)}, /*index=5*/f32[3...) custom-call(bf16[3072,768]{1,0:T(8,128)(2,1)} %get-tuple-element.101, ...), custom_call_target="tpu_custom_call" | custom-call | tf_op jit(solution)/shard_map/finish/pallas_call | solution.py:2238

commit v5 on v4

--- a/solution.py
+++ b/solution.py
@@ -679,8 +679,8 @@
     pos_ref,
     cot_ref,
     layer_ref,
-    resid_ref,
-    datt_ref,
+    resid_out,
+    datt_out,
     dwo_ref,
     o1_ref,
     o2_ref,
@@ -706,11 +706,14 @@
     dw1_ref,
     dw2_ref,
     out_ref,
+    resid_ref,
+    datt_ref,
     sem,
     store,
     give_s,
     give_r,
     local,
+    out_sem,
 ):
     z, x, y, c = place()
     along_y, along_c = dev(z, x, 1 - y, c), dev(z, x, y, 1 - c)
@@ -869,6 +872,12 @@
         give(k, 0).wait_recv()
         give(k, 2).start()
 
+    leave = [
+        pltpu.make_async_copy(resid_ref, resid_out, out_sem.at[0]),
+        pltpu.make_async_copy(datt_ref, datt_out, out_sem.at[1]),
+    ]
+    start(leave)
+
     def six(b, carry):
         for p in range(2):
             grad = dot(d2_low_t[at(b), :], att_ref[p]).astype(bf16)
@@ -878,6 +887,8 @@
         return carry
 
     lax.fori_loop(0, blocks, six, 0)
+    for copy in leave:
+        copy.wait()
     for j in range(4):
         pltpu.make_async_copy(dw2_ref.at[j], o2_ref.at[j], store.at[0, j]).wait()
         pltpu.make_async_copy(dw1_ref.at[j], o1_ref.at[j], store.at[1, j]).wait()
@@ -903,7 +914,7 @@
             jax.ShapeDtypeStruct((8, WIDTH), f32),
         ],
         in_specs=[SM, VM, SM, VM, VM, HBM, HBM, VM, VM, HBM, VM, HBM],
-        out_specs=[HBM, VM, VM, VM, HBM, HBM, VM, VM],
+        out_specs=[HBM, HBM, HBM, VM, HBM, HBM, VM, VM],
         scratch_shapes=[
             pltpu.VMEM(big, bf16),
             pltpu.VMEM((2, slots, WIDTH), bf16),
@@ -925,15 +936,37 @@
             pltpu.VMEM((4,) + big, bf16),
             pltpu.VMEM((4,) + big, bf16),
             pltpu.VMEM(big, bf16),
+            pltpu.VMEM(big, f32),
+            pltpu.VMEM((2, WIDTH, 384), bf16),
             DMA((6,)),
             DMA((2, 4)),
             DMA((2, 3)),
             DMA((2, 3)),
             DMA((2,)),
+            DMA((2,)),
         ],
         compiler_params=pltpu.CompilerParams(collective_id=7, has_side_effects=True, vmem_limit_bytes=VMEM_CAP),
         name="core",
     )(keep_flags, kept, counts, att, wo, w1, w2, shifts, vectors, activations, positions, cotangents)
+
+
+GATHER_ORDERS = ("zxy", "zyx", "zxy", "zxy", "zxy", "zyx", "zyx", "zxy", "zyx", "zxy")
+GATHER_FIRST = (3, 1,)
+GATHER_START = [(1, 3), (0, 0), (1, 1), (0, 7), (2, 3), (1, 0), (0, 8), (2, 1), (2, 0), (3, 3), (1, 7), (0, 2), (3, 1), (1, 8), (0, 9), (3, 0)]
+GATHER_STEPS = {
+    0: [(1, 2), (0, 5), (0, 6)],
+    2: [(2, 7)],
+    4: [(2, 8), (2, 2)],
+    5: [(1, 9), (0, 4)],
+    6: [(1, 5)],
+    10: [(1, 6)],
+    11: [(1, 4)],
+    13: [(2, 5)],
+    15: [(2, 9)],
+    17: [(2, 6), (2, 4)],
+}
+GATHER_LAST_PAIR = [(3, 7), (3, 8), (3, 2)]
+GATHER_END = [(3, 5), (3, 9), (3, 6), (3, 4)]
 
 
 def front_kernel(
@@ -948,17 +981,21 @@
     off_ref,
     shift_ref,
     keep_ref,
-    w_ref,
+    w_out,
     g_out,
     g_one,
     g_two,
     small_ref,
     kept_ref,
+    qkv_out,
+    att_out,
+    rows_ref,
+    lse_out,
+    rows,
+    w_ref,
     qkv_ref,
     att_ref,
-    rows_ref,
     lse_ref,
-    rows,
     sh_qa,
     sh_qb,
     sh_out,
@@ -973,10 +1010,10 @@
     bias,
     zs,
     zr,
-    two_s,
-    two_r,
-    three_s,
-    three_r,
+    x_s,
+    x_r,
+    y_s,
+    y_r,
     core_s,
     core_r,
     local,
@@ -986,6 +1023,7 @@
     keep_r,
     row_s,
     row_r,
+    out_sem,
 ):
     z, x, y, c = place()
     others = [dev(lax.rem(z + d, nz), x, y, c) for d in range(1, nz)]
@@ -1033,22 +1071,18 @@
     chunks = [(a, h) for a in range(5) for h in range(2)]
     total = len(chunks)
 
-    def stage_z(i):
+    def stage(i, k):
         a, h = chunks[i]
-        return [
-            remote(shards[a].at[h], own[a].at[y, z, x, h], zs.at[i, d - 1], zr.at[i, d - 1], others[d - 1])
-            for d in range(1, nz)
-        ]
-
-    def stage_two(i):
-        a, h = chunks[i]
-        block = own[a].at[y, :, x, h]
-        return [remote(block, block, two_s.at[i], two_r.at[i], along_x if h == 0 else along_y)]
-
-    def stage_three(i):
-        a, h = chunks[i]
-        block = own[a].at[y, :, :, h] if h == 0 else own[a].at[:, :, x, h]
-        return [remote(block, block, three_s.at[i], three_r.at[i], along_y if h == 0 else along_x)]
+        order = GATHER_ORDERS[i]
+        done, axis = order[:k], order[k]
+        spots = tuple(slice(None) if name in done else spot for name, spot in (("y", y), ("z", z), ("x", x)))
+        block = own[a].at[spots + (h,)]
+        source = block if k else shards[a].at[h]
+        if axis == "x":
+            return [remote(source, block, x_s.at[i], x_r.at[i], along_x)]
+        if axis == "y":
+            return [remote(source, block, y_s.at[i], y_r.at[i], along_y)]
+        return [remote(source, block, zs.at[i, d - 1], zr.at[i, d - 1], others[d - 1]) for d in range(1, nz)]
 
     def stage_core(i):
         a, h = chunks[i]
@@ -1067,32 +1101,25 @@
         pltpu.make_async_copy(sh_keep, keep_in.at[z, x], local.at[8]),
     ]
     start(kept)
-    start(stage_z(0) + stage_z(1) + small_first + keep_first)
-    for i in range(2, total):
-        start(stage_z(i))
+    start(small_first + keep_first)
+    for i in GATHER_FIRST:
+        start(stage(i, 0))
     for copy in kept + loads:
         copy.wait()
 
-    def s1(i):
-        arrived(stage_z(i))
-        start(stage_two(i))
-
-    def s2(i):
-        arrived(stage_two(i))
-        start(stage_three(i))
-
-    def s3(i):
-        arrived(stage_three(i))
-        start(stage_core(i))
-
-    s1(0)
-    s1(1)
+    def run(steps):
+        for k, i in steps:
+            if k:
+                arrived(stage(i, k - 1))
+            if k < 3:
+                start(stage(i, k))
+            elif i >= 4:
+                start(stage_core(i))
+
+    run(GATHER_START[:2])
     arrived(keep_first + small_first)
     start(keep_second + small_second)
-    s2(0)
-    s1(2)
-    s2(1)
-    s1(3)
+    run(GATHER_START[2:])
     arrived(keep_second + small_second)
     for yy in range(2):
         bias[yy] = jnp.zeros((1, 384), f32)
@@ -1107,7 +1134,6 @@
         for xx in range(2):
             acc = acc + keep_in[zz, xx]
     kept_ref[...] = acc
-    arrived(stage_three(0) + stage_three(1))
 
     def place_pair(i, carry):
         yy, k = i // (4 * nz), lax.rem(i, 4 * nz)
@@ -1126,6 +1152,12 @@
             for i, (there, here) in enumerate(rows_of(1 - c))
         ]
 
+    def pair_out(p):
+        return [
+            pltpu.make_async_copy(w_ref.at[p], w_out.at[p], out_sem.at[p]),
+            pltpu.make_async_copy(qkv_ref.at[p], qkv_out.at[p], out_sem.at[3 + p]),
+        ]
+
     def row_kept(p):
         col = pl.ds(pl.multiple_of(p * 128, 128), 128)
         return [
@@ -1133,22 +1165,13 @@
             for i, (there, here) in enumerate(rows_of(c))
         ]
 
-    hooks = {
-        0: [lambda: s2(2), lambda: s2(3)],
-        1: [lambda: s1(4), lambda: s1(5)],
-        3: [lambda: s2(4), lambda: s2(5)],
-        4: [lambda: s1(6), lambda: s1(7)],
-        9: [lambda: s3(4), lambda: s3(5)],
-        10: [lambda: s2(6), lambda: s2(7)],
-        11: [lambda: s1(8), lambda: s1(9)],
-    }
     lanes = lax.broadcasted_iota(jnp.int32, (BLK, 128), 1)
     ones = jnp.ones((LEN, 128), bf16)
 
     def pair(p, carry):
         @pl.when(p == 2)
         def _():
-            arrived(stage_three(2) + stage_three(3))
+            run(GATHER_LAST_PAIR)
 
             def place_last(k, carry):
                 zz, xx, h = k // 4, lax.rem(k // 2, 2), lax.rem(k, 2)
@@ -1169,12 +1192,11 @@
         lax.fori_loop(0, 2 * LEN // BLK, project, 0)
 
         def unit(u, carry):
-            for when, todo in hooks.items():
+            for when, todo in GATHER_STEPS.items():
 
                 @pl.when(p * 6 + u == when)
                 def _(todo=todo):
-                    for step in todo:
-                        step()
+                    run(todo)
 
             shared = u >= LEN // BLK
             at = pl.ds(pl.multiple_of(u * BLK, BLK), BLK)
@@ -1201,18 +1223,18 @@
             return carry
 
         lax.fori_loop(0, 6, unit, 0)
-        start(row_copies(p) + row_kept(p))
+        start(row_copies(p) + row_kept(p) + pair_out(p))
         for copy in row_kept(p):
             copy.wait()
         return carry
 
     lax.fori_loop(0, 3, pair, 0)
-    s3(6)
-    s3(7)
-    s2(8)
-    s2(9)
-    s3(8)
-    s3(9)
+    last_out = [
+        pltpu.make_async_copy(att_ref, att_out, out_sem.at[6]),
+        pltpu.make_async_copy(lse_ref, lse_out, out_sem.at[7]),
+    ]
+    start(last_out)
+    run(GATHER_END)
     for p in range(3):
         arrived(row_copies(p))
     for i in range(4, total):
@@ -1220,10 +1242,12 @@
     for p in range(3):
         sent(row_copies(p))
     for i in range(total):
-        sent(stage_z(i) + stage_two(i) + stage_three(i))
+        sent(stage(i, 0) + stage(i, 1) + stage(i, 2))
     for i in range(4, total):
         sent(stage_core(i))
     sent(keep_first + small_first + keep_second + small_second)
+    for copy in pair_out(0) + pair_out(1) + pair_out(2) + last_out:
+        copy.wait()
 
 
 def front(activations, projections, combiner, expander, reducer, offsets, shifts, keep_flags, nz):
@@ -1245,9 +1269,13 @@
             jax.ShapeDtypeStruct((1536, 128), f32),
         ],
         in_specs=[HBM] + [VM] * 6 + [SM],
-        out_specs=[VM, HBM, HBM, HBM, VM, VM, VM, VM, VM, VM],
+        out_specs=[HBM, HBM, HBM, HBM, VM, VM, HBM, HBM, VM, HBM],
         scratch_shapes=[
             pltpu.VMEM((2 * LEN, WIDTH), bf16),
+            pltpu.VMEM((3, WIDTH, 384), bf16),
+            pltpu.VMEM((3, 2 * LEN, 384), bf16),
+            pltpu.VMEM((1536, 384), bf16),
+            pltpu.VMEM((1536, 128), f32),
             pltpu.VMEM((2, half, 384), bf16),
             pltpu.VMEM((2, half, 256), bf16),
             pltpu.VMEM((2, half, 256), bf16),
@@ -1264,7 +1292,7 @@
             DMA((10, nz - 1)),
         ]
         + [DMA((10,))] * 6
-        + [DMA((11,)), DMA((2,)), DMA((2,)), DMA((nz,)), DMA((nz,)), DMA((3, 2)), DMA((3, 2))],
+        + [DMA((11,)), DMA((2,)), DMA((2,)), DMA((nz,)), DMA((nz,)), DMA((3, 2)), DMA((3, 2)), DMA((8,))],
         compiler_params=pltpu.CompilerParams(collective_id=5, has_side_effects=True, vmem_limit_bytes=VMEM_CAP),
         name="front",
     )(activations, projections, combiner, expander, reducer.T, offsets, shifts, keep_flags)
@@ -1318,15 +1346,15 @@
     nz,
     half,
     x_ref,
-    w_ref,
-    qkv_ref,
-    out_ref,
-    lse_ref,
+    w_in,
+    qkv_in,
+    out_in,
+    lse_in,
     datt_ref,
     p_two,
     p_one,
     p_out,
-    resid_ref,
+    resid_in,
     dvec_ref,
     dshift_ref,
     t_two,
@@ -1337,6 +1365,11 @@
     sums_ref,
     norm_ref,
     input_ref,
+    w_ref,
+    qkv_ref,
+    out_ref,
+    lse_ref,
+    resid_ref,
     dout,
     rows,
     rows_t,
@@ -1362,7 +1395,7 @@
     own, gap = take(6), take(6)
     recv_two, recv_three, recv_z = take(10), take(10), take(10)
     small_buf, small_in, small_z, norm_buf, norm_in, norm_z, dx_in, dx_sum, dx_y, mine = take(10)
-    (core_s, core_r, two_s, two_r, three_s, three_r, zs, zr, bs, br, bzs, bzr, os, orr, load, local, head_s, head_r) = take(18)
+    (core_s, core_r, two_s, two_r, three_s, three_r, zs, zr, bs, br, bzs, bzr, os, orr, load, local, head_s, head_r, in_sem) = take(19)
     z, x, y, c = place()
     others = [dev(lax.rem(z + d, nz), x, y, c) for d in range(1, nz)]
     along_x, along_y, along_c = dev(z, 1 - x, y, c), dev(z, x, 1 - y, c), dev(z, x, y, 1 - c)
@@ -1386,8 +1419,15 @@
 
     load_rows(0).start()
     load_rows(1).start()
+    inbound = [
+        pltpu.make_async_copy(source, target, in_sem.at[i])
+        for i, (source, target) in enumerate(
+            ((out_in, out_ref), (lse_in, lse_ref), (qkv_in, qkv_ref), (w_in, w_ref), (resid_in, resid_ref))
+        )
+    ]
     for i in CORE_ORDER:
         load_own(i).start()
+    start(inbound)
     greet(others + [along_x, along_y, along_c])
     heads = [
         remote(datt_ref.at[1 - c, here], dout.at[there], head_s.at[i], head_r.at[i], along_c)
@@ -1506,7 +1546,7 @@
     lax.fori_loop(0, 2 * LEN // BLK, turn, 0)
     doff[...] = jnp.zeros_like(doff)
     arrived(heads)
-    for copy in heads_kept:
+    for copy in heads_kept + inbound:
         copy.wait()
 
     def prepare(u, carry):
@@ -1807,9 +1847,14 @@
             jax.ShapeDtypeStruct((8, 128), f32),
             jax.ShapeDtypeStruct((3 * LEN, WIDTH), bf16),
         ],
-        in_specs=[HBM] + [VM] * 5 + [HBM] * 3 + [VM] * 3,
+        in_specs=[HBM] * 10 + [VM] * 2,
         out_specs=[VM] * 7 + [HBM],
         scratch_shapes=[
+            pltpu.VMEM((3, WIDTH, 384), bf16),
+            pltpu.VMEM((3, 2 * LEN, 384), bf16),
+            pltpu.VMEM((1536, 384), bf16),
+            pltpu.VMEM((1536, 128), f32),
+            pltpu.VMEM((WIDTH, WIDTH), f32),
             pltpu.VMEM((1536, 384), bf16),
             pltpu.VMEM((2, BLK, WIDTH), bf16),
             pltpu.VMEM((WIDTH, 2 * LEN), bf16),
@@ -1846,7 +1891,7 @@
         + [DMA((6,))] * 2
         + [DMA((2, nz - 1))] * 2
         + [DMA((13,))] * 2
-        + [DMA((6,)), DMA((7,)), DMA((2,)), DMA((2,))],
+        + [DMA((6,)), DMA((7,)), DMA((2,)), DMA((2,)), DMA((5,))],
         compiler_params=pltpu.CompilerParams(collective_id=6, has_side_effects=True, vmem_limit_bytes=VMEM_CAP),
         name="rear",
     )(activations, weights, qkv, out, lse, datt, p_two, p_one, p_out, resid, dvec, dshift)

time: 278 us -> 267 us (0.960)
  Pallas kernels: 277 us -> 266 us
    pallas_call x1, Pallas kernels: 95 us -> 84.9 us  [front(): pl.pallas_call(functools.partial(front_kernel, nz, half, cols), out_shape...]
where the time goes in v5:
time: 267 us
  Pallas kernels  266 us (100%)
    pallas_call x1, Pallas kernels, rear(): pl.pallas_call(functools.partial(rear_kernel, nz, half), out_shape=[jax.S...  113 us
    pallas_call x1, Pallas kernels, front(): pl.pallas_call(functools.partial(front_kernel, nz, half, cols), out_shape...  84.9 us
    pallas_call x1, Pallas kernels, core(): pl.pallas_call(functools.partial(core_kernel, seqs), out_shape=[jax.Shape...  55.9 us
    pallas_call x1, Pallas kernels, finish(): pl.pallas_call(functools.partial(finish_kernel, half), out_shape=[shape((...  12.8 us

profile of v5, /device:TPU:0, one launch (start us, length us, event | category | flops | bytes accessed | tf_op | source)
XLA Modules:
  0.0 267.1 jit_solution(1078095815648419424)
XLA Ops:
  0.7 84.9 %front.1 = (bf16[3,768,384]{2,1,0:T(8,128)(2,1)}, bf16[2,2,4,2,2,48,256]{6,5,4,3,2,1,0:T(8,128)(2,1)}, bf16[2,2,4,2,2,48,768]{6,5,4,3,2,1,0:T(8,128)(2,1)}, bf16...) custom-call(bf16[3072,768]{1,0:T(8,128)(2,1)} %x_ref.5, ...), custom_call_target="tpu_custom_call" | custom-call | tf_op jit(solution)/shard_map/front/pallas_call | solution.py:1257
  85.6 55.9 %core.1 = (bf16[3072,768]{1,0:T(8,128)(2,1)}, f32[768,768]{1,0:T(8,128)}, bf16[2,768,384]{2,1,0:T(8,128)(2,1)}, bf16[2,2,768,256]{3,2,1,0:T(8,128)(2,1)}, bf16[4...) custom-call(s32[3]{0:T(128)} %keep_ref.3, ...), custom_call_target="tpu_custom_call" | custom-call | tf_op jit(solution)/shard_map/core/pallas_call | solution.py:904
  141.5 112.7 %rear.1 = (f32[2,48,768]{2,1,0:T(8,128)}, f32[2,48,768]{2,1,0:T(8,128)}, f32[2,48,256]{2,1,0:T(8,128)}, f32[2,48,384]{2,1,0:T(8,128)}, f32[2,48,256]{2,1,0:T(8,1...) custom-call(bf16[3072,768]{1,0:T(8,128)(2,1)} %x_ref.5, ...), custom_call_target="tpu_custom_call" | custom-call | tf_op jit(solution)/shard_map/rear/pallas_call | solution.py:1842
  254.2 12.8 %finish.1 = (f32[3072,768]{1,0:T(8,128)}, bf16[3072,768]{1,0:T(8,128)(2,1)}, f32[1]{0:T(128)}, s32[1]{0:T(128)}, f32[3,96,192]{2,1,0:T(8,128)}, /*index=5*/f32[3...) custom-call(bf16[3072,768]{1,0:T(8,128)(2,1)} %get-tuple-element.101, ...), custom_call_target="tpu_custom_call" | custom-call | tf_op jit(solution)/shard_map/finish/pallas_call | solution.py:2283

commit v6 on v5

--- a/solution.py
+++ b/solution.py
@@ -1298,7 +1298,7 @@
     )(activations, projections, combiner, expander, reducer.T, offsets, shifts, keep_flags)
 
 
-Y_FIRST = (False, False, True, False, True, False, False, True, False, False)
+Y_FIRST = (True, False, False, False, True, False, False, False, False, True)
 CORE_ORDER = (5, 4, 1, 2, 0, 3)
 SHARED_STEPS = {
     0: [(1, 5), (1, 4)],
@@ -1308,38 +1308,16 @@
 }
 WHOLE_STEPS = {
     1: [(2, 1)],
-    2: ["sum", (2, 2)],
+    2: ["sum", (2, 0)],
     3: [(3, 5)],
     6: [(4, 5), (3, 1)],
-    7: [(2, 0)],
+    7: [(2, 2)],
     8: ["done", (3, 4), (1, 6), (1, 7)],
     10: [(4, 1)],
-    11: [(4, 4), (3, 0)],
+    11: [(4, 4), (3, 2)],
 }
 LATE_STEPS = [(2, 3), (1, 8), (1, 9)]
-TAIL_STEPS = [
-    "pass",
-    (3, 2),
-    (4, 0),
-    (2, 7),
-    (2, 6),
-    (2, 8),
-    (4, 2),
-    (3, 3),
-    "small",
-    (2, 9),
-    "give",
-    (3, 6),
-    (3, 7),
-    (3, 8),
-    "small z",
-    (3, 9),
-    (4, 3),
-    (4, 6),
-    (4, 7),
-    (4, 8),
-    (4, 9),
-]
+TAIL_STEPS = ["pass", (3, 0), (4, 2), (2, 6), (3, 3), (2, 9), (4, 0), "small", (2, 7), (3, 6), (2, 8), "give", (4, 3), (3, 7), (3, 9), "small z", (3, 8), (4, 6), (4, 7), (4, 9), (4, 8)]
 
 
 def rear_kernel(
@@ -1443,7 +1421,7 @@
         a, h = chunks[i]
         return [remote(partial[a].at[1 - c, :, :, :, h], gap[i], core_s.at[i], core_r.at[i], along_c)]
 
-    for i in CORE_ORDER:
+    for i in CORE_ORDER[:3]:
         start(core_stage(i))
 
     def cell(i, yy, zz, xx):
@@ -1479,6 +1457,8 @@
         if i < 6:
             load_own(i).wait()
             arrived(core_stage(i))
+            for later in CORE_ORDER[CORE_ORDER.index(i) + 3 :][:1]:
+                start(core_stage(later))
 
             def body(k, carry):
                 yy, zz, xx = k // (2 * nz), lax.rem(k // 2, nz), lax.rem(k, 2)

time: 267 us -> 265 us (level)
  no operation moved by 1% of the time
where the time goes in v6:
time: 265 us
  Pallas kernels  264 us (100%)
    pallas_call x1, Pallas kernels, rear(): pl.pallas_call(functools.partial(rear_kernel, nz, half), out_shape=[jax.S...  111 us
    pallas_call x1, Pallas kernels, front(): pl.pallas_call(functools.partial(front_kernel, nz, half, cols), out_shape...  84.9 us
    pallas_call x1, Pallas kernels, core(): pl.pallas_call(functools.partial(core_kernel, seqs), out_shape=[jax.Shape...  55.9 us
    pallas_call x1, Pallas kernels, finish(): pl.pallas_call(functools.partial(finish_kernel, half), out_shape=[shape((...  12.8 us

profile of v6, /device:TPU:0, one launch (start us, length us, event | category | flops | bytes accessed | tf_op | source)
XLA Modules:
  0.0 265.1 jit_solution(571030459785220451)
XLA Ops:
  0.7 84.9 %front.1 = (bf16[3,768,384]{2,1,0:T(8,128)(2,1)}, bf16[2,2,4,2,2,48,256]{6,5,4,3,2,1,0:T(8,128)(2,1)}, bf16[2,2,4,2,2,48,768]{6,5,4,3,2,1,0:T(8,128)(2,1)}, bf16...) custom-call(bf16[3072,768]{1,0:T(8,128)(2,1)} %x_ref.5, ...), custom_call_target="tpu_custom_call" | custom-call | tf_op jit(solution)/shard_map/front/pallas_call | solution.py:1257
  85.6 55.9 %core.1 = (bf16[3072,768]{1,0:T(8,128)(2,1)}, f32[768,768]{1,0:T(8,128)}, bf16[2,768,384]{2,1,0:T(8,128)(2,1)}, bf16[2,2,768,256]{3,2,1,0:T(8,128)(2,1)}, bf16[4...) custom-call(s32[3]{0:T(128)} %keep_ref.3, ...), custom_call_target="tpu_custom_call" | custom-call | tf_op jit(solution)/shard_map/core/pallas_call | solution.py:904
  141.5 110.7 %rear.1 = (f32[2,48,768]{2,1,0:T(8,128)}, f32[2,48,768]{2,1,0:T(8,128)}, f32[2,48,256]{2,1,0:T(8,128)}, f32[2,48,384]{2,1,0:T(8,128)}, f32[2,48,256]{2,1,0:T(8,1...) custom-call(bf16[3072,768]{1,0:T(8,128)(2,1)} %x_ref.5, ...), custom_call_target="tpu_custom_call" | custom-call | tf_op jit(solution)/shard_map/rear/pallas_call | solution.py:1822
  252.2 12.8 %finish.1 = (f32[3072,768]{1,0:T(8,128)}, bf16[3072,768]{1,0:T(8,128)(2,1)}, f32[1]{0:T(128)}, s32[1]{0:T(128)}, f32[3,96,192]{2,1,0:T(8,128)}, /*index=5*/f32[3...) custom-call(bf16[3072,768]{1,0:T(8,128)(2,1)} %get-tuple-element.101, ...), custom_call_target="tpu_custom_call" | custom-call | tf_op jit(solution)/shard_map/finish/pallas_call | solution.py:2263
